TPU v7x, 32 devices: a whole 2x2x4 slice. The times are simulated.
32 devices in a mesh: groups: 2 (over y), seq: 4 (over z), mp: 2 (over x), section: 2 (over core).
Axes of the slice: x: 2, y: 2, z: 4, core: 2. Of those that a mesh axis runs over, the one named last changes fastest.
Arguments:
- readout: bfloat16 [8, 64, 32, 1024], P(('groups', 'mp', 'section'), None, 'seq'), parts along dimension 0, may hold values from -6 to 6
- first_kernel: bfloat16 [3, 3, 64, 128], replicated, may hold values from -0.25 to 0.25
- second_kernel: bfloat16 [3, 3, 128, 256], replicated, may hold values from -0.1875 to 0.1875
- embed_weight: bfloat16 [1024, 768], P(('mp', 'section')), may hold values from -0.1875 to 0.1875
- project_weight: bfloat16 [768, 2304], P(('mp', 'section'))
- output_weight: bfloat16 [768, 768], P(('mp', 'section')), may hold values from -0.4375 to 0.4375
- order: int32 [8, 512], P(('groups', 'mp', 'section')), parts along dimension 0, may hold values from 0 to 511, as said below
- active: int32 [8, 512], P(('groups', 'mp', 'section'), 'seq'), parts along dimension 0, may hold values 0 or 1
Outputs:
- encoded: bfloat16 [8, 512, 768], P(('groups', 'mp', 'section'), 'seq'), parts along dimension 0
There are 2 independent parts, one for each index of `groups`. A program takes and returns all parts, laid end to end along the dimension named above; an argument that names none is the same for every part. Nothing has to cross between parts.
Inputs may be any that keep to these rules, and one draw needn't show every extreme that they name: Each row of order lists each of the 512 patches of its region once. Patch i comes from the wire tile i // 128; each block of 128 positions k * 128 to (k + 1) * 128 - 1 holds exactly 32 patches of every wire tile.
All inputs are finite; a program needn't handle non-finite values. No bound on the sum of `active` on one device may be relied on, other than what follows from the above.
Results may differ from a plain program's by a relative error of at most 0.017.
Values may be sent and summed in bfloat16 or wider, within the bound.
No kernel may reach another device: no remote copies, remote signals or barrier semaphores. Data moves between devices by JAX's collectives and lax.ppermute only.
A program may use at most 64 MiB of HBM per device.

v0:
```python
import functools

import jax
import jax.numpy as jnp
from jax import lax
from jax.experimental import pallas as pl
from jax.experimental.pallas import tpu as pltpu
from jax.sharding import PartitionSpec as P


HEADS = 12
masked_score = -1e30
largest = 3e38
epsilon = 1e-05
BF = jnp.bfloat16
F32 = jnp.float32
EXTRA = 8


def dot(a, b, ca=1, cb=0):
    return lax.dot_general(a, b, (((ca,), (cb,)), ((), ())), preferred_element_type=F32)


def iota(shape, axis):
    return lax.broadcasted_iota(jnp.int32, shape, axis)


def one_hot(mask):
    return jnp.where(mask, 1.0, 0.0).astype(BF)


def silu(v):
    half = 0.5 * v
    return half + half * jnp.tanh(half)


def split_matrix():
    row, col = iota((256, 256), 0), iota((256, 256), 1)
    return one_hot(row == jnp.where(col < 128, 2 * col, 2 * col - 255))


def split_time(rows, splitter):
    even, odd = [], []
    for start in range(0, rows.shape[1], 256):
        both = dot(rows[:, start : start + 256], splitter)
        even.append(both[:, :128])
        odd.append(both[:, 128:])
    if len(even) == 1:
        return even[0], odd[0]
    return jnp.concatenate(even, axis=1), jnp.concatenate(odd, axis=1)


def later(odd):
    moved = pltpu.roll(odd, 1, 1)
    return jnp.where(iota(odd.shape, 1) == 0, 0.0, moved)


def store_taps(taps, base, even, odd):
    height = even.shape[0]
    taps[base : base + height, :] = later(odd).astype(BF)
    taps[base + height : base + 2 * height, :] = even.astype(BF)
    taps[base + 2 * height : base + 3 * height, :] = odd.astype(BF)


def block_of(paired, flip=0):
    if not paired:
        return 0
    return (lax.axis_index("mp") * 2 + lax.axis_index("section")) ^ flip


def front_kernel(x_hbm, k1_hbm, k2_hbm, *refs, wires, channels, middle, paired):
    if paired:
        project_hbm, output_hbm = refs[:2]
        refs = refs[2:]
    msg_ref, taps1_ref, taps2_ref, k1_ref, k2_ref = refs[:5]
    all1, x_ref, sems = refs[-3:]
    part = 256 // wires
    blocks = channels // part
    loads = []
    for block in range(blocks):
        here = pl.ds(block * 256, 256)
        loads.append(pltpu.make_async_copy(x_hbm.at[here, :], x_ref.at[here, :], sems.at[block]))
    loads.append(pltpu.make_async_copy(k1_hbm, k1_ref, sems.at[blocks]))
    others = [pltpu.make_async_copy(k2_hbm, k2_ref, sems.at[blocks + 1])]
    if paired:
        near_ref, query_ref = refs[5:7]
        depth, width = output_hbm.shape
        half = depth // 2
        rows = pl.ds(pl.multiple_of(lax.axis_index("groups") * half, half), half)
        others.append(
            pltpu.make_async_copy(
                project_hbm.at[rows, pl.ds(width, 2 * width)], near_ref, sems.at[blocks + 2]
            )
        )
        others.append(
            pltpu.make_async_copy(
                project_hbm.at[:, pl.ds(0, width)], query_ref.at[:, pl.ds(0, width)], sems.at[blocks + 3]
            )
        )
        others.append(
            pltpu.make_async_copy(output_hbm, query_ref.at[:, pl.ds(width, width)], sems.at[blocks + 4])
        )
    for copy in loads + others:
        copy.start()
    splitter = split_matrix()
    row, col = iota((256, 256), 0), iota((256, 256), 1)
    mixer = one_hot(col == (row % part) * wires + row // part)
    for block in range(blocks):
        loads[block].wait()
        rows = dot(mixer, x_ref[block * 256 : (block + 1) * 256, :]).astype(BF)
        even, odd = split_time(rows, splitter)
        lagged = later(odd)
        for wire in range(wires):
            here = slice(wire * part, (wire + 1) * part)
            base = wire * 3 * channels + block * part
            all1[base : base + part, :] = lagged[here].astype(BF)
            all1[base + channels : base + channels + part, :] = even[here].astype(BF)
            all1[base + 2 * channels : base + 2 * channels + part, :] = odd[here].astype(BF)
    taps1_ref[...] = all1[: 6 * channels, :]
    last = (wires - 1) * 3 * channels
    msg_ref[: 2 * channels, :] = all1[last + channels : last + 3 * channels, :]
    loads[blocks].wait()
    k1 = k1_ref[...]
    for level in range(1, wires // 2):
        start = (2 * level - 1) * 3 * channels
        out = silu(dot(k1, all1[start : start + 9 * channels, :], 0, 0)).astype(BF)
        if level == wires // 2 - 1:
            msg_ref[2 * channels :, :] = out
        even, odd = split_time(out, splitter)
        store_taps(taps2_ref, (level - 1) * 3 * middle, even, odd)
    for copy in others:
        copy.wait()


def central_kernel(taps1_ref, taps2_ref, k1_ref, k2_ref, first_ref, second_ref, patch, *, channels, middle):
    splitter = split_matrix()
    first_ref[...] = dot(k1_ref[3 * channels :, :], taps1_ref[...], 0, 0)
    second_ref[...] = dot(k2_ref[6 * middle :, :], taps2_ref[: 3 * middle, :], 0, 0)
    out = silu(dot(k2_ref[...], taps2_ref[...], 0, 0)).astype(BF)
    store_patch(patch, out, splitter)


def mix_kernel(patch, *refs, pieces):
    embed_refs = refs[:pieces]
    token_ref, low_ref, high, own, sem = refs[pieces:]
    copy = pltpu.make_async_copy(embed_refs[0], own, sem)
    copy.start()
    row, col = iota((256, 256), 0), iota((256, 256), 1)
    mixer = one_hot(col == (row % 64) * 4 + row // 64)
    for piece in list(range(1, pieces)) + [0]:
        ref = embed_refs[piece]
        if piece == 0:
            copy.wait()
            ref = own
        parts = ref.shape[0] // 256
        for part in range(parts):
            rows = dot(mixer, ref[part * 256 : (part + 1) * 256, :]).astype(BF)
            base = pl.multiple_of((block_of(pieces > 1, piece) * parts + part) * 128, 128)
            low_ref[pl.ds(base, 128), :] = rows[:128]
            high[pl.ds(base, 128), :] = rows[128:]
    token_ref[...] = dot(patch[...], high[...], 0, 0)


def store_patch(patch, out, splitter):
    even, odd = split_time(out, splitter)
    even, odd = even.astype(BF), odd.astype(BF)
    for block in range(out.shape[0] // 64):
        here = slice(block * 64, (block + 1) * 64)
        patch[block * 128 : block * 128 + 64, :] = even[here]
        patch[block * 128 + 64 : (block + 1) * 128, :] = odd[here]


def back_kernel(
    got_ref, first_ref, second_ref, token_ref, low_ref, k1_ref, k2_ref, active_ref,
    out_ref, all1, all2, patch, *, channels, middle
):
    splitter = split_matrix()
    odd = got_ref[channels : 2 * channels, :].astype(F32)
    all1[:channels, :] = later(odd).astype(BF)
    all1[channels:, :] = got_ref[: 2 * channels, :]
    even, odd = split_time(got_ref[2 * channels :, :], splitter)
    store_taps(all2, 0, even, odd)
    first = silu(first_ref[...] + dot(k1_ref[: 3 * channels, :], all1[...], 0, 0)).astype(BF)
    even, odd = split_time(first, splitter)
    store_taps(all2, 3 * middle, even, odd)
    out = silu(second_ref[...] + dot(k2_ref[: 6 * middle, :], all2[...], 0, 0)).astype(BF)
    store_patch(patch, out, splitter)
    total = token_ref[...] + dot(patch[...], low_ref[...], 0, 0)
    count, width = total.shape
    out_ref[:count, :] = total.astype(BF)
    tail = jnp.broadcast_to(active_ref[...].astype(F32), (EXTRA, count))
    tail = jnp.concatenate([tail, jnp.zeros((EXTRA, width - count), F32)], axis=1)
    out_ref[count:, :] = tail.astype(BF)


def normal(tokens):
    value = tokens.astype(F32)
    value = value - jnp.mean(value, axis=-1, keepdims=True)
    spread = jnp.mean(value * value, axis=-1, keepdims=True)
    return (value * lax.rsqrt(spread + epsilon)).astype(BF)


def lift(joined, normed, keys, values):
    width = joined.shape[0]
    rows = normed[...]
    keys[...] = dot(rows, joined[:, :width]).astype(BF)
    values[...] = dot(rows, joined[:, width:]).astype(BF)


def collect(sources, target, sems):
    copies = []
    for index, (ref, base, column, align) in enumerate(sources):
        if not isinstance(base, int):
            base = pl.multiple_of(base, align)
        copies.append(
            pltpu.make_async_copy(
                ref.at[:, pl.ds(column, target.shape[1])],
                target.at[pl.ds(base, ref.shape[0]), :],
                sems.at[index],
            )
        )
        copies[-1].start()
    return copies


def place_of(slot, swap):
    position = lax.axis_index("seq")
    return position ^ slot if swap else slot


def prepare_kernel(order_ref, *refs, pieces, chunks, swap):
    kv_refs = refs[:pieces]
    chunk_refs = refs[pieces : pieces + chunks]
    joined, normed, keys, values, perm_ref, sems = refs[pieces + chunks :]
    width = joined.shape[0]
    if pieces > 1:
        own, beside, near, far, near_corner, far_corner = kv_refs
        depth, half = own.shape[0], near.shape[0]
        group = lax.axis_index("groups")
        sources = [
            (own, block_of(True, 0) * depth, width, depth),
            (beside, block_of(True, 1) * depth, width, depth),
        ]
        for flip, first, second in ((2, near, far), (3, near_corner, far_corner)):
            base = block_of(True, flip) * depth
            sources.append((first, base + group * half, 0, half))
            sources.append((second, base + (group ^ 1) * half, 0, half))
    else:
        sources = [(kv_refs[0], 0, width, 1)]
    copies = collect(sources, joined, sems)
    shards, count = order_ref.shape
    square = iota((count, count), 0) == iota((count, count), 1)
    lane = iota((1, count), 1)
    labels = jnp.concatenate([lane + place_of(slot, swap) * count for slot in range(shards)], axis=1)
    labels = labels.astype(F32)
    for slot in range(shards):
        row = order_ref[pl.ds(place_of(slot, swap), 1), :].astype(F32)
        across = jnp.broadcast_to(row, (count, count))
        down = jnp.sum(jnp.where(square, across, 0.0), axis=1, keepdims=True)
        perm_ref[slot * count : (slot + 1) * count, :] = one_hot(labels == down)
    for slot, ref in enumerate(chunk_refs):
        normed[slot * count : (slot + 1) * count, :] = normal(ref[:count, :])
    for copy in copies:
        copy.wait()
    lift(joined, normed, keys, values)


def finish_kernel(perm_ref, joined, normed0, keys0, values0, *refs, pieces, chunks, early, count, swap):
    chunk_refs = refs[:chunks]
    weight_refs = refs[chunks : chunks + 2 * pieces]
    out_ref, query, output, normed1, keys1, values1, cap, mixed, sems = refs[chunks + 2 * pieces :]
    width = joined.shape[0]
    sources = [[], []]
    for kind in range(2):
        for piece in range(pieces):
            ref = weight_refs[kind * pieces + piece]
            depth = ref.shape[0]
            column = width if kind and piece > 1 else 0
            sources[kind].append((ref, block_of(pieces > 1, piece) * depth, column, depth))
    wait_query = collect(sources[0], query, sems.at[0])
    wait_output = collect(sources[1], output, sems.at[1])
    for slot, ref in enumerate(chunk_refs[early:]):
        normed1[slot * count : (slot + 1) * count, :] = normal(ref[:count, :])
    lift(joined, normed1, keys1, values1)
    near = early * count
    slot = 0 if swap else lax.axis_index("seq")
    own = perm_ref[pl.ds(pl.multiple_of(slot * count, count), count), :]
    picked = (dot(own[:, :near], normed0[...]) + dot(own[:, near:], normed1[...])).astype(BF)
    head = width // HEADS
    for copy in wait_query:
        copy.wait()
    queries = (dot(picked, query[...]) * head ** (-0.5)).astype(BF)
    on = None
    token = None
    for slot, ref in enumerate(chunk_refs):
        here = slice(slot * count, (slot + 1) * count)
        term = dot(ref[count:, :count], perm_ref[here, :])
        on = term if on is None else on + term
        term = dot(own[:, here], ref[:count, :])
        token = term if token is None else token + term
    allowed = (own.astype(F32) + jnp.broadcast_to(on[:1], own.shape)) > 0.5
    cap[...] = jnp.where(allowed, largest, masked_score)
    low = iota((count, 2 * head), 1) < head
    for pair in range(HEADS // 2):
        here = slice(pair * 2 * head, (pair + 1) * 2 * head)
        query = queries[:, here]
        zero = jnp.zeros_like(query)
        both = jnp.concatenate([jnp.where(low, query, zero), jnp.where(low, zero, query)], axis=0)
        scores = jnp.concatenate([dot(both, keys0[:, here], 1, 1), dot(both, keys1[:, here], 1, 1)], axis=1)
        weights, scale = [], []
        for half in range(2):
            score = jnp.minimum(scores[half * count : (half + 1) * count], cap[...])
            weight = jnp.exp(score - jnp.max(score, axis=-1, keepdims=True))
            scale.append(1.0 / jnp.sum(weight, axis=-1, keepdims=True))
            weights.append(weight.astype(BF))
        weights = jnp.concatenate(weights, axis=0)
        part = dot(weights[:, :near], values0[:, here]) + dot(weights[:, near:], values1[:, here])
        mixed[:, here] = jnp.where(low, part[:count] * scale[0], part[count:] * scale[1]).astype(BF)
    for copy in wait_output:
        copy.wait()
    out_ref[...] = (token + dot(mixed[...], output[...])).astype(BF)


def vmem():
    return pl.BlockSpec(memory_space=pltpu.VMEM)


def hbm():
    return pl.BlockSpec(memory_space=pl.ANY)


def fixed():
    return pl.BlockSpec(memory_space=pltpu.HBM)


def params(mib):
    return pltpu.CompilerParams(vmem_limit_bytes=mib * 1024 * 1024)


def array(shape, dtype=BF):
    return jax.ShapeDtypeStruct(shape, dtype)


def front(rows, k1, k2, wires, weights):
    channels = rows.shape[0] // wires
    middle = k1.shape[1]
    length = rows.shape[1] // 2
    outs = [
        array((2 * channels + middle, length)),
        array((6 * channels, length)),
        array(((wires // 2 - 1) * 3 * middle, length // 2)),
        array(k1.shape),
        array(k2.shape),
    ]
    if weights:
        depth, width = weights[1].shape
        outs += [array((depth // 2, 2 * width)), array((depth, 2 * width))]
    return pl.pallas_call(
        functools.partial(
            front_kernel, wires=wires, channels=channels, middle=middle, paired=len(weights) > 0
        ),
        out_shape=outs,
        in_specs=[fixed()] * (3 + len(weights)),
        out_specs=[vmem()] * len(outs),
        scratch_shapes=[
            pltpu.VMEM((wires * 3 * channels, length), BF),
            pltpu.VMEM(rows.shape, BF),
            pltpu.SemaphoreType.DMA((channels * wires // 256 + 5,)),
        ],
        compiler_params=params(12),
        name="front",
    )(*[pltpu.with_memory_space_constraint(v, pltpu.HBM) for v in (rows, k1, k2, *weights)])


def central(taps1, taps2, k1, k2, count):
    middle, outer = k1.shape[1], k2.shape[1]
    channels = k1.shape[0] // 9
    return pl.pallas_call(
        functools.partial(central_kernel, channels=channels, middle=middle),
        out_shape=(
            array((middle, taps1.shape[1]), F32),
            array((outer, taps2.shape[1]), F32),
            array((2 * outer, count)),
        ),
        in_specs=[vmem()] * 4,
        out_specs=[vmem()] * 3,
        compiler_params=params(8),
        name="central",
    )(taps1, taps2, k1, k2)


def mix(patch, embeds):
    width = embeds[0].shape[1]
    return pl.pallas_call(
        functools.partial(mix_kernel, pieces=len(embeds)),
        out_shape=(array((patch.shape[1], width), F32), array((patch.shape[0], width))),
        in_specs=[vmem()] + [fixed()] + [vmem()] * (len(embeds) - 1),
        out_specs=[vmem()] * 2,
        scratch_shapes=[
            pltpu.VMEM((patch.shape[0], width), BF),
            pltpu.VMEM(embeds[0].shape, BF),
            pltpu.SemaphoreType.DMA,
        ],
        compiler_params=params(8),
        name="mix",
    )(patch, *embeds)


def back(got, parts, k1, k2, active):
    middle = k1.shape[1]
    channels = k1.shape[0] // 9
    length = got.shape[1]
    count = active.shape[1]
    width = parts[-1].shape[1]
    return pl.pallas_call(
        functools.partial(back_kernel, channels=channels, middle=middle),
        out_shape=array((count + EXTRA, width)),
        in_specs=[vmem()] * (4 + len(parts)),
        out_specs=vmem(),
        scratch_shapes=[
            pltpu.VMEM((3 * channels, length), BF),
            pltpu.VMEM((6 * middle, length // 2), BF),
            pltpu.VMEM((2 * k2.shape[1], count), BF),
        ],
        compiler_params=params(8),
        name="back",
    )(got, *parts, k1, k2, active)


def prepare(order, weights, chunks, swap):
    shards, count = order.shape
    width = chunks[0].shape[1]
    size, near = shards * count, len(chunks) * count
    return pl.pallas_call(
        functools.partial(prepare_kernel, pieces=len(weights), chunks=len(chunks), swap=swap),
        out_shape=(array((width, 2 * width)),) + (array((near, width)),) * 3 + (array((size, size)),),
        in_specs=[vmem()] + [fixed()] + [hbm()] * (len(weights) - 1) + [vmem()] * len(chunks),
        out_specs=[vmem()] * 5,
        scratch_shapes=[pltpu.SemaphoreType.DMA((len(weights),))],
        compiler_params=params(8 + size // 128),
        name="prepare",
    )(order, *weights, *chunks)


def finish(ready, chunks, weights, early, swap):
    joined, normed, keys, values, perm = ready
    width = joined.shape[0]
    size = perm.shape[0]
    count = size // len(chunks)
    far = size - early * count
    pieces = len(weights) // 2
    return pl.pallas_call(
        functools.partial(
            finish_kernel, pieces=pieces, chunks=len(chunks), early=early, count=count, swap=swap
        ),
        out_shape=array((count, width)),
        in_specs=[vmem()] * (5 + len(chunks))
        + ([fixed()] + [hbm()] * (pieces - 1)) * 2,
        out_specs=vmem(),
        scratch_shapes=[
            pltpu.VMEM((width, width), BF),
            pltpu.VMEM((width, width), BF),
            pltpu.VMEM((far, width), BF),
            pltpu.VMEM((far, width), BF),
            pltpu.VMEM((far, width), BF),
            pltpu.VMEM((count, size), F32),
            pltpu.VMEM((count, width), BF),
            pltpu.SemaphoreType.DMA((2, pieces)),
        ],
        compiler_params=params(8 + size // 64),
        name="finish",
    )(perm, joined, normed, keys, values, *chunks, *weights)


def exchanged(value, axis, flip):
    count = lax.axis_size(axis)
    return lax.ppermute(value, axis, [(i, i ^ flip) for i in range(count)])


def layer(
    readout, first_kernel, second_kernel, embed_weight, project_weight, output_weight, order, active
):
    shards = lax.axis_size("seq")
    paired = lax.axis_size("mp") == 2 and lax.axis_size("section") == 2 and lax.axis_size("groups") == 2
    swap = shards == 4
    channels, wires, ticks = readout.shape[1:]
    k1 = first_kernel.reshape(-1, first_kernel.shape[-1])
    k2 = second_kernel.reshape(-1, second_kernel.shape[-1])
    order = order.reshape(shards, -1)
    count = order.shape[1]
    rows = readout.reshape(channels * wires, ticks)
    weights = (project_weight, output_weight)
    if paired:
        embed_across = exchanged(embed_weight, "mp", 1)
        embed_beside = exchanged(embed_weight, "section", 1)
        embeds = [embed_weight, embed_beside, embed_across]
        embeds.append(exchanged(embed_across, "section", 1))
        front_out = front(rows, k1, k2, wires, weights)
        msg, taps1, taps2, k1, k2, near, packed = front_out
    else:
        embeds = [lax.all_gather(embed_weight, ("mp", "section"), axis=0, tiled=True)]
        msg, taps1, taps2, k1, k2 = front(rows, k1, k2, wires, ())
    got = lax.ppermute(msg, "seq", [(i, i + 1) for i in range(shards - 1)])
    first, second, patch = central(taps1, taps2, k1, k2, count)
    token, low = mix(patch, embeds)
    tokens = back(got, (first, second, token, low), k1, k2, active)
    if swap:
        chunks = [tokens] + [exchanged(tokens, "seq", flip) for flip in (1, 2, 3)]
    else:
        everyone = lax.all_gather(tokens, "seq", axis=0, tiled=True)
        chunks = [everyone[i * (count + EXTRA) : (i + 1) * (count + EXTRA)] for i in range(shards)]
    if paired:
        project_beside = exchanged(project_weight, "section", 1)
        output_beside = exchanged(output_weight, "section", 1)
        near = exchanged(near, "mp", 1)
        far = exchanged(near, "groups", 1)
        packed = exchanged(packed, "mp", 1)
        kv_weights = [project_weight, project_beside, near, far]
        kv_weights.append(exchanged(near, "section", 1))
        kv_weights.append(exchanged(far, "section", 1))
        corner = exchanged(packed, "section", 1)
        last_weights = [project_weight, project_beside, packed, corner]
        last_weights += [output_weight, output_beside, packed, corner]
    else:
        kv_weights = [lax.all_gather(project_weight, ("mp", "section"), axis=0, tiled=True)]
        last_weights = kv_weights + [lax.all_gather(output_weight, ("mp", "section"), axis=0, tiled=True)]
    early = shards // 2
    ready = prepare(order, kv_weights, chunks[:early], swap)
    result = finish(ready, chunks, last_weights, early, swap)
    return result[None]


def solution(mesh):
    in_specs = (
        P(("groups", "mp", "section"), None, "seq", None),
        P(),
        P(),
        P(("mp", "section"), None),
        P(("mp", "section"), None),
        P(("mp", "section"), None),
        P(("groups", "mp", "section"), None),
        P(("groups", "mp", "section"), "seq"),
    )
    out_specs = P(("groups", "mp", "section"), "seq", None)
    return jax.shard_map(layer, mesh=mesh, in_specs=in_specs, out_specs=out_specs, check_vma=False)
```

profile of v0, /device:TPU:0, one launch (start us, length us, event | category | flops | bytes accessed | tf_op | source)
XLA Modules:
  0.0 64.3 jit_solution(11992692568809675240)
XLA Ops:
  0.0 3.3 %front.1 = (bf16[256,512]{1,0:T(8,128)(2,1)S(1)}, bf16[384,512]{1,0:T(8,128)(2,1)S(1)}, bf16[1152,256]{1,0:T(8,128)(2,1)S(1)}, bf16[576,128]{1,0:T(8,128)(2,1)S(...) custom-call(bf16[512,1024]{1,0:T(8,128)(2,1)} %bitcast.6, ...), custom_call_target="tpu_custom_call" | custom-call | tf_op jit(solution)/shard_map/front/pallas_call | solution.py:358
  3.3 0.0 copy-start.4
  3.3 3.0 %collective-permute-start.12 = (bf16[192,1536]{1,0:T(8,128)(2,1)S(1)}, bf16[192,1536]{1,0:T(8,128)(2,1)S(1)}, u32[]{:S(2)}, u32[]{:S(2)}) collective-permute-start(bf16[192,1536]{1,0:T(8,128)(2,1)S(1)} %get-tuple-element.38), channel_id=1, source_target_pairs={{0,2},{2,0},{1,3},{3,1},{4,6},{6,4},{5,7},{7,5},{8,10},{10,8},{9,1... | collective-permute-start | bytes 1769480 | tf_op jit(solution)/shard_map/ppermute | solution.py:477
  6.4 3.5 %collective-permute-start.5 = (bf16[256,512]{1,0:T(8,128)(2,1)S(1)}, bf16[256,512]{1,0:T(8,128)(2,1)S(1)}, u32[]{:S(2)}, u32[]{:S(2)}) collective-permute-start(bf16[256,512]{1,0:T(8,128)(2,1)S(1)} %get-tuple-element.23), channel_id=1, source_target_pairs={{0,4},{4,8},{8,12},{1,5},{5,9},{9,13},{2,6},{6,10},{10,14},{3,7},{... | collective-permute-start | bytes 786440 | tf_op jit(solution)/shard_map/ppermute | solution.py:503
  9.9 0.6 collective-permute-start.1
  10.5 1.6 %collective-permute-start.7 = (bf16[256,768]{1,0:T(8,128)(2,1)S(1)}, bf16[256,768]{1,0:T(8,128)(2,1)S(1)}, u32[]{:S(2)}, u32[]{:S(2)}) collective-permute-start(bf16[256,768]{1,0:T(8,128)(2,1)S(1)} %copy-done.2), channel_id=1, source_target_pairs={{0,2},{2,0},{1,3},{3,1},{4,6},{6,4},{5,7},{7,5},{8,10},{10,8},{9,1... | collective-permute-start | bytes 1179656 | tf_op jit(solution)/shard_map/ppermute | solution.py:477
  12.0 3.1 %collective-permute-done.5.got_ref = bf16[256,512]{1,0:T(8,128)(2,1)S(1)} collective-permute-done((bf16[256,512]{1,0:T(8,128)(2,1)S(1)}, bf16[256,512]{1,0:T(8,128)(2,1)S(1)}, u32[]{:S(2)}, u32[]{:S(2)}) %collective-permute-start.5) | collective-permute-done | bytes 262176 | tf_op jit(solution)/shard_map/ppermute | solution.py:503
  15.1 11.8 %collective-permute-done.1.refs_2_ = bf16[96,1536]{1,0:T(8,128)(2,1)S(1)} collective-permute-done((bf16[96,1536]{1,0:T(8,128)(2,1)S(1)}, bf16[96,1536]{1,0:T(8,128)(2,1)S(1)}, u32[]{:S(2)}, u32[]{:S(2)}) %collective-permute-start.1) | collective-permute-done | bytes 294944 | tf_op jit(solution)/shard_map/ppermute | solution.py:477
  26.9 2.1 %collective-permute-start.2 = (bf16[96,1536]{1,0:T(8,128)(2,1)S(1)}, bf16[96,1536]{1,0:T(8,128)(2,1)S(1)}, u32[]{:S(2)}, u32[]{:S(2)}) collective-permute-start(bf16[96,1536]{1,0:T(8,128)(2,1)S(1)} %collective-permute-done.1.refs_2_), channel_id=1, source_target_pairs={{0,16},{16,0},{1,17},{17,1},{2,18},{18,2},{3,19},{19,3},{4,20},{20... | collective-permute-start | bytes 884744 | tf_op jit(solution)/shard_map/ppermute | solution.py:477
  28.9 5.5 %collective-permute-done.7.refs_2_ = bf16[256,768]{1,0:T(8,128)(2,1)S(1)} collective-permute-done((bf16[256,768]{1,0:T(8,128)(2,1)S(1)}, bf16[256,768]{1,0:T(8,128)(2,1)S(1)}, u32[]{:S(2)}, u32[]{:S(2)}) %collective-permute-start.7) | collective-permute-done | bytes 393248 | tf_op jit(solution)/shard_map/ppermute | solution.py:477
  34.5 0.5 collective-permute-start.13
  35.0 0.1 collective-permute-start.3
  35.0 0.4 collective-permute-start.4
  35.5 0.7 %collective-permute-done.8.refs_3_ = bf16[256,768]{1,0:T(8,128)(2,1)S(1)} collective-permute-done((bf16[256,768]{1,0:T(8,128)(2,1)S(1)}, bf16[256,768]{1,0:T(8,128)(2,1)S(1)}, u32[]{:S(2)}, u32[]{:S(2)}) %collective-permute-start.8) | collective-permute-done | bytes 393248 | tf_op jit(solution)/shard_map/ppermute | solution.py:477
  36.2 0.1 collective-permute-start.14
  36.3 0.7 %central.1 = (f32[128,512]{1,0:T(8,128)S(1)}, f32[256,256]{1,0:T(8,128)S(1)}, bf16[512,128]{1,0:T(8,128)(2,1)S(1)}) custom-call(bf16[384,512]{1,0:T(8,128)(2,1)S(1)} %get-tuple-element.24.taps1_ref, bf16[1152,256]{1,0:T(8,128)(2,1)S(1)} %get-tuple-element.25.taps2_ref, bf16[576,128]{1,0:T(8,128)(2,1)S(1)} %get-tuple-element.26.k1_ref, ...), custom_call_target="tpu_custom_call" | custom-call | tf_op jit(solution)/shard_map/central/pallas_call | solution.py:378
  37.0 1.2 %mix.1 = (f32[128,768]{1,0:T(8,128)S(1)}, bf16[512,768]{1,0:T(8,128)(2,1)S(1)}) custom-call(bf16[512,128]{1,0:T(8,128)(2,1)S(1)} %get-tuple-element.30.patch, bf16[256,768]{1,0:T(8,128)(2,1)S(1)} %copy-done.2, bf16[256,768]{1,0:T(8,128)(2,1)S(1)} %collective-permute-done.6.refs_1_, bf16[256,768]{1,0:T(8,128)(2,1)S(1)} %collective-permute-done.7.refs_2_, ...), custom_call_target="tpu_custom_call" | custom-call | tf_op jit(solution)/shard_map/mix/pallas_call | solution.py:394
  38.3 1.2 %back.1.refs_6_.refs_0_ = bf16[136,768]{1,0:T(8,128)(2,1)S(1)} custom-call(bf16[256,512]{1,0:T(8,128)(2,1)S(1)} %collective-permute-done.5.got_ref, f32[128,512]{1,0:T(8,128)S(1)} %get-tuple-element.28.first_ref, f32[256,256]{1,0:T(8,128)S(1)} %get-tuple-element.29.second_ref, f32[128,768]{1,0:T(8,128)S(1)} %get-tuple-element.31.token_ref, ...), custom_call_target="tpu_custom_call" | custom-call | tf_op jit(solution)/shard_map/back/pallas_call | solution.py:415
  39.5 1.9 %collective-permute-start.9 = (bf16[136,768]{1,0:T(8,128)(2,1)S(1)}, bf16[136,768]{1,0:T(8,128)(2,1)S(1)}, u32[]{:S(2)}, u32[]{:S(2)}) collective-permute-start(bf16[136,768]{1,0:T(8,128)(2,1)S(1)} %back.1.refs_6_.refs_0_), channel_id=1, source_target_pairs={{0,4},{4,0},{8,12},{12,8},{1,5},{5,1},{9,13},{13,9},{2,6},{6,2},{1... | collective-permute-start | bytes 626696 | tf_op jit(solution)/shard_map/ppermute | solution.py:477
  41.3 2.6 %collective-permute-start.10 = (bf16[136,768]{1,0:T(8,128)(2,1)S(1)}, bf16[136,768]{1,0:T(8,128)(2,1)S(1)}, u32[]{:S(2)}, u32[]{:S(2)}) collective-permute-start(bf16[136,768]{1,0:T(8,128)(2,1)S(1)} %back.1.refs_6_.refs_0_), channel_id=1, source_target_pairs={{0,8},{4,12},{8,0},{12,4},{1,9},{5,13},{9,1},{13,5},{2,10},{6,14},... | collective-permute-start | bytes 626696 | tf_op jit(solution)/shard_map/ppermute | solution.py:477
  43.9 7.1 %collective-permute-done.9.refs_7_.refs_1_ = bf16[136,768]{1,0:T(8,128)(2,1)S(1)} collective-permute-done((bf16[136,768]{1,0:T(8,128)(2,1)S(1)}, bf16[136,768]{1,0:T(8,128)(2,1)S(1)}, u32[]{:S(2)}, u32[]{:S(2)}) %collective-permute-start.9) | collective-permute-done | bytes 208928 | tf_op jit(solution)/shard_map/ppermute | solution.py:477
  51.0 1.5 %prepare.1 = (bf16[768,1536]{1,0:T(8,128)(2,1)S(1)}, bf16[256,768]{1,0:T(8,128)(2,1)S(1)}, bf16[256,768]{1,0:T(8,128)(2,1)S(1)}, bf16[256,768]{1,0:T(8,128)(2,1)S(1)}, bf16[512,512]{1,0:T(8,128)(2,1)S(1)}) custom-call(s32[4,128]{1,0:T(4,128)S(1)} %bitcast.5, bf16[192,2304]{1,0:T(8,128)(2,1)S(1)} %copy-done, ...), custom_call_target="tpu_custom_call" | custom-call | tf_op jit(solution)/shard_map/prepare/pallas_call | solution.py:434
  52.6 6.7 %collective-permute-done.10.refs_2_ = bf16[136,768]{1,0:T(8,128)(2,1)S(1)} collective-permute-done((bf16[136,768]{1,0:T(8,128)(2,1)S(1)}, bf16[136,768]{1,0:T(8,128)(2,1)S(1)}, u32[]{:S(2)}, u32[]{:S(2)}) %collective-permute-start.10) | collective-permute-done | bytes 208928 | tf_op jit(solution)/shard_map/ppermute | solution.py:477
  59.3 5.0 %finish.1 = bf16[128,768]{1,0:T(8,128)(2,1)} custom-call(bf16[512,512]{1,0:T(8,128)(2,1)S(1)} %get-tuple-element.33.perm_ref, bf16[768,1536]{1,0:T(8,128)(2,1)S(1)} %get-tuple-element.34.joined, bf16[256,768]{1,0:T(8,128)(2,1)S(1)} %get-tuple-element.35.normed0, bf16[256,768]{1,0:T(8,128)(2,1)S(1)} %get-tuple-element.36.keys0, ...), custom_call_target="tpu_custom_call" | custom-call | tf_op jit(solution)/shard_map/finish/pallas_call | solution.py:452
  (22 shorter events, 0.1 us)
Async XLA Ops:
  0.0 10.5 %copy-start = (bf16[192,2304]{1,0:T(8,128)(2,1)S(1)}, bf16[192,2304]{1,0:T(8,128)(2,1)}, u32[]{:S(2)}) copy-start(bf16[192,2304]{1,0:T(8,128)(2,1)} %refs_4_.1) | copy-start | bytes 2654212
  0.0 36.2 %copy-start.1 = (bf16[192,768]{1,0:T(8,128)(2,1)S(1)}, bf16[192,768]{1,0:T(8,128)(2,1)}, u32[]{:S(2)}) copy-start(bf16[192,768]{1,0:T(8,128)(2,1)} %refs_8_.1) | copy-start | bytes 884740
  0.0 10.5 %copy-start.2 = (bf16[256,768]{1,0:T(8,128)(2,1)S(1)}, bf16[256,768]{1,0:T(8,128)(2,1)}, u32[]{:S(2)}) copy-start(bf16[256,768]{1,0:T(8,128)(2,1)} %refs_0_.4) | copy-start | bytes 1179652
  3.3 34.9 %copy-start.4 = (s32[1,128]{1,0:T(1,128)S(1)}, s32[1,128]{1,0:T(1,128)}, u32[]{:S(2)}) copy-start(s32[1,128]{1,0:T(1,128)} %active_ref.1) | copy-start | bytes 1540
  3.3 31.1 %collective-permute-start.12 = (bf16[192,1536]{1,0:T(8,128)(2,1)S(1)}, bf16[192,1536]{1,0:T(8,128)(2,1)S(1)}, u32[]{:S(2)}, u32[]{:S(2)}) collective-permute-start(bf16[192,1536]{1,0:T(8,128)(2,1)S(1)} %get-tuple-element.38), channel_id=1, source_target_pairs={{0,2},{2,0},{1,3},{3,1},{4,6},{6,4},{5,7},{7,5},{8,10},{10,8},{9,1... | collective-permute-start | bytes 1769480 | tf_op jit(solution)/shard_map/ppermute | solution.py:477
  6.4 8.7 %collective-permute-start.5 = (bf16[256,512]{1,0:T(8,128)(2,1)S(1)}, bf16[256,512]{1,0:T(8,128)(2,1)S(1)}, u32[]{:S(2)}, u32[]{:S(2)}) collective-permute-start(bf16[256,512]{1,0:T(8,128)(2,1)S(1)} %get-tuple-element.23), channel_id=1, source_target_pairs={{0,4},{4,8},{8,12},{1,5},{5,9},{9,13},{2,6},{6,10},{10,14},{3,7},{... | collective-permute-start | bytes 786440 | tf_op jit(solution)/shard_map/ppermute | solution.py:503
  9.9 17.0 %collective-permute-start.1 = (bf16[96,1536]{1,0:T(8,128)(2,1)S(1)}, bf16[96,1536]{1,0:T(8,128)(2,1)S(1)}, u32[]{:S(2)}, u32[]{:S(2)}) collective-permute-start(bf16[96,1536]{1,0:T(8,128)(2,1)S(1)} %get-tuple-element.22), channel_id=1, source_target_pairs={{0,2},{2,0},{1,3},{3,1},{4,6},{6,4},{5,7},{7,5},{8,10},{10,8},{9,1... | collective-permute-start | bytes 884744 | tf_op jit(solution)/shard_map/ppermute | solution.py:477
  10.5 33.5 %collective-permute-start = (bf16[192,2304]{1,0:T(8,128)(2,1)S(1)}, bf16[192,2304]{1,0:T(8,128)(2,1)S(1)}, u32[]{:S(2)}, u32[]{:S(2)}) collective-permute-start(bf16[192,2304]{1,0:T(8,128)(2,1)S(1)} %copy-done), channel_id=1, source_target_pairs={{0,1},{1,0},{2,3},{3,2},{4,5},{5,4},{6,7},{7,6},{8,9},{9,8},{10,11... | collective-permute-start | bytes 2654216 | tf_op jit(solution)/shard_map/ppermute | solution.py:477
  10.5 24.0 %collective-permute-start.7 = (bf16[256,768]{1,0:T(8,128)(2,1)S(1)}, bf16[256,768]{1,0:T(8,128)(2,1)S(1)}, u32[]{:S(2)}, u32[]{:S(2)}) collective-permute-start(bf16[256,768]{1,0:T(8,128)(2,1)S(1)} %copy-done.2), channel_id=1, source_target_pairs={{0,2},{2,0},{1,3},{3,1},{4,6},{6,4},{5,7},{7,5},{8,10},{10,8},{9,1... | collective-permute-start | bytes 1179656 | tf_op jit(solution)/shard_map/ppermute | solution.py:477
  15.1 19.9 %collective-permute-start.6 = (bf16[256,768]{1,0:T(8,128)(2,1)S(1)}, bf16[256,768]{1,0:T(8,128)(2,1)S(1)}, u32[]{:S(2)}, u32[]{:S(2)}) collective-permute-start(bf16[256,768]{1,0:T(8,128)(2,1)S(1)} %copy-done.2), channel_id=1, source_target_pairs={{0,1},{1,0},{2,3},{3,2},{4,5},{5,4},{6,7},{7,6},{8,9},{9,8},{10,11... | collective-permute-start | bytes 1179656 | tf_op jit(solution)/shard_map/ppermute | solution.py:477
  26.9 8.2 %collective-permute-start.2 = (bf16[96,1536]{1,0:T(8,128)(2,1)S(1)}, bf16[96,1536]{1,0:T(8,128)(2,1)S(1)}, u32[]{:S(2)}, u32[]{:S(2)}) collective-permute-start(bf16[96,1536]{1,0:T(8,128)(2,1)S(1)} %collective-permute-done.1.refs_2_), channel_id=1, source_target_pairs={{0,16},{16,0},{1,17},{17,1},{2,18},{18,2},{3,19},{19,3},{4,20},{20... | collective-permute-start | bytes 884744 | tf_op jit(solution)/shard_map/ppermute | solution.py:477
  34.5 1.7 %collective-permute-start.8 = (bf16[256,768]{1,0:T(8,128)(2,1)S(1)}, bf16[256,768]{1,0:T(8,128)(2,1)S(1)}, u32[]{:S(2)}, u32[]{:S(2)}) collective-permute-start(bf16[256,768]{1,0:T(8,128)(2,1)S(1)} %collective-permute-done.7.refs_2_), channel_id=1, source_target_pairs={{0,1},{1,0},{2,3},{3,2},{4,5},{5,4},{6,7},{7,6},{8,9},{9,8},{10,11... | collective-permute-start | bytes 1179656 | tf_op jit(solution)/shard_map/ppermute | solution.py:477
  34.5 24.8 %collective-permute-start.13 = (bf16[192,1536]{1,0:T(8,128)(2,1)S(1)}, bf16[192,1536]{1,0:T(8,128)(2,1)S(1)}, u32[]{:S(2)}, u32[]{:S(2)}) collective-permute-start(bf16[192,1536]{1,0:T(8,128)(2,1)S(1)} %collective-permute-done.12.refs_6_.refs_10_), channel_id=1, source_target_pairs={{0,1},{1,0},{2,3},{3,2},{4,5},{5,4},{6,7},{7,6},{8,9},{9,8},{10,11... | collective-permute-start | bytes 1769480 | tf_op jit(solution)/shard_map/ppermute | solution.py:477
  35.0 4.5 %collective-permute-start.3 = (bf16[96,1536]{1,0:T(8,128)(2,1)S(1)}, bf16[96,1536]{1,0:T(8,128)(2,1)S(1)}, u32[]{:S(2)}, u32[]{:S(2)}) collective-permute-start(bf16[96,1536]{1,0:T(8,128)(2,1)S(1)} %collective-permute-done.1.refs_2_), channel_id=1, source_target_pairs={{0,1},{1,0},{2,3},{3,2},{4,5},{5,4},{6,7},{7,6},{8,9},{9,8},{10,11... | collective-permute-start | bytes 884744 | tf_op jit(solution)/shard_map/ppermute | solution.py:477
  35.0 6.3 %collective-permute-start.4 = (bf16[96,1536]{1,0:T(8,128)(2,1)S(1)}, bf16[96,1536]{1,0:T(8,128)(2,1)S(1)}, u32[]{:S(2)}, u32[]{:S(2)}) collective-permute-start(bf16[96,1536]{1,0:T(8,128)(2,1)S(1)} %collective-permute-done.2.refs_3_), channel_id=1, source_target_pairs={{0,1},{1,0},{2,3},{3,2},{4,5},{5,4},{6,7},{7,6},{8,9},{9,8},{10,11... | collective-permute-start | bytes 884744 | tf_op jit(solution)/shard_map/ppermute | solution.py:477
  36.2 16.4 %collective-permute-start.14 = (bf16[192,768]{1,0:T(8,128)(2,1)S(1)}, bf16[192,768]{1,0:T(8,128)(2,1)S(1)}, u32[]{:S(2)}, u32[]{:S(2)}) collective-permute-start(bf16[192,768]{1,0:T(8,128)(2,1)S(1)} %copy-done.1), channel_id=1, source_target_pairs={{0,1},{1,0},{2,3},{3,2},{4,5},{5,4},{6,7},{7,6},{8,9},{9,8},{10,11... | collective-permute-start | bytes 884744 | tf_op jit(solution)/shard_map/ppermute | solution.py:477
  37.0 14.0 %copy-start.3 = (s32[1,512]{1,0:T(1,128)S(1)}, s32[1,512]{1,0:T(1,128)}, u32[]{:S(2)}) copy-start(s32[1,512]{1,0:T(1,128)} %param.14) | copy-start | bytes 6148
  39.5 11.6 %collective-permute-start.9 = (bf16[136,768]{1,0:T(8,128)(2,1)S(1)}, bf16[136,768]{1,0:T(8,128)(2,1)S(1)}, u32[]{:S(2)}, u32[]{:S(2)}) collective-permute-start(bf16[136,768]{1,0:T(8,128)(2,1)S(1)} %back.1.refs_6_.refs_0_), channel_id=1, source_target_pairs={{0,4},{4,0},{8,12},{12,8},{1,5},{5,1},{9,13},{13,9},{2,6},{6,2},{1... | collective-permute-start | bytes 626696 | tf_op jit(solution)/shard_map/ppermute | solution.py:477
  41.3 17.9 %collective-permute-start.10 = (bf16[136,768]{1,0:T(8,128)(2,1)S(1)}, bf16[136,768]{1,0:T(8,128)(2,1)S(1)}, u32[]{:S(2)}, u32[]{:S(2)}) collective-permute-start(bf16[136,768]{1,0:T(8,128)(2,1)S(1)} %back.1.refs_6_.refs_0_), channel_id=1, source_target_pairs={{0,8},{4,12},{8,0},{12,4},{1,9},{5,13},{9,1},{13,5},{2,10},{6,14},... | collective-permute-start | bytes 626696 | tf_op jit(solution)/shard_map/ppermute | solution.py:477
  43.9 15.4 %collective-permute-start.11 = (bf16[136,768]{1,0:T(8,128)(2,1)S(1)}, bf16[136,768]{1,0:T(8,128)(2,1)S(1)}, u32[]{:S(2)}, u32[]{:S(2)}) collective-permute-start(bf16[136,768]{1,0:T(8,128)(2,1)S(1)} %back.1.refs_6_.refs_0_), channel_id=1, source_target_pairs={{0,12},{4,8},{8,4},{12,0},{1,13},{5,9},{9,5},{13,1},{2,14},{6,10},... | collective-permute-start | bytes 626696 | tf_op jit(solution)/shard_map/ppermute | solution.py:477
where the time goes:
time: 65.6 us; the launch traced here: 64.3 us
  waiting for transfers between devices  34.9 us (53%)
  starting transfers between devices  16.4 us (25%)
  Pallas kernels  13 us (20%)
    ppermute x14, waiting for transfers between devices, exchanged(): return lax.ppermute(value, axis, [(i, i ^ flip) for i in range(count)])  31.8 us
    ppermute x14, starting transfers between devices, exchanged(): return lax.ppermute(value, axis, [(i, i ^ flip) for i in range(count)])  12.9 us
    pallas_call x1, Pallas kernels, finish(): pl.pallas_call(functools.partial(finish_kernel, pieces=pieces, chunks=len...  5.05 us
    ppermute x1, starting transfers between devices, layer(): got = lax.ppermute(msg, 'seq', [(i, i + 1) for i in range(shards - 1)])  3.49 us
    pallas_call x1, Pallas kernels, front(): pl.pallas_call(functools.partial(front_kernel, wires=wires, channels=chan...  3.31 us
    ppermute x1, waiting for transfers between devices, layer(): got = lax.ppermute(msg, 'seq', [(i, i + 1) for i in range(shards - 1)])  3.07 us
    pallas_call x1, Pallas kernels, prepare(): pl.pallas_call(functools.partial(prepare_kernel, pieces=len(weights), chu...  1.53 us
  transfers between devices with their start and end apart: 15, of which 6 were waited for; matrix products, arithmetic and copies ran while one was open for 0% of the time, Pallas kernels for 7%

commit v1 on v0

--- a/solution.py
+++ b/solution.py
@@ -265,48 +265,79 @@
     lift(joined, normed, keys, values)
 
 
-def finish_kernel(perm_ref, joined, normed0, keys0, values0, *refs, pieces, chunks, early, count, swap):
+def extend_kernel(perm_ref, joined, normed0, *refs, pieces, chunks, early, swap):
     chunk_refs = refs[:chunks]
     weight_refs = refs[chunks : chunks + 2 * pieces]
-    out_ref, query, output, normed1, keys1, values1, cap, mixed, sems = refs[chunks + 2 * pieces :]
+    refs = refs[chunks + 2 * pieces :]
+    query, output, keys1, values1, token_ref, picked_ref, on_ref, normed1, sems = refs
     width = joined.shape[0]
-    sources = [[], []]
-    for kind in range(2):
+    count = token_ref.shape[0]
+    copies = []
+    for kind, target in enumerate((query, output)):
+        sources = []
         for piece in range(pieces):
             ref = weight_refs[kind * pieces + piece]
             depth = ref.shape[0]
             column = width if kind and piece > 1 else 0
-            sources[kind].append((ref, block_of(pieces > 1, piece) * depth, column, depth))
-    wait_query = collect(sources[0], query, sems.at[0])
-    wait_output = collect(sources[1], output, sems.at[1])
+            sources.append((ref, block_of(pieces > 1, piece) * depth, column, depth))
+        copies += collect(sources, target, sems.at[kind])
     for slot, ref in enumerate(chunk_refs[early:]):
         normed1[slot * count : (slot + 1) * count, :] = normal(ref[:count, :])
     lift(joined, normed1, keys1, values1)
+    own = own_rows(perm_ref, count, swap)
     near = early * count
+    picked_ref[...] = dot(own[:, :near], normed0[...]) + dot(own[:, near : chunks * count], normed1[...])
+    on, token = flags_and_tokens(perm_ref, own, chunk_refs, 0)
+    on_ref[...] = on
+    token_ref[...] = token
+    for copy in copies:
+        copy.wait()
+
+
+def own_rows(perm_ref, count, swap):
     slot = 0 if swap else lax.axis_index("seq")
-    own = perm_ref[pl.ds(pl.multiple_of(slot * count, count), count), :]
-    picked = (dot(own[:, :near], normed0[...]) + dot(own[:, near:], normed1[...])).astype(BF)
+    return perm_ref[pl.ds(pl.multiple_of(slot * count, count), count), :]
+
+
+def flags_and_tokens(perm_ref, own, chunk_refs, first):
+    count = own.shape[0]
+    on = token = 0.0
+    for slot, ref in enumerate(chunk_refs):
+        here = slice((first + slot) * count, (first + slot + 1) * count)
+        on += dot(ref[count:, :count], perm_ref[here, :])
+        token += dot(own[:, here], ref[:count, :])
+    return on, token
+
+
+def finish_kernel(
+    perm_ref, joined, keys0, values0, keys1, values1, query, output, token_ref, picked_ref, on_ref, *refs,
+    chunks, swap
+):
+    chunk_refs = refs[:chunks]
+    out_ref, normed2, keys2, values2, cap, mixed = refs[chunks:]
+    count, width = token_ref.shape
+    first = perm_ref.shape[0] // count - chunks
+    for slot, ref in enumerate(chunk_refs):
+        normed2[slot * count : (slot + 1) * count, :] = normal(ref[:count, :])
+    lift(joined, normed2, keys2, values2)
+    own = own_rows(perm_ref, count, swap)
+    picked = (picked_ref[...] + dot(own[:, first * count :], normed2[...])).astype(BF)
     head = width // HEADS
-    for copy in wait_query:
-        copy.wait()
     queries = (dot(picked, query[...]) * head ** (-0.5)).astype(BF)
-    on = None
-    token = None
-    for slot, ref in enumerate(chunk_refs):
-        here = slice(slot * count, (slot + 1) * count)
-        term = dot(ref[count:, :count], perm_ref[here, :])
-        on = term if on is None else on + term
-        term = dot(own[:, here], ref[:count, :])
-        token = term if token is None else token + term
+    on, token = flags_and_tokens(perm_ref, own, chunk_refs, first)
+    on += on_ref[...]
+    token += token_ref[...]
     allowed = (own.astype(F32) + jnp.broadcast_to(on[:1], own.shape)) > 0.5
     cap[...] = jnp.where(allowed, largest, masked_score)
     low = iota((count, 2 * head), 1) < head
+    groups = ((keys0, values0), (keys1, values1), (keys2, values2))
     for pair in range(HEADS // 2):
         here = slice(pair * 2 * head, (pair + 1) * 2 * head)
-        query = queries[:, here]
-        zero = jnp.zeros_like(query)
-        both = jnp.concatenate([jnp.where(low, query, zero), jnp.where(low, zero, query)], axis=0)
-        scores = jnp.concatenate([dot(both, keys0[:, here], 1, 1), dot(both, keys1[:, here], 1, 1)], axis=1)
+        part_query = queries[:, here]
+        zero = jnp.zeros_like(part_query)
+        both = [jnp.where(low, part_query, zero), jnp.where(low, zero, part_query)]
+        both = jnp.concatenate(both, axis=0)
+        scores = jnp.concatenate([dot(both, keys[:, here], 1, 1) for keys, _ in groups], axis=1)
         weights, scale = [], []
         for half in range(2):
             score = jnp.minimum(scores[half * count : (half + 1) * count], cap[...])
@@ -314,10 +345,11 @@
             scale.append(1.0 / jnp.sum(weight, axis=-1, keepdims=True))
             weights.append(weight.astype(BF))
         weights = jnp.concatenate(weights, axis=0)
-        part = dot(weights[:, :near], values0[:, here]) + dot(weights[:, near:], values1[:, here])
+        part, start = 0.0, 0
+        for keys, values in groups:
+            part += dot(weights[:, start : start + keys.shape[0]], values[:, here])
+            start += keys.shape[0]
         mixed[:, here] = jnp.where(low, part[:count] * scale[0], part[count:] * scale[1]).astype(BF)
-    for copy in wait_output:
-        copy.wait()
     out_ref[...] = (token + dot(mixed[...], output[...])).astype(BF)
 
 
@@ -442,34 +474,54 @@
     )(order, *weights, *chunks)
 
 
-def finish(ready, chunks, weights, early, swap):
-    joined, normed, keys, values, perm = ready
+def extend(ready, chunks, weights, early, swap):
+    joined, normed, _, _, perm = ready
     width = joined.shape[0]
     size = perm.shape[0]
-    count = size // len(chunks)
-    far = size - early * count
+    count = chunks[0].shape[0] - EXTRA
+    far = (len(chunks) - early) * count
     pieces = len(weights) // 2
     return pl.pallas_call(
-        functools.partial(
-            finish_kernel, pieces=pieces, chunks=len(chunks), early=early, count=count, swap=swap
+        functools.partial(extend_kernel, pieces=pieces, chunks=len(chunks), early=early, swap=swap),
+        out_shape=(
+            array((width, width)),
+            array((width, width)),
+            array((far, width)),
+            array((far, width)),
+            array((count, width), F32),
+            array((count, width), F32),
+            array((EXTRA, size), F32),
         ),
+        in_specs=[vmem()] * (3 + len(chunks)) + ([fixed()] + [hbm()] * (pieces - 1)) * 2,
+        out_specs=[vmem()] * 7,
+        scratch_shapes=[pltpu.VMEM((far, width), BF), pltpu.SemaphoreType.DMA((2, pieces))],
+        compiler_params=params(8 + size // 128),
+        name="extend",
+    )(perm, joined, normed, *chunks, *weights)
+
+
+def finish(ready, extra, chunks, swap):
+    joined, _, keys, values, perm = ready
+    query, output, keys1, values1, token, picked, on = extra
+    width = joined.shape[0]
+    size = perm.shape[0]
+    count = token.shape[0]
+    far = len(chunks) * count
+    return pl.pallas_call(
+        functools.partial(finish_kernel, chunks=len(chunks), swap=swap),
         out_shape=array((count, width)),
-        in_specs=[vmem()] * (5 + len(chunks))
-        + ([fixed()] + [hbm()] * (pieces - 1)) * 2,
+        in_specs=[vmem()] * (11 + len(chunks)),
         out_specs=vmem(),
         scratch_shapes=[
-            pltpu.VMEM((width, width), BF),
-            pltpu.VMEM((width, width), BF),
             pltpu.VMEM((far, width), BF),
             pltpu.VMEM((far, width), BF),
             pltpu.VMEM((far, width), BF),
             pltpu.VMEM((count, size), F32),
             pltpu.VMEM((count, width), BF),
-            pltpu.SemaphoreType.DMA((2, pieces)),
         ],
         compiler_params=params(8 + size // 64),
         name="finish",
-    )(perm, joined, normed, keys, values, *chunks, *weights)
+    )(perm, joined, keys, values, keys1, values1, query, output, token, picked, on, *chunks)
 
 
 def exchanged(value, axis, flip):
@@ -505,7 +557,8 @@
     token, low = mix(patch, embeds)
     tokens = back(got, (first, second, token, low), k1, k2, active)
     if swap:
-        chunks = [tokens] + [exchanged(tokens, "seq", flip) for flip in (1, 2, 3)]
+        chunks = [tokens] + [exchanged(tokens, "seq", flip) for flip in (1, 2)]
+        chunks.append(exchanged(chunks[2], "seq", 1))
     else:
         everyone = lax.all_gather(tokens, "seq", axis=0, tiled=True)
         chunks = [everyone[i * (count + EXTRA) : (i + 1) * (count + EXTRA)] for i in range(shards)]
@@ -524,9 +577,10 @@
     else:
         kv_weights = [lax.all_gather(project_weight, ("mp", "section"), axis=0, tiled=True)]
         last_weights = kv_weights + [lax.all_gather(output_weight, ("mp", "section"), axis=0, tiled=True)]
-    early = shards // 2
+    early, later = shards // 2, shards // 2 + shards // 4
     ready = prepare(order, kv_weights, chunks[:early], swap)
-    result = finish(ready, chunks, last_weights, early, swap)
+    extra = extend(ready, chunks[:later], last_weights, early, swap)
+    result = finish(ready, extra, chunks[later:], swap)
     return result[None]
 
 

time: 65.6 us -> 64.1 us (0.977); the launches traced: 64.3 us -> 64 us
  waiting for transfers between devices: 34.9 us -> 33.1 us
  starting transfers between devices: 16.4 us -> 17.4 us
    ppermute x1, waiting for transfers between devices: 3.07 us -> 0.62 us  [layer(): got = lax.ppermute(msg, 'seq', [(i, i + 1) for i in range(shards - 1)])]
    ppermute x14, starting transfers between devices: 12.9 us -> 13.6 us  [exchanged(): return lax.ppermute(value, axis, [(i, i ^ flip) for i in range(count)])]
    ppermute x14, waiting for transfers between devices: 31.8 us -> 32.5 us  [exchanged(): return lax.ppermute(value, axis, [(i, i ^ flip) for i in range(count)])]
    pallas_call x1 -> x2, Pallas kernels: 5.05 us -> 5.38 us  [the longest x1 4.08 us: finish(): pl.pallas_call(functools.partial(finish_kernel, chunks=len(chunks), swap=...]
  transfers between devices with their start and end apart: 15 -> 15, of which waited for: 6 -> 6; matrix products, arithmetic and copies ran while one was open for 0% -> 0% of each run, Pallas kernels for 7% -> 14%
where the time goes in v1:
time: 64.1 us; the launch traced here: 64 us
  waiting for transfers between devices  33.1 us (52%)
  starting transfers between devices  17.4 us (27%)
  Pallas kernels  13.3 us (21%)
    ppermute x14, waiting for transfers between devices, exchanged(): return lax.ppermute(value, axis, [(i, i ^ flip) for i in range(count)])  32.5 us
    ppermute x14, starting transfers between devices, exchanged(): return lax.ppermute(value, axis, [(i, i ^ flip) for i in range(count)])  13.6 us
    pallas_call x1, Pallas kernels, finish(): pl.pallas_call(functools.partial(finish_kernel, chunks=len(chunks), swap=...  4.08 us
    ppermute x1, starting transfers between devices, layer(): got = lax.ppermute(msg, 'seq', [(i, i + 1) for i in range(shards - 1)])  3.74 us
    pallas_call x1, Pallas kernels, front(): pl.pallas_call(functools.partial(front_kernel, wires=wires, channels=chan...  3.28 us
    pallas_call x1, Pallas kernels, prepare(): pl.pallas_call(functools.partial(prepare_kernel, pieces=len(weights), chu...  1.53 us
    pallas_call x1, Pallas kernels, extend(): pl.pallas_call(functools.partial(extend_kernel, pieces=pieces, chunks=len...  1.3 us
  transfers between devices with their start and end apart: 15, of which 6 were waited for; matrix products, arithmetic and copies ran while one was open for 0% of the time, Pallas kernels for 14%

profile of v1, /device:TPU:0, one launch (start us, length us, event | category | flops | bytes accessed | tf_op | source)
XLA Modules:
  0.0 64.0 jit_solution(1413550770984270501)
XLA Ops:
  0.0 3.0 %collective-permute-start.7 = (bf16[256,768]{1,0:T(8,128)(2,1)}, bf16[256,768]{1,0:T(8,128)(2,1)S(1)}, u32[]{:S(2)}, u32[]{:S(2)}) collective-permute-start(bf16[256,768]{1,0:T(8,128)(2,1)} %refs_0_.4), channel_id=1, source_target_pairs={{0,2},{2,0},{1,3},{3,1},{4,6},{6,4},{5,7},{7,5},{8,10},{10,8},{9,1... | collective-permute-start | bytes 1179656 | tf_op jit(solution)/shard_map/ppermute | solution.py:529
  3.0 3.3 %front.1 = (bf16[256,512]{1,0:T(8,128)(2,1)S(1)}, bf16[384,512]{1,0:T(8,128)(2,1)S(1)}, bf16[1152,256]{1,0:T(8,128)(2,1)S(1)}, bf16[576,128]{1,0:T(8,128)(2,1)S(...) custom-call(bf16[512,1024]{1,0:T(8,128)(2,1)} %bitcast.6, ...), custom_call_target="tpu_custom_call" | custom-call | tf_op jit(solution)/shard_map/front/pallas_call | solution.py:390
  6.3 0.1 collective-permute-start.11
  6.4 0.5 collective-permute-start.6
  6.9 6.2 %collective-permute-done.7.refs_2_ = bf16[256,768]{1,0:T(8,128)(2,1)S(1)} collective-permute-done((bf16[256,768]{1,0:T(8,128)(2,1)}, bf16[256,768]{1,0:T(8,128)(2,1)S(1)}, u32[]{:S(2)}, u32[]{:S(2)}) %collective-permute-start.7) | collective-permute-done | bytes 393248 | tf_op jit(solution)/shard_map/ppermute | solution.py:529
  13.1 2.0 %collective-permute-start.1 = (bf16[96,1536]{1,0:T(8,128)(2,1)S(1)}, bf16[96,1536]{1,0:T(8,128)(2,1)S(1)}, u32[]{:S(2)}, u32[]{:S(2)}) collective-permute-start(bf16[96,1536]{1,0:T(8,128)(2,1)S(1)} %get-tuple-element.29), channel_id=1, source_target_pairs={{0,2},{2,0},{1,3},{3,1},{4,6},{6,4},{5,7},{7,5},{8,10},{10,8},{9,1... | collective-permute-start | bytes 884744 | tf_op jit(solution)/shard_map/ppermute | solution.py:529
  15.2 16.1 %collective-permute-done.1.refs_2_ = bf16[96,1536]{1,0:T(8,128)(2,1)S(1)} collective-permute-done((bf16[96,1536]{1,0:T(8,128)(2,1)S(1)}, bf16[96,1536]{1,0:T(8,128)(2,1)S(1)}, u32[]{:S(2)}, u32[]{:S(2)}) %collective-permute-start.1) | collective-permute-done | bytes 294944 | tf_op jit(solution)/shard_map/ppermute | solution.py:529
  31.2 3.7 %collective-permute-start.5 = (bf16[256,512]{1,0:T(8,128)(2,1)S(1)}, bf16[256,512]{1,0:T(8,128)(2,1)S(1)}, u32[]{:S(2)}, u32[]{:S(2)}) collective-permute-start(bf16[256,512]{1,0:T(8,128)(2,1)S(1)} %get-tuple-element.30), channel_id=1, source_target_pairs={{0,4},{4,8},{8,12},{1,5},{5,9},{9,13},{2,6},{6,10},{10,14},{3,7},{... | collective-permute-start | bytes 786440 | tf_op jit(solution)/shard_map/ppermute | solution.py:555
  35.0 1.6 %collective-permute-start.2 = (bf16[96,1536]{1,0:T(8,128)(2,1)S(1)}, bf16[96,1536]{1,0:T(8,128)(2,1)S(1)}, u32[]{:S(2)}, u32[]{:S(2)}) collective-permute-start(bf16[96,1536]{1,0:T(8,128)(2,1)S(1)} %collective-permute-done.1.refs_2_), channel_id=1, source_target_pairs={{0,16},{16,0},{1,17},{17,1},{2,18},{18,2},{3,19},{19,3},{4,20},{20... | collective-permute-start | bytes 884744 | tf_op jit(solution)/shard_map/ppermute | solution.py:529
  36.6 0.5 collective-permute-start.12
  37.1 0.7 %central.1 = (f32[128,512]{1,0:T(8,128)S(1)}, f32[256,256]{1,0:T(8,128)S(1)}, bf16[512,128]{1,0:T(8,128)(2,1)S(1)}) custom-call(bf16[384,512]{1,0:T(8,128)(2,1)S(1)} %get-tuple-element.31.taps1_ref, bf16[1152,256]{1,0:T(8,128)(2,1)S(1)} %get-tuple-element.32.taps2_ref, bf16[576,128]{1,0:T(8,128)(2,1)S(1)} %get-tuple-element.33.k1_ref, ...), custom_call_target="tpu_custom_call" | custom-call | tf_op jit(solution)/shard_map/central/pallas_call | solution.py:410
  37.8 1.2 %mix.1 = (f32[128,768]{1,0:T(8,128)S(1)}, bf16[512,768]{1,0:T(8,128)(2,1)S(1)}) custom-call(bf16[512,128]{1,0:T(8,128)(2,1)S(1)} %get-tuple-element.37.patch, bf16[256,768]{1,0:T(8,128)(2,1)S(1)} %copy-done.2, bf16[256,768]{1,0:T(8,128)(2,1)S(1)} %collective-permute-done.6.refs_1_, bf16[256,768]{1,0:T(8,128)(2,1)S(1)} %collective-permute-done.7.refs_2_, ...), custom_call_target="tpu_custom_call" | custom-call | tf_op jit(solution)/shard_map/mix/pallas_call | solution.py:426
  39.1 0.6 collective-permute-done.5.got_ref
  39.7 1.2 %back.1.refs_6_.refs_0_ = bf16[136,768]{1,0:T(8,128)(2,1)S(1)} custom-call(bf16[256,512]{1,0:T(8,128)(2,1)S(1)} %collective-permute-done.5.got_ref, f32[128,512]{1,0:T(8,128)S(1)} %get-tuple-element.35.first_ref, f32[256,256]{1,0:T(8,128)S(1)} %get-tuple-element.36.second_ref, f32[128,768]{1,0:T(8,128)S(1)} %get-tuple-element.38.token_ref, ...), custom_call_target="tpu_custom_call" | custom-call | tf_op jit(solution)/shard_map/back/pallas_call | solution.py:447
  40.9 3.6 %collective-permute-start.10 = (bf16[136,768]{1,0:T(8,128)(2,1)S(1)}, bf16[136,768]{1,0:T(8,128)(2,1)S(1)}, u32[]{:S(2)}, u32[]{:S(2)}) collective-permute-start(bf16[136,768]{1,0:T(8,128)(2,1)S(1)} %back.1.refs_6_.refs_0_), channel_id=1, source_target_pairs={{0,8},{4,12},{8,0},{12,4},{1,9},{5,13},{9,1},{13,5},{2,10},{6,14},... | collective-permute-start | bytes 626696 | tf_op jit(solution)/shard_map/ppermute | solution.py:529
  44.4 0.5 collective-permute-start.13
  44.9 1.6 %collective-permute-start.9 = (bf16[136,768]{1,0:T(8,128)(2,1)S(1)}, bf16[136,768]{1,0:T(8,128)(2,1)S(1)}, u32[]{:S(2)}, u32[]{:S(2)}) collective-permute-start(bf16[136,768]{1,0:T(8,128)(2,1)S(1)} %back.1.refs_6_.refs_0_), channel_id=1, source_target_pairs={{0,4},{4,0},{8,12},{12,8},{1,5},{5,1},{9,13},{13,9},{2,6},{6,2},{1... | collective-permute-start | bytes 626696 | tf_op jit(solution)/shard_map/ppermute | solution.py:529
  46.5 6.4 %collective-permute-done.10.refs_2_ = bf16[136,768]{1,0:T(8,128)(2,1)S(1)} collective-permute-done((bf16[136,768]{1,0:T(8,128)(2,1)S(1)}, bf16[136,768]{1,0:T(8,128)(2,1)S(1)}, u32[]{:S(2)}, u32[]{:S(2)}) %collective-permute-start.10) | collective-permute-done | bytes 208928 | tf_op jit(solution)/shard_map/ppermute | solution.py:529
  53.0 0.3 collective-permute-start.14
  53.2 2.7 %collective-permute-done.9.refs_7_.refs_1_ = bf16[136,768]{1,0:T(8,128)(2,1)S(1)} collective-permute-done((bf16[136,768]{1,0:T(8,128)(2,1)S(1)}, bf16[136,768]{1,0:T(8,128)(2,1)S(1)}, u32[]{:S(2)}, u32[]{:S(2)}) %collective-permute-start.9) | collective-permute-done | bytes 208928 | tf_op jit(solution)/shard_map/ppermute | solution.py:529
  56.0 1.5 %prepare.1 = (bf16[768,1536]{1,0:T(8,128)(2,1)S(1)}, bf16[256,768]{1,0:T(8,128)(2,1)S(1)}, bf16[256,768]{1,0:T(8,128)(2,1)S(1)}, bf16[256,768]{1,0:T(8,128)(2,1)S(1)}, bf16[512,512]{1,0:T(8,128)(2,1)S(1)}) custom-call(s32[4,128]{1,0:T(4,128)S(1)} %bitcast.5, bf16[192,2304]{1,0:T(8,128)(2,1)S(1)} %copy-done, ...), custom_call_target="tpu_custom_call" | custom-call | tf_op jit(solution)/shard_map/prepare/pallas_call | solution.py:466
  57.5 1.3 %extend.1 = (bf16[768,768]{1,0:T(8,128)(2,1)S(1)}, bf16[768,768]{1,0:T(8,128)(2,1)S(1)}, bf16[128,768]{1,0:T(8,128)(2,1)S(1)}, bf16[128,768]{1,0:T(8,128)(2,1)S(...) custom-call(bf16[512,512]{1,0:T(8,128)(2,1)S(1)} %get-tuple-element.40.perm_ref, ...), custom_call_target="tpu_custom_call" | custom-call | tf_op jit(solution)/shard_map/extend/pallas_call | solution.py:484
  58.9 1.0 %collective-permute-done.14.refs_0_ = bf16[136,768]{1,0:T(8,128)(2,1)S(1)} collective-permute-done((bf16[136,768]{1,0:T(8,128)(2,1)S(1)}, bf16[136,768]{1,0:T(8,128)(2,1)S(1)}, u32[]{:S(2)}, u32[]{:S(2)}) %collective-permute-start.14) | collective-permute-done | bytes 208928 | tf_op jit(solution)/shard_map/ppermute | solution.py:529
  59.9 4.1 %finish.1 = bf16[128,768]{1,0:T(8,128)(2,1)} custom-call(bf16[512,512]{1,0:T(8,128)(2,1)S(1)} %get-tuple-element.40.perm_ref, bf16[768,1536]{1,0:T(8,128)(2,1)S(1)} %get-tuple-element.41.joined, bf16[256,768]{1,0:T(8,128)(2,1)S(1)} %get-tuple-element.42.keys0, bf16[256,768]{1,0:T(8,128)(2,1)S(1)} %get-tuple-element.43.values0, ...), custom_call_target="tpu_custom_call" | custom-call | tf_op jit(solution)/shard_map/finish/pallas_call | solution.py:510
  (23 shorter events, 0.1 us)
Async XLA Ops:
  0.0 13.1 %collective-permute-start.7 = (bf16[256,768]{1,0:T(8,128)(2,1)}, bf16[256,768]{1,0:T(8,128)(2,1)S(1)}, u32[]{:S(2)}, u32[]{:S(2)}) collective-permute-start(bf16[256,768]{1,0:T(8,128)(2,1)} %refs_0_.4), channel_id=1, source_target_pairs={{0,2},{2,0},{1,3},{3,1},{4,6},{6,4},{5,7},{7,5},{8,10},{10,8},{9,1... | collective-permute-start | bytes 1179656 | tf_op jit(solution)/shard_map/ppermute | solution.py:529
  3.0 3.4 %copy-start = (bf16[192,2304]{1,0:T(8,128)(2,1)S(1)}, bf16[192,2304]{1,0:T(8,128)(2,1)}, u32[]{:S(2)}) copy-start(bf16[192,2304]{1,0:T(8,128)(2,1)} %refs_3_.1) | copy-start | bytes 2654212
  3.0 3.5 %copy-start.2 = (bf16[256,768]{1,0:T(8,128)(2,1)S(1)}, bf16[256,768]{1,0:T(8,128)(2,1)}, u32[]{:S(2)}) copy-start(bf16[256,768]{1,0:T(8,128)(2,1)} %refs_0_.4) | copy-start | bytes 1179652
  6.3 30.3 %collective-permute-start.11 = (bf16[192,1536]{1,0:T(8,128)(2,1)S(1)}, bf16[192,1536]{1,0:T(8,128)(2,1)S(1)}, u32[]{:S(2)}, u32[]{:S(2)}) collective-permute-start(bf16[192,1536]{1,0:T(8,128)(2,1)S(1)} %get-tuple-element.45), channel_id=1, source_target_pairs={{0,2},{2,0},{1,3},{3,1},{4,6},{6,4},{5,7},{7,5},{8,10},{10,8},{9,1... | collective-permute-start | bytes 1769480 | tf_op jit(solution)/shard_map/ppermute | solution.py:529
  6.3 38.6 %collective-permute-start = (bf16[192,2304]{1,0:T(8,128)(2,1)S(1)}, bf16[192,2304]{1,0:T(8,128)(2,1)S(1)}, u32[]{:S(2)}, u32[]{:S(2)}) collective-permute-start(bf16[192,2304]{1,0:T(8,128)(2,1)S(1)} %copy-done), channel_id=1, source_target_pairs={{0,1},{1,0},{2,3},{3,2},{4,5},{5,4},{6,7},{7,6},{8,9},{9,8},{10,11... | collective-permute-start | bytes 2654216 | tf_op jit(solution)/shard_map/ppermute | solution.py:529
  6.4 28.6 %collective-permute-start.6 = (bf16[256,768]{1,0:T(8,128)(2,1)S(1)}, bf16[256,768]{1,0:T(8,128)(2,1)S(1)}, u32[]{:S(2)}, u32[]{:S(2)}) collective-permute-start(bf16[256,768]{1,0:T(8,128)(2,1)S(1)} %copy-done.2), channel_id=1, source_target_pairs={{0,1},{1,0},{2,3},{3,2},{4,5},{5,4},{6,7},{7,6},{8,9},{9,8},{10,11... | collective-permute-start | bytes 1179656 | tf_op jit(solution)/shard_map/ppermute | solution.py:529
  13.1 23.5 %collective-permute-start.8 = (bf16[256,768]{1,0:T(8,128)(2,1)S(1)}, bf16[256,768]{1,0:T(8,128)(2,1)S(1)}, u32[]{:S(2)}, u32[]{:S(2)}) collective-permute-start(bf16[256,768]{1,0:T(8,128)(2,1)S(1)} %collective-permute-done.7.refs_2_), channel_id=1, source_target_pairs={{0,1},{1,0},{2,3},{3,2},{4,5},{5,4},{6,7},{7,6},{8,9},{9,8},{10,11... | collective-permute-start | bytes 1179656 | tf_op jit(solution)/shard_map/ppermute | solution.py:529
  13.1 18.1 %collective-permute-start.1 = (bf16[96,1536]{1,0:T(8,128)(2,1)S(1)}, bf16[96,1536]{1,0:T(8,128)(2,1)S(1)}, u32[]{:S(2)}, u32[]{:S(2)}) collective-permute-start(bf16[96,1536]{1,0:T(8,128)(2,1)S(1)} %get-tuple-element.29), channel_id=1, source_target_pairs={{0,2},{2,0},{1,3},{3,1},{4,6},{6,4},{5,7},{7,5},{8,10},{10,8},{9,1... | collective-permute-start | bytes 884744 | tf_op jit(solution)/shard_map/ppermute | solution.py:529
  31.2 8.4 %collective-permute-start.5 = (bf16[256,512]{1,0:T(8,128)(2,1)S(1)}, bf16[256,512]{1,0:T(8,128)(2,1)S(1)}, u32[]{:S(2)}, u32[]{:S(2)}) collective-permute-start(bf16[256,512]{1,0:T(8,128)(2,1)S(1)} %get-tuple-element.30), channel_id=1, source_target_pairs={{0,4},{4,8},{8,12},{1,5},{5,9},{9,13},{2,6},{6,10},{10,14},{3,7},{... | collective-permute-start | bytes 786440 | tf_op jit(solution)/shard_map/ppermute | solution.py:555
  35.0 9.4 %collective-permute-start.2 = (bf16[96,1536]{1,0:T(8,128)(2,1)S(1)}, bf16[96,1536]{1,0:T(8,128)(2,1)S(1)}, u32[]{:S(2)}, u32[]{:S(2)}) collective-permute-start(bf16[96,1536]{1,0:T(8,128)(2,1)S(1)} %collective-permute-done.1.refs_2_), channel_id=1, source_target_pairs={{0,16},{16,0},{1,17},{17,1},{2,18},{18,2},{3,19},{19,3},{4,20},{20... | collective-permute-start | bytes 884744 | tf_op jit(solution)/shard_map/ppermute | solution.py:529
  36.6 7.8 %collective-permute-start.3 = (bf16[96,1536]{1,0:T(8,128)(2,1)S(1)}, bf16[96,1536]{1,0:T(8,128)(2,1)S(1)}, u32[]{:S(2)}, u32[]{:S(2)}) collective-permute-start(bf16[96,1536]{1,0:T(8,128)(2,1)S(1)} %collective-permute-done.1.refs_2_), channel_id=1, source_target_pairs={{0,1},{1,0},{2,3},{3,2},{4,5},{5,4},{6,7},{7,6},{8,9},{9,8},{10,11... | collective-permute-start | bytes 884744 | tf_op jit(solution)/shard_map/ppermute | solution.py:529
  36.6 20.9 %collective-permute-start.12 = (bf16[192,1536]{1,0:T(8,128)(2,1)S(1)}, bf16[192,1536]{1,0:T(8,128)(2,1)S(1)}, u32[]{:S(2)}, u32[]{:S(2)}) collective-permute-start(bf16[192,1536]{1,0:T(8,128)(2,1)S(1)} %collective-permute-done.11.refs_5_.refs_9_), channel_id=1, source_target_pairs={{0,1},{1,0},{2,3},{3,2},{4,5},{5,4},{6,7},{7,6},{8,9},{9,8},{10,11... | collective-permute-start | bytes 1769480 | tf_op jit(solution)/shard_map/ppermute | solution.py:529
  37.8 1.9 %copy-start.4 = (s32[1,128]{1,0:T(1,128)S(1)}, s32[1,128]{1,0:T(1,128)}, u32[]{:S(2)}) copy-start(s32[1,128]{1,0:T(1,128)} %active_ref.1) | copy-start | bytes 1540
  39.7 4.8 %copy-start.1 = (bf16[192,768]{1,0:T(8,128)(2,1)S(1)}, bf16[192,768]{1,0:T(8,128)(2,1)}, u32[]{:S(2)}) copy-start(bf16[192,768]{1,0:T(8,128)(2,1)} %refs_7_.1) | copy-start | bytes 884740
  39.7 16.3 %copy-start.3 = (s32[1,512]{1,0:T(1,128)S(1)}, s32[1,512]{1,0:T(1,128)}, u32[]{:S(2)}) copy-start(s32[1,512]{1,0:T(1,128)} %param.14) | copy-start | bytes 6148
  40.9 12.1 %collective-permute-start.10 = (bf16[136,768]{1,0:T(8,128)(2,1)S(1)}, bf16[136,768]{1,0:T(8,128)(2,1)S(1)}, u32[]{:S(2)}, u32[]{:S(2)}) collective-permute-start(bf16[136,768]{1,0:T(8,128)(2,1)S(1)} %back.1.refs_6_.refs_0_), channel_id=1, source_target_pairs={{0,8},{4,12},{8,0},{12,4},{1,9},{5,13},{9,1},{13,5},{2,10},{6,14},... | collective-permute-start | bytes 626696 | tf_op jit(solution)/shard_map/ppermute | solution.py:529
  44.4 8.8 %collective-permute-start.4 = (bf16[96,1536]{1,0:T(8,128)(2,1)S(1)}, bf16[96,1536]{1,0:T(8,128)(2,1)S(1)}, u32[]{:S(2)}, u32[]{:S(2)}) collective-permute-start(bf16[96,1536]{1,0:T(8,128)(2,1)S(1)} %collective-permute-done.2.refs_3_), channel_id=1, source_target_pairs={{0,1},{1,0},{2,3},{3,2},{4,5},{5,4},{6,7},{7,6},{8,9},{9,8},{10,11... | collective-permute-start | bytes 884744 | tf_op jit(solution)/shard_map/ppermute | solution.py:529
  44.4 13.1 %collective-permute-start.13 = (bf16[192,768]{1,0:T(8,128)(2,1)S(1)}, bf16[192,768]{1,0:T(8,128)(2,1)S(1)}, u32[]{:S(2)}, u32[]{:S(2)}) collective-permute-start(bf16[192,768]{1,0:T(8,128)(2,1)S(1)} %copy-done.1), channel_id=1, source_target_pairs={{0,1},{1,0},{2,3},{3,2},{4,5},{5,4},{6,7},{7,6},{8,9},{9,8},{10,11... | collective-permute-start | bytes 884744 | tf_op jit(solution)/shard_map/ppermute | solution.py:529
  44.9 11.0 %collective-permute-start.9 = (bf16[136,768]{1,0:T(8,128)(2,1)S(1)}, bf16[136,768]{1,0:T(8,128)(2,1)S(1)}, u32[]{:S(2)}, u32[]{:S(2)}) collective-permute-start(bf16[136,768]{1,0:T(8,128)(2,1)S(1)} %back.1.refs_6_.refs_0_), channel_id=1, source_target_pairs={{0,4},{4,0},{8,12},{12,8},{1,5},{5,1},{9,13},{13,9},{2,6},{6,2},{1... | collective-permute-start | bytes 626696 | tf_op jit(solution)/shard_map/ppermute | solution.py:529
  53.0 6.9 %collective-permute-start.14 = (bf16[136,768]{1,0:T(8,128)(2,1)S(1)}, bf16[136,768]{1,0:T(8,128)(2,1)S(1)}, u32[]{:S(2)}, u32[]{:S(2)}) collective-permute-start(bf16[136,768]{1,0:T(8,128)(2,1)S(1)} %collective-permute-done.10.refs_2_), channel_id=1, source_target_pairs={{0,4},{4,0},{8,12},{12,8},{1,5},{5,1},{9,13},{13,9},{2,6},{6,2},{1... | collective-permute-start | bytes 626696 | tf_op jit(solution)/shard_map/ppermute | solution.py:529

commit v2 on v1

--- a/solution.py
+++ b/solution.py
@@ -68,12 +68,30 @@
     return (lax.axis_index("mp") * 2 + lax.axis_index("section")) ^ flip
 
 
+def wire_rows(x_ref, block, first, wires, part):
+    height = (wires - first[0]) * part if first[1] is None else (first[1] - first[0]) * part
+    row, col = iota((height, 256), 0), iota((height, 256), 1)
+    mixer = one_hot(col == (row % part) * wires + row // part + first[0])
+    return dot(mixer, x_ref[block * 256 : (block + 1) * 256, :]).astype(BF)
+
+
+def fill_taps(taps, rows, block, splitter, part, channels):
+    even, odd = split_time(rows, splitter)
+    lagged = later(odd)
+    for wire in range(rows.shape[0] // part):
+        here = slice(wire * part, (wire + 1) * part)
+        base = wire * 3 * channels + block * part
+        taps[base : base + part, :] = lagged[here].astype(BF)
+        taps[base + channels : base + channels + part, :] = even[here].astype(BF)
+        taps[base + 2 * channels : base + 2 * channels + part, :] = odd[here].astype(BF)
+
+
 def front_kernel(x_hbm, k1_hbm, k2_hbm, *refs, wires, channels, middle, paired):
     if paired:
-        project_hbm, output_hbm = refs[:2]
-        refs = refs[2:]
-    msg_ref, taps1_ref, taps2_ref, k1_ref, k2_ref = refs[:5]
-    all1, x_ref, sems = refs[-3:]
+        project_hbm = refs[0]
+        refs = refs[1:]
+    msg_ref, x_ref, k1_ref, k2_ref = refs[:4]
+    taps, sems = refs[-2:]
     part = 256 // wires
     blocks = channels // part
     loads = []
@@ -83,8 +101,8 @@
     loads.append(pltpu.make_async_copy(k1_hbm, k1_ref, sems.at[blocks]))
     others = [pltpu.make_async_copy(k2_hbm, k2_ref, sems.at[blocks + 1])]
     if paired:
-        near_ref, query_ref = refs[5:7]
-        depth, width = output_hbm.shape
+        near_ref, query_ref = refs[4:6]
+        depth, width = query_ref.shape
         half = depth // 2
         rows = pl.ds(pl.multiple_of(lax.axis_index("groups") * half, half), half)
         others.append(
@@ -93,50 +111,41 @@
             )
         )
         others.append(
-            pltpu.make_async_copy(
-                project_hbm.at[:, pl.ds(0, width)], query_ref.at[:, pl.ds(0, width)], sems.at[blocks + 3]
-            )
-        )
-        others.append(
-            pltpu.make_async_copy(output_hbm, query_ref.at[:, pl.ds(width, width)], sems.at[blocks + 4])
+            pltpu.make_async_copy(project_hbm.at[:, pl.ds(0, width)], query_ref, sems.at[blocks + 3])
         )
     for copy in loads + others:
         copy.start()
     splitter = split_matrix()
-    row, col = iota((256, 256), 0), iota((256, 256), 1)
-    mixer = one_hot(col == (row % part) * wires + row // part)
     for block in range(blocks):
         loads[block].wait()
-        rows = dot(mixer, x_ref[block * 256 : (block + 1) * 256, :]).astype(BF)
-        even, odd = split_time(rows, splitter)
-        lagged = later(odd)
-        for wire in range(wires):
-            here = slice(wire * part, (wire + 1) * part)
-            base = wire * 3 * channels + block * part
-            all1[base : base + part, :] = lagged[here].astype(BF)
-            all1[base + channels : base + channels + part, :] = even[here].astype(BF)
-            all1[base + 2 * channels : base + 2 * channels + part, :] = odd[here].astype(BF)
-    taps1_ref[...] = all1[: 6 * channels, :]
-    last = (wires - 1) * 3 * channels
-    msg_ref[: 2 * channels, :] = all1[last + channels : last + 3 * channels, :]
+        rows = wire_rows(x_ref, block, (wires - 3, None), wires, part)
+        fill_taps(taps, rows, block, splitter, part, channels)
+    msg_ref[: 2 * channels, :] = taps[7 * channels :, :]
     loads[blocks].wait()
-    k1 = k1_ref[...]
-    for level in range(1, wires // 2):
-        start = (2 * level - 1) * 3 * channels
-        out = silu(dot(k1, all1[start : start + 9 * channels, :], 0, 0)).astype(BF)
-        if level == wires // 2 - 1:
-            msg_ref[2 * channels :, :] = out
-        even, odd = split_time(out, splitter)
-        store_taps(taps2_ref, (level - 1) * 3 * middle, even, odd)
+    msg_ref[2 * channels :, :] = silu(dot(k1_ref[...], taps[...], 0, 0)).astype(BF)
     for copy in others:
         copy.wait()
 
 
-def central_kernel(taps1_ref, taps2_ref, k1_ref, k2_ref, first_ref, second_ref, patch, *, channels, middle):
+def central_kernel(
+    msg_ref, x_ref, k1_ref, k2_ref, first_ref, second_ref, patch, taps1, taps2, *, wires, channels, middle
+):
     splitter = split_matrix()
-    first_ref[...] = dot(k1_ref[3 * channels :, :], taps1_ref[...], 0, 0)
-    second_ref[...] = dot(k2_ref[6 * middle :, :], taps2_ref[: 3 * middle, :], 0, 0)
-    out = silu(dot(k2_ref[...], taps2_ref[...], 0, 0)).astype(BF)
+    part = 256 // wires
+    for block in range(channels // part):
+        rows = wire_rows(x_ref, block, (0, wires - 2), wires, part)
+        fill_taps(taps1, rows, block, splitter, part, channels)
+    first_ref[...] = dot(k1_ref[3 * channels :, :], taps1[: 6 * channels, :], 0, 0)
+    for level in range(1, wires // 2):
+        if level == wires // 2 - 1:
+            out = msg_ref[2 * channels :, :]
+        else:
+            start = (2 * level - 1) * 3 * channels
+            out = silu(dot(k1_ref[...], taps1[start : start + 9 * channels, :], 0, 0)).astype(BF)
+        even, odd = split_time(out, splitter)
+        store_taps(taps2, (level - 1) * 3 * middle, even, odd)
+    second_ref[...] = dot(k2_ref[6 * middle :, :], taps2[: 3 * middle, :], 0, 0)
+    out = silu(dot(k2_ref[...], taps2[...], 0, 0)).astype(BF)
     store_patch(patch, out, splitter)
 
 
@@ -270,7 +279,6 @@
     weight_refs = refs[chunks : chunks + 2 * pieces]
     refs = refs[chunks + 2 * pieces :]
     query, output, keys1, values1, token_ref, picked_ref, on_ref, normed1, sems = refs
-    width = joined.shape[0]
     count = token_ref.shape[0]
     copies = []
     for kind, target in enumerate((query, output)):
@@ -278,8 +286,7 @@
         for piece in range(pieces):
             ref = weight_refs[kind * pieces + piece]
             depth = ref.shape[0]
-            column = width if kind and piece > 1 else 0
-            sources.append((ref, block_of(pieces > 1, piece) * depth, column, depth))
+            sources.append((ref, block_of(pieces > 1, piece) * depth, 0, depth))
         copies += collect(sources, target, sems.at[kind])
     for slot, ref in enumerate(chunk_refs[early:]):
         normed1[slot * count : (slot + 1) * count, :] = normal(ref[:count, :])
@@ -377,48 +384,47 @@
     channels = rows.shape[0] // wires
     middle = k1.shape[1]
     length = rows.shape[1] // 2
-    outs = [
-        array((2 * channels + middle, length)),
-        array((6 * channels, length)),
-        array(((wires // 2 - 1) * 3 * middle, length // 2)),
-        array(k1.shape),
-        array(k2.shape),
-    ]
+    outs = [array((2 * channels + middle, length)), array(rows.shape), array(k1.shape), array(k2.shape)]
     if weights:
-        depth, width = weights[1].shape
-        outs += [array((depth // 2, 2 * width)), array((depth, 2 * width))]
+        depth, width = weights[0].shape
+        outs += [array((depth // 2, width // 3 * 2)), array((depth, width // 3))]
+    operands = [pltpu.with_memory_space_constraint(v, pltpu.HBM) for v in (rows, k1, k2, *weights)]
     return pl.pallas_call(
         functools.partial(
             front_kernel, wires=wires, channels=channels, middle=middle, paired=len(weights) > 0
         ),
         out_shape=outs,
-        in_specs=[fixed()] * (3 + len(weights)),
+        in_specs=[fixed()] * len(operands),
         out_specs=[vmem()] * len(outs),
         scratch_shapes=[
-            pltpu.VMEM((wires * 3 * channels, length), BF),
-            pltpu.VMEM(rows.shape, BF),
-            pltpu.SemaphoreType.DMA((channels * wires // 256 + 5,)),
+            pltpu.VMEM((9 * channels, length), BF),
+            pltpu.SemaphoreType.DMA((channels * wires // 256 + 4,)),
         ],
-        compiler_params=params(12),
+        compiler_params=params(8),
         name="front",
-    )(*[pltpu.with_memory_space_constraint(v, pltpu.HBM) for v in (rows, k1, k2, *weights)])
-
-
-def central(taps1, taps2, k1, k2, count):
+    )(*operands)
+
+
+def central(msg, rows, k1, k2, wires, count):
     middle, outer = k1.shape[1], k2.shape[1]
     channels = k1.shape[0] // 9
+    length = msg.shape[1]
     return pl.pallas_call(
-        functools.partial(central_kernel, channels=channels, middle=middle),
+        functools.partial(central_kernel, wires=wires, channels=channels, middle=middle),
         out_shape=(
-            array((middle, taps1.shape[1]), F32),
-            array((outer, taps2.shape[1]), F32),
+            array((middle, length), F32),
+            array((outer, length // 2), F32),
             array((2 * outer, count)),
         ),
         in_specs=[vmem()] * 4,
         out_specs=[vmem()] * 3,
-        compiler_params=params(8),
+        scratch_shapes=[
+            pltpu.VMEM(((wires - 2) * 3 * channels, length), BF),
+            pltpu.VMEM(((wires // 2 - 1) * 3 * middle, length // 2), BF),
+        ],
+        compiler_params=params(10),
         name="central",
-    )(taps1, taps2, k1, k2)
+    )(msg, rows, k1, k2)
 
 
 def mix(patch, embeds):
@@ -541,19 +547,17 @@
     order = order.reshape(shards, -1)
     count = order.shape[1]
     rows = readout.reshape(channels * wires, ticks)
-    weights = (project_weight, output_weight)
     if paired:
         embed_across = exchanged(embed_weight, "mp", 1)
         embed_beside = exchanged(embed_weight, "section", 1)
         embeds = [embed_weight, embed_beside, embed_across]
         embeds.append(exchanged(embed_across, "section", 1))
-        front_out = front(rows, k1, k2, wires, weights)
-        msg, taps1, taps2, k1, k2, near, packed = front_out
+        msg, rows, k1, k2, near, query = front(rows, k1, k2, wires, (project_weight,))
     else:
         embeds = [lax.all_gather(embed_weight, ("mp", "section"), axis=0, tiled=True)]
-        msg, taps1, taps2, k1, k2 = front(rows, k1, k2, wires, ())
+        msg, rows, k1, k2 = front(rows, k1, k2, wires, ())
     got = lax.ppermute(msg, "seq", [(i, i + 1) for i in range(shards - 1)])
-    first, second, patch = central(taps1, taps2, k1, k2, count)
+    first, second, patch = central(msg, rows, k1, k2, wires, count)
     token, low = mix(patch, embeds)
     tokens = back(got, (first, second, token, low), k1, k2, active)
     if swap:
@@ -567,13 +571,15 @@
         output_beside = exchanged(output_weight, "section", 1)
         near = exchanged(near, "mp", 1)
         far = exchanged(near, "groups", 1)
-        packed = exchanged(packed, "mp", 1)
+        query = exchanged(query, "mp", 1)
+        output_across = exchanged(output_weight, "mp", 1)
         kv_weights = [project_weight, project_beside, near, far]
         kv_weights.append(exchanged(near, "section", 1))
         kv_weights.append(exchanged(far, "section", 1))
-        corner = exchanged(packed, "section", 1)
-        last_weights = [project_weight, project_beside, packed, corner]
-        last_weights += [output_weight, output_beside, packed, corner]
+        last_weights = [project_weight, project_beside, query]
+        last_weights.append(exchanged(query, "section", 1))
+        last_weights += [output_weight, output_beside, output_across]
+        last_weights.append(exchanged(output_across, "section", 1))
     else:
         kv_weights = [lax.all_gather(project_weight, ("mp", "section"), axis=0, tiled=True)]
         last_weights = kv_weights + [lax.all_gather(output_weight, ("mp", "section"), axis=0, tiled=True)]

time: 64.1 us -> 54.8 us (0.85)
  waiting for transfers between devices: 33.1 us -> 23.4 us
    ppermute x14 -> x16, waiting for transfers between devices: 32.5 us -> 23.4 us  [exchanged(): return lax.ppermute(value, axis, [(i, i ^ flip) for i in range(count)])]
    pallas_call x1, Pallas kernels: 0.67 us -> 2.05 us  [central(): pl.pallas_call(functools.partial(central_kernel, wires=wires, channels=ch...]
    pallas_call x1, Pallas kernels: 3.28 us -> 2.38 us  [front(): pl.pallas_call(functools.partial(front_kernel, wires=wires, channels=chan...]
    ppermute x14 -> x16, starting transfers between devices: 13.6 us -> 13.3 us  [exchanged(): return lax.ppermute(value, axis, [(i, i ^ flip) for i in range(count)])]
  transfers between devices with their start and end apart: 15 -> 17, of which waited for: 6 -> 6; matrix products, arithmetic and copies ran while one was open for 0% -> 0% of each run, Pallas kernels for 14% -> 18%
where the time goes in v2:
time: 54.8 us; the launch traced here: 54.7 us
  waiting for transfers between devices  23.4 us (43%)
  starting transfers between devices  17.2 us (31%)
  Pallas kernels  13.9 us (25%)
    ppermute x16, waiting for transfers between devices, exchanged(): return lax.ppermute(value, axis, [(i, i ^ flip) for i in range(count)])  23.4 us
    ppermute x16, starting transfers between devices, exchanged(): return lax.ppermute(value, axis, [(i, i ^ flip) for i in range(count)])  13.3 us
    pallas_call x1, Pallas kernels, finish(): pl.pallas_call(functools.partial(finish_kernel, chunks=len(chunks), swap=...  4.08 us
    ppermute x1, starting transfers between devices, layer(): got = lax.ppermute(msg, 'seq', [(i, i + 1) for i in range(shards - 1)])  3.93 us
    pallas_call x1, Pallas kernels, front(): pl.pallas_call(functools.partial(front_kernel, wires=wires, channels=chan...  2.38 us
    pallas_call x1, Pallas kernels, central(): pl.pallas_call(functools.partial(central_kernel, wires=wires, channels=ch...  2.05 us
    pallas_call x1, Pallas kernels, prepare(): pl.pallas_call(functools.partial(prepare_kernel, pieces=len(weights), chu...  1.53 us
    pallas_call x1, Pallas kernels, extend(): pl.pallas_call(functools.partial(extend_kernel, pieces=pieces, chunks=len...  1.47 us
  transfers between devices with their start and end apart: 17, of which 6 were waited for; matrix products, arithmetic and copies ran while one was open for 0% of the time, Pallas kernels for 18%

profile of v2, /device:TPU:0, one launch (start us, length us, event | category | flops | bytes accessed | tf_op | source)
XLA Modules:
  0.0 54.7 jit_solution(8826751628547740940)
XLA Ops:
  0.0 3.0 %collective-permute-start.7 = (bf16[256,768]{1,0:T(8,128)(2,1)}, bf16[256,768]{1,0:T(8,128)(2,1)S(1)}, u32[]{:S(2)}, u32[]{:S(2)}) collective-permute-start(bf16[256,768]{1,0:T(8,128)(2,1)} %refs_0_.4), channel_id=1, source_target_pairs={{0,2},{2,0},{1,3},{3,1},{4,6},{6,4},{5,7},{7,5},{8,10},{10,8},{9,1... | collective-permute-start | bytes 1179656 | tf_op jit(solution)/shard_map/ppermute | solution.py:535
  3.0 2.4 %front.1 = (bf16[256,512]{1,0:T(8,128)(2,1)S(1)}, bf16[512,1024]{1,0:T(8,128)(2,1)S(1)}, bf16[576,128]{1,0:T(8,128)(2,1)S(1)}, bf16[1152,256]{1,0:T(8,128)(2,1)S...) custom-call(bf16[512,1024]{1,0:T(8,128)(2,1)} %bitcast.6, bf16[576,128]{1,0:T(8,128)(2,1)} %bitcast.8, ...), custom_call_target="tpu_custom_call" | custom-call | tf_op jit(solution)/shard_map/front/pallas_call | solution.py:392
  5.5 0.5 collective-permute-start.6
  6.0 3.9 %collective-permute-start.5 = (bf16[256,512]{1,0:T(8,128)(2,1)S(1)}, bf16[256,512]{1,0:T(8,128)(2,1)S(1)}, u32[]{:S(2)}, u32[]{:S(2)}) collective-permute-start(bf16[256,512]{1,0:T(8,128)(2,1)S(1)} %get-tuple-element.29.msg_ref), channel_id=1, source_target_pairs={{0,4},{4,8},{8,12},{1,5},{5,9},{9,13},{2,6},{6,10},{10,14},{3,7},{... | collective-permute-start | bytes 786440 | tf_op jit(solution)/shard_map/ppermute | solution.py:559
  10.0 3.2 %collective-permute-done.7.refs_2_ = bf16[256,768]{1,0:T(8,128)(2,1)S(1)} collective-permute-done((bf16[256,768]{1,0:T(8,128)(2,1)}, bf16[256,768]{1,0:T(8,128)(2,1)S(1)}, u32[]{:S(2)}, u32[]{:S(2)}) %collective-permute-start.7) | collective-permute-done | bytes 393248 | tf_op jit(solution)/shard_map/ppermute | solution.py:535
  13.1 5.5 %collective-permute-done.1.refs_2_ = bf16[96,1536]{1,0:T(8,128)(2,1)S(1)} collective-permute-done((bf16[96,1536]{1,0:T(8,128)(2,1)S(1)}, bf16[96,1536]{1,0:T(8,128)(2,1)S(1)}, u32[]{:S(2)}, u32[]{:S(2)}) %collective-permute-start.1) | collective-permute-done | bytes 294944 | tf_op jit(solution)/shard_map/ppermute | solution.py:535
  18.6 1.8 %collective-permute-start.2 = (bf16[96,1536]{1,0:T(8,128)(2,1)S(1)}, bf16[96,1536]{1,0:T(8,128)(2,1)S(1)}, u32[]{:S(2)}, u32[]{:S(2)}) collective-permute-start(bf16[96,1536]{1,0:T(8,128)(2,1)S(1)} %collective-permute-done.1.refs_2_), channel_id=1, source_target_pairs={{0,16},{16,0},{1,17},{17,1},{2,18},{18,2},{3,19},{19,3},{4,20},{20... | collective-permute-start | bytes 884744 | tf_op jit(solution)/shard_map/ppermute | solution.py:535
  20.4 1.5 %collective-permute-start.11 = (bf16[192,768]{1,0:T(8,128)(2,1)S(1)}, bf16[192,768]{1,0:T(8,128)(2,1)S(1)}, u32[]{:S(2)}, u32[]{:S(2)}) collective-permute-start(bf16[192,768]{1,0:T(8,128)(2,1)S(1)} %get-tuple-element.43), channel_id=1, source_target_pairs={{0,2},{2,0},{1,3},{3,1},{4,6},{6,4},{5,7},{7,5},{8,10},{10,8},{9,1... | collective-permute-start | bytes 884744 | tf_op jit(solution)/shard_map/ppermute | solution.py:535
  21.9 0.5 collective-permute-start.14
  22.4 4.4 %collective-permute-done.2.refs_3_ = bf16[96,1536]{1,0:T(8,128)(2,1)S(1)} collective-permute-done((bf16[96,1536]{1,0:T(8,128)(2,1)S(1)}, bf16[96,1536]{1,0:T(8,128)(2,1)S(1)}, u32[]{:S(2)}, u32[]{:S(2)}) %collective-permute-start.2) | collective-permute-done | bytes 294944 | tf_op jit(solution)/shard_map/ppermute | solution.py:535
  26.8 0.5 collective-permute-start.4
  27.3 2.0 %central.1 = (f32[128,512]{1,0:T(8,128)S(1)}, f32[256,256]{1,0:T(8,128)S(1)}, bf16[512,128]{1,0:T(8,128)(2,1)S(1)}) custom-call(bf16[256,512]{1,0:T(8,128)(2,1)S(1)} %get-tuple-element.29.msg_ref, bf16[512,1024]{1,0:T(8,128)(2,1)S(1)} %get-tuple-element.30.x_ref, bf16[576,128]{1,0:T(8,128)(2,1)S(1)} %get-tuple-element.31.k1_ref, ...), custom_call_target="tpu_custom_call" | custom-call | tf_op jit(solution)/shard_map/central/pallas_call | solution.py:412
  29.4 1.2 %mix.1 = (f32[128,768]{1,0:T(8,128)S(1)}, bf16[512,768]{1,0:T(8,128)(2,1)S(1)}) custom-call(bf16[512,128]{1,0:T(8,128)(2,1)S(1)} %get-tuple-element.35.patch, bf16[256,768]{1,0:T(8,128)(2,1)S(1)} %copy-done.1, bf16[256,768]{1,0:T(8,128)(2,1)S(1)} %collective-permute-done.6.refs_1_, bf16[256,768]{1,0:T(8,128)(2,1)S(1)} %collective-permute-done.7.refs_2_, ...), custom_call_target="tpu_custom_call" | custom-call | tf_op jit(solution)/shard_map/mix/pallas_call | solution.py:432
  30.6 1.2 %back.1.refs_6_.refs_0_ = bf16[136,768]{1,0:T(8,128)(2,1)S(1)} custom-call(bf16[256,512]{1,0:T(8,128)(2,1)S(1)} %collective-permute-done.5.got_ref, f32[128,512]{1,0:T(8,128)S(1)} %get-tuple-element.33.first_ref, f32[256,256]{1,0:T(8,128)S(1)} %get-tuple-element.34.second_ref, f32[128,768]{1,0:T(8,128)S(1)} %get-tuple-element.36.token_ref, ...), custom_call_target="tpu_custom_call" | custom-call | tf_op jit(solution)/shard_map/back/pallas_call | solution.py:453
  31.8 2.6 %collective-permute-start.10 = (bf16[136,768]{1,0:T(8,128)(2,1)S(1)}, bf16[136,768]{1,0:T(8,128)(2,1)S(1)}, u32[]{:S(2)}, u32[]{:S(2)}) collective-permute-start(bf16[136,768]{1,0:T(8,128)(2,1)S(1)} %back.1.refs_6_.refs_0_), channel_id=1, source_target_pairs={{0,8},{4,12},{8,0},{12,4},{1,9},{5,13},{9,1},{13,5},{2,10},{6,14},... | collective-permute-start | bytes 626696 | tf_op jit(solution)/shard_map/ppermute | solution.py:535
  34.5 0.5 collective-permute-start.12
  35.1 1.6 %collective-permute-start.9 = (bf16[136,768]{1,0:T(8,128)(2,1)S(1)}, bf16[136,768]{1,0:T(8,128)(2,1)S(1)}, u32[]{:S(2)}, u32[]{:S(2)}) collective-permute-start(bf16[136,768]{1,0:T(8,128)(2,1)S(1)} %back.1.refs_6_.refs_0_), channel_id=1, source_target_pairs={{0,4},{4,0},{8,12},{12,8},{1,5},{5,1},{9,13},{13,9},{2,6},{6,2},{1... | collective-permute-start | bytes 626696 | tf_op jit(solution)/shard_map/ppermute | solution.py:535
  36.6 7.8 %collective-permute-done.10.refs_2_ = bf16[136,768]{1,0:T(8,128)(2,1)S(1)} collective-permute-done((bf16[136,768]{1,0:T(8,128)(2,1)S(1)}, bf16[136,768]{1,0:T(8,128)(2,1)S(1)}, u32[]{:S(2)}, u32[]{:S(2)}) %collective-permute-start.10) | collective-permute-done | bytes 208928 | tf_op jit(solution)/shard_map/ppermute | solution.py:535
  44.5 0.6 %collective-permute-start.16 = (bf16[136,768]{1,0:T(8,128)(2,1)S(1)}, bf16[136,768]{1,0:T(8,128)(2,1)S(1)}, u32[]{:S(2)}, u32[]{:S(2)}) collective-permute-start(bf16[136,768]{1,0:T(8,128)(2,1)S(1)} %collective-permute-done.10.refs_2_), channel_id=1, source_target_pairs={{0,4},{4,0},{8,12},{12,8},{1,5},{5,1},{9,13},{13,9},{2,6},{6,2},{1... | collective-permute-start | bytes 626696 | tf_op jit(solution)/shard_map/ppermute | solution.py:535
  45.0 0.9 %collective-permute-done.9.refs_7_.refs_1_ = bf16[136,768]{1,0:T(8,128)(2,1)S(1)} collective-permute-done((bf16[136,768]{1,0:T(8,128)(2,1)S(1)}, bf16[136,768]{1,0:T(8,128)(2,1)S(1)}, u32[]{:S(2)}, u32[]{:S(2)}) %collective-permute-start.9) | collective-permute-done | bytes 208928 | tf_op jit(solution)/shard_map/ppermute | solution.py:535
  46.0 1.5 %prepare.1 = (bf16[768,1536]{1,0:T(8,128)(2,1)S(1)}, bf16[256,768]{1,0:T(8,128)(2,1)S(1)}, bf16[256,768]{1,0:T(8,128)(2,1)S(1)}, bf16[256,768]{1,0:T(8,128)(2,1)S(1)}, bf16[512,512]{1,0:T(8,128)(2,1)S(1)}) custom-call(s32[4,128]{1,0:T(4,128)S(1)} %bitcast.5, bf16[192,2304]{1,0:T(8,128)(2,1)S(1)} %copy-done, ...), custom_call_target="tpu_custom_call" | custom-call | tf_op jit(solution)/shard_map/prepare/pallas_call | solution.py:472
  47.5 1.5 %extend.1 = (bf16[768,768]{1,0:T(8,128)(2,1)S(1)}, bf16[768,768]{1,0:T(8,128)(2,1)S(1)}, bf16[128,768]{1,0:T(8,128)(2,1)S(1)}, bf16[128,768]{1,0:T(8,128)(2,1)S(...) custom-call(bf16[512,512]{1,0:T(8,128)(2,1)S(1)} %get-tuple-element.38.perm_ref, ...), custom_call_target="tpu_custom_call" | custom-call | tf_op jit(solution)/shard_map/extend/pallas_call | solution.py:490
  49.0 1.6 %collective-permute-done.16.refs_0_ = bf16[136,768]{1,0:T(8,128)(2,1)S(1)} collective-permute-done((bf16[136,768]{1,0:T(8,128)(2,1)S(1)}, bf16[136,768]{1,0:T(8,128)(2,1)S(1)}, u32[]{:S(2)}, u32[]{:S(2)}) %collective-permute-start.16) | collective-permute-done | bytes 208928 | tf_op jit(solution)/shard_map/ppermute | solution.py:535
  50.6 4.1 %finish.1 = bf16[128,768]{1,0:T(8,128)(2,1)} custom-call(bf16[512,512]{1,0:T(8,128)(2,1)S(1)} %get-tuple-element.38.perm_ref, bf16[768,1536]{1,0:T(8,128)(2,1)S(1)} %get-tuple-element.39.joined, bf16[256,768]{1,0:T(8,128)(2,1)S(1)} %get-tuple-element.40.keys0, bf16[256,768]{1,0:T(8,128)(2,1)S(1)} %get-tuple-element.41.values0, ...), custom_call_target="tpu_custom_call" | custom-call | tf_op jit(solution)/shard_map/finish/pallas_call | solution.py:516
  (27 shorter events, 0.3 us)
Async XLA Ops:
  0.0 13.1 %collective-permute-start.7 = (bf16[256,768]{1,0:T(8,128)(2,1)}, bf16[256,768]{1,0:T(8,128)(2,1)S(1)}, u32[]{:S(2)}, u32[]{:S(2)}) collective-permute-start(bf16[256,768]{1,0:T(8,128)(2,1)} %refs_0_.4), channel_id=1, source_target_pairs={{0,2},{2,0},{1,3},{3,1},{4,6},{6,4},{5,7},{7,5},{8,10},{10,8},{9,1... | collective-permute-start | bytes 1179656 | tf_op jit(solution)/shard_map/ppermute | solution.py:535
  3.0 2.5 %copy-start = (bf16[192,2304]{1,0:T(8,128)(2,1)S(1)}, bf16[192,2304]{1,0:T(8,128)(2,1)}, u32[]{:S(2)}) copy-start(bf16[192,2304]{1,0:T(8,128)(2,1)} %refs_3_.1) | copy-start | bytes 2654212
  3.0 2.6 %copy-start.1 = (bf16[256,768]{1,0:T(8,128)(2,1)S(1)}, bf16[256,768]{1,0:T(8,128)(2,1)}, u32[]{:S(2)}) copy-start(bf16[256,768]{1,0:T(8,128)(2,1)} %refs_0_.4) | copy-start | bytes 1179652
  3.0 18.9 %copy-start.2 = (bf16[192,768]{1,0:T(8,128)(2,1)S(1)}, bf16[192,768]{1,0:T(8,128)(2,1)}, u32[]{:S(2)}) copy-start(bf16[192,768]{1,0:T(8,128)(2,1)} %refs_7_.1) | copy-start | bytes 884740
  5.4 13.2 %collective-permute-start.1 = (bf16[96,1536]{1,0:T(8,128)(2,1)S(1)}, bf16[96,1536]{1,0:T(8,128)(2,1)S(1)}, u32[]{:S(2)}, u32[]{:S(2)}) collective-permute-start(bf16[96,1536]{1,0:T(8,128)(2,1)S(1)} %get-tuple-element.28), channel_id=1, source_target_pairs={{0,2},{2,0},{1,3},{3,1},{4,6},{6,4},{5,7},{7,5},{8,10},{10,8},{9,1... | collective-permute-start | bytes 884744 | tf_op jit(solution)/shard_map/ppermute | solution.py:535
  5.5 29.5 %collective-permute-start = (bf16[192,2304]{1,0:T(8,128)(2,1)S(1)}, bf16[192,2304]{1,0:T(8,128)(2,1)S(1)}, u32[]{:S(2)}, u32[]{:S(2)}) collective-permute-start(bf16[192,2304]{1,0:T(8,128)(2,1)S(1)} %copy-done), channel_id=1, source_target_pairs={{0,1},{1,0},{2,3},{3,2},{4,5},{5,4},{6,7},{7,6},{8,9},{9,8},{10,11... | collective-permute-start | bytes 2654216 | tf_op jit(solution)/shard_map/ppermute | solution.py:535
  5.5 16.3 %collective-permute-start.6 = (bf16[256,768]{1,0:T(8,128)(2,1)S(1)}, bf16[256,768]{1,0:T(8,128)(2,1)S(1)}, u32[]{:S(2)}, u32[]{:S(2)}) collective-permute-start(bf16[256,768]{1,0:T(8,128)(2,1)S(1)} %copy-done.1), channel_id=1, source_target_pairs={{0,1},{1,0},{2,3},{3,2},{4,5},{5,4},{6,7},{7,6},{8,9},{9,8},{10,11... | collective-permute-start | bytes 1179656 | tf_op jit(solution)/shard_map/ppermute | solution.py:535
  6.0 14.4 %collective-permute-start.5 = (bf16[256,512]{1,0:T(8,128)(2,1)S(1)}, bf16[256,512]{1,0:T(8,128)(2,1)S(1)}, u32[]{:S(2)}, u32[]{:S(2)}) collective-permute-start(bf16[256,512]{1,0:T(8,128)(2,1)S(1)} %get-tuple-element.29.msg_ref), channel_id=1, source_target_pairs={{0,4},{4,8},{8,12},{1,5},{5,9},{9,13},{2,6},{6,10},{10,14},{3,7},{... | collective-permute-start | bytes 786440 | tf_op jit(solution)/shard_map/ppermute | solution.py:559
  13.1 13.6 %collective-permute-start.8 = (bf16[256,768]{1,0:T(8,128)(2,1)S(1)}, bf16[256,768]{1,0:T(8,128)(2,1)S(1)}, u32[]{:S(2)}, u32[]{:S(2)}) collective-permute-start(bf16[256,768]{1,0:T(8,128)(2,1)S(1)} %collective-permute-done.7.refs_2_), channel_id=1, source_target_pairs={{0,1},{1,0},{2,3},{3,2},{4,5},{5,4},{6,7},{7,6},{8,9},{9,8},{10,11... | collective-permute-start | bytes 1179656 | tf_op jit(solution)/shard_map/ppermute | solution.py:535
  18.6 8.2 %collective-permute-start.2 = (bf16[96,1536]{1,0:T(8,128)(2,1)S(1)}, bf16[96,1536]{1,0:T(8,128)(2,1)S(1)}, u32[]{:S(2)}, u32[]{:S(2)}) collective-permute-start(bf16[96,1536]{1,0:T(8,128)(2,1)S(1)} %collective-permute-done.1.refs_2_), channel_id=1, source_target_pairs={{0,16},{16,0},{1,17},{17,1},{2,18},{18,2},{3,19},{19,3},{4,20},{20... | collective-permute-start | bytes 884744 | tf_op jit(solution)/shard_map/ppermute | solution.py:535
  20.4 11.4 %collective-permute-start.11 = (bf16[192,768]{1,0:T(8,128)(2,1)S(1)}, bf16[192,768]{1,0:T(8,128)(2,1)S(1)}, u32[]{:S(2)}, u32[]{:S(2)}) collective-permute-start(bf16[192,768]{1,0:T(8,128)(2,1)S(1)} %get-tuple-element.43), channel_id=1, source_target_pairs={{0,2},{2,0},{1,3},{3,1},{4,6},{6,4},{5,7},{7,5},{8,10},{10,8},{9,1... | collective-permute-start | bytes 884744 | tf_op jit(solution)/shard_map/ppermute | solution.py:535
  21.9 12.6 %collective-permute-start.14 = (bf16[192,768]{1,0:T(8,128)(2,1)S(1)}, bf16[192,768]{1,0:T(8,128)(2,1)S(1)}, u32[]{:S(2)}, u32[]{:S(2)}) collective-permute-start(bf16[192,768]{1,0:T(8,128)(2,1)S(1)} %copy-done.2), channel_id=1, source_target_pairs={{0,2},{2,0},{1,3},{3,1},{4,6},{6,4},{5,7},{7,5},{8,10},{10,8},{9,1... | collective-permute-start | bytes 884744 | tf_op jit(solution)/shard_map/ppermute | solution.py:535
  26.8 7.7 %collective-permute-start.3 = (bf16[96,1536]{1,0:T(8,128)(2,1)S(1)}, bf16[96,1536]{1,0:T(8,128)(2,1)S(1)}, u32[]{:S(2)}, u32[]{:S(2)}) collective-permute-start(bf16[96,1536]{1,0:T(8,128)(2,1)S(1)} %collective-permute-done.1.refs_2_), channel_id=1, source_target_pairs={{0,1},{1,0},{2,3},{3,2},{4,5},{5,4},{6,7},{7,6},{8,9},{9,8},{10,11... | collective-permute-start | bytes 884744 | tf_op jit(solution)/shard_map/ppermute | solution.py:535
  26.8 8.3 %collective-permute-start.4 = (bf16[96,1536]{1,0:T(8,128)(2,1)S(1)}, bf16[96,1536]{1,0:T(8,128)(2,1)S(1)}, u32[]{:S(2)}, u32[]{:S(2)}) collective-permute-start(bf16[96,1536]{1,0:T(8,128)(2,1)S(1)} %collective-permute-done.2.refs_3_), channel_id=1, source_target_pairs={{0,1},{1,0},{2,3},{3,2},{4,5},{5,4},{6,7},{7,6},{8,9},{9,8},{10,11... | collective-permute-start | bytes 884744 | tf_op jit(solution)/shard_map/ppermute | solution.py:535
  29.4 1.3 %copy-start.4 = (s32[1,128]{1,0:T(1,128)S(1)}, s32[1,128]{1,0:T(1,128)}, u32[]{:S(2)}) copy-start(s32[1,128]{1,0:T(1,128)} %active_ref.1) | copy-start | bytes 1540
  30.6 15.3 %copy-start.3 = (s32[1,512]{1,0:T(1,128)S(1)}, s32[1,512]{1,0:T(1,128)}, u32[]{:S(2)}) copy-start(s32[1,512]{1,0:T(1,128)} %param.14) | copy-start | bytes 6148
  31.8 12.6 %collective-permute-start.10 = (bf16[136,768]{1,0:T(8,128)(2,1)S(1)}, bf16[136,768]{1,0:T(8,128)(2,1)S(1)}, u32[]{:S(2)}, u32[]{:S(2)}) collective-permute-start(bf16[136,768]{1,0:T(8,128)(2,1)S(1)} %back.1.refs_6_.refs_0_), channel_id=1, source_target_pairs={{0,8},{4,12},{8,0},{12,4},{1,9},{5,13},{9,1},{13,5},{2,10},{6,14},... | collective-permute-start | bytes 626696 | tf_op jit(solution)/shard_map/ppermute | solution.py:535
  34.5 13.0 %collective-permute-start.13 = (bf16[192,768]{1,0:T(8,128)(2,1)S(1)}, bf16[192,768]{1,0:T(8,128)(2,1)S(1)}, u32[]{:S(2)}, u32[]{:S(2)}) collective-permute-start(bf16[192,768]{1,0:T(8,128)(2,1)S(1)} %copy-done.2), channel_id=1, source_target_pairs={{0,1},{1,0},{2,3},{3,2},{4,5},{5,4},{6,7},{7,6},{8,9},{9,8},{10,11... | collective-permute-start | bytes 884744 | tf_op jit(solution)/shard_map/ppermute | solution.py:535
  34.5 13.0 %collective-permute-start.12 = (bf16[192,768]{1,0:T(8,128)(2,1)S(1)}, bf16[192,768]{1,0:T(8,128)(2,1)S(1)}, u32[]{:S(2)}, u32[]{:S(2)}) collective-permute-start(bf16[192,768]{1,0:T(8,128)(2,1)S(1)} %collective-permute-done.11.refs_5_), channel_id=1, source_target_pairs={{0,1},{1,0},{2,3},{3,2},{4,5},{5,4},{6,7},{7,6},{8,9},{9,8},{10,11... | collective-permute-start | bytes 884744 | tf_op jit(solution)/shard_map/ppermute | solution.py:535
  35.0 12.5 %collective-permute-start.15 = (bf16[192,768]{1,0:T(8,128)(2,1)S(1)}, bf16[192,768]{1,0:T(8,128)(2,1)S(1)}, u32[]{:S(2)}, u32[]{:S(2)}) collective-permute-start(bf16[192,768]{1,0:T(8,128)(2,1)S(1)} %collective-permute-done.14.refs_9_), channel_id=1, source_target_pairs={{0,1},{1,0},{2,3},{3,2},{4,5},{5,4},{6,7},{7,6},{8,9},{9,8},{10,11... | collective-permute-start | bytes 884744 | tf_op jit(solution)/shard_map/ppermute | solution.py:535
  35.1 10.9 %collective-permute-start.9 = (bf16[136,768]{1,0:T(8,128)(2,1)S(1)}, bf16[136,768]{1,0:T(8,128)(2,1)S(1)}, u32[]{:S(2)}, u32[]{:S(2)}) collective-permute-start(bf16[136,768]{1,0:T(8,128)(2,1)S(1)} %back.1.refs_6_.refs_0_), channel_id=1, source_target_pairs={{0,4},{4,0},{8,12},{12,8},{1,5},{5,1},{9,13},{13,9},{2,6},{6,2},{1... | collective-permute-start | bytes 626696 | tf_op jit(solution)/shard_map/ppermute | solution.py:535
  44.5 6.2 %collective-permute-start.16 = (bf16[136,768]{1,0:T(8,128)(2,1)S(1)}, bf16[136,768]{1,0:T(8,128)(2,1)S(1)}, u32[]{:S(2)}, u32[]{:S(2)}) collective-permute-start(bf16[136,768]{1,0:T(8,128)(2,1)S(1)} %collective-permute-done.10.refs_2_), channel_id=1, source_target_pairs={{0,4},{4,0},{8,12},{12,8},{1,5},{5,1},{9,13},{13,9},{2,6},{6,2},{1... | collective-permute-start | bytes 626696 | tf_op jit(solution)/shard_map/ppermute | solution.py:535

commit v3 on v2

--- a/solution.py
+++ b/solution.py
@@ -68,10 +68,10 @@
     return (lax.axis_index("mp") * 2 + lax.axis_index("section")) ^ flip
 
 
-def wire_rows(x_ref, block, first, wires, part):
-    height = (wires - first[0]) * part if first[1] is None else (first[1] - first[0]) * part
-    row, col = iota((height, 256), 0), iota((height, 256), 1)
-    mixer = one_hot(col == (row % part) * wires + row // part + first[0])
+def wire_rows(x_ref, block, first, last, wires, part):
+    shape = ((last - first) * part, 256)
+    row, col = iota(shape, 0), iota(shape, 1)
+    mixer = one_hot(col == (row % part) * wires + row // part + first)
     return dot(mixer, x_ref[block * 256 : (block + 1) * 256, :]).astype(BF)
 
 
@@ -118,7 +118,7 @@
     splitter = split_matrix()
     for block in range(blocks):
         loads[block].wait()
-        rows = wire_rows(x_ref, block, (wires - 3, None), wires, part)
+        rows = wire_rows(x_ref, block, wires - 3, wires, wires, part)
         fill_taps(taps, rows, block, splitter, part, channels)
     msg_ref[: 2 * channels, :] = taps[7 * channels :, :]
     loads[blocks].wait()
@@ -133,7 +133,7 @@
     splitter = split_matrix()
     part = 256 // wires
     for block in range(channels // part):
-        rows = wire_rows(x_ref, block, (0, wires - 2), wires, part)
+        rows = wire_rows(x_ref, block, 0, wires - 2, wires, part)
         fill_taps(taps1, rows, block, splitter, part, channels)
     first_ref[...] = dot(k1_ref[3 * channels :, :], taps1[: 6 * channels, :], 0, 0)
     for level in range(1, wires // 2):
@@ -149,25 +149,35 @@
     store_patch(patch, out, splitter)
 
 
+def embed_mixer():
+    row, col = iota((256, 256), 0), iota((256, 256), 1)
+    return one_hot(col == (row % 64) * 4 + row // 64)
+
+
 def mix_kernel(patch, *refs, pieces):
     embed_refs = refs[:pieces]
-    token_ref, low_ref, high, own, sem = refs[pieces:]
-    copy = pltpu.make_async_copy(embed_refs[0], own, sem)
-    copy.start()
-    row, col = iota((256, 256), 0), iota((256, 256), 1)
-    mixer = one_hot(col == (row % 64) * 4 + row // 64)
-    for piece in list(range(1, pieces)) + [0]:
+    token_ref, low_ref, high = refs[pieces:]
+    mixer = embed_mixer()
+    for piece in reversed(range(pieces)):
         ref = embed_refs[piece]
-        if piece == 0:
-            copy.wait()
-            ref = own
         parts = ref.shape[0] // 256
         for part in range(parts):
             rows = dot(mixer, ref[part * 256 : (part + 1) * 256, :]).astype(BF)
             base = pl.multiple_of((block_of(pieces > 1, piece) * parts + part) * 128, 128)
             low_ref[pl.ds(base, 128), :] = rows[:128]
             high[pl.ds(base, 128), :] = rows[128:]
+    if pieces > 1:
+        base = pl.multiple_of(block_of(True, pieces) * 128, 128)
+        low_ref[pl.ds(base, 128), :] = jnp.zeros((128, low_ref.shape[1]), BF)
+        high[pl.ds(base, 128), :] = jnp.zeros((128, high.shape[1]), BF)
     token_ref[...] = dot(patch[...], high[...], 0, 0)
+
+
+def blend_kernel(patch, token_ref, embed_ref, out_ref, low_ref):
+    rows = dot(embed_mixer(), embed_ref[...]).astype(BF)
+    low_ref[...] = rows[:128]
+    base = pl.multiple_of(block_of(True, 3) * 128, 128)
+    out_ref[...] = token_ref[...] + dot(patch[pl.ds(base, 128), :], rows[128:], 0, 0)
 
 
 def store_patch(patch, out, splitter):
@@ -180,9 +190,9 @@
 
 
 def back_kernel(
-    got_ref, first_ref, second_ref, token_ref, low_ref, k1_ref, k2_ref, active_ref,
-    out_ref, all1, all2, patch, *, channels, middle
+    got_ref, k1_ref, k2_ref, active_ref, first_ref, second_ref, token_ref, low_ref, *refs, channels, middle
 ):
+    out_ref, upper_ref, lower_ref, all1, all2, patch = refs[-6:]
     splitter = split_matrix()
     odd = got_ref[channels : 2 * channels, :].astype(F32)
     all1[:channels, :] = later(odd).astype(BF)
@@ -195,11 +205,19 @@
     out = silu(second_ref[...] + dot(k2_ref[: 6 * middle, :], all2[...], 0, 0)).astype(BF)
     store_patch(patch, out, splitter)
     total = token_ref[...] + dot(patch[...], low_ref[...], 0, 0)
+    if len(refs) > 6:
+        base = pl.multiple_of(block_of(True, 3) * 128, 128)
+        total += dot(patch[pl.ds(base, 128), :], refs[0][...], 0, 0)
     count, width = total.shape
-    out_ref[:count, :] = total.astype(BF)
+    total = total.astype(BF)
+    half = count // 2
+    out_ref[:count, :] = total
+    upper_ref[...] = total[:half]
+    lower_ref[:half, :] = total[half:]
     tail = jnp.broadcast_to(active_ref[...].astype(F32), (EXTRA, count))
     tail = jnp.concatenate([tail, jnp.zeros((EXTRA, width - count), F32)], axis=1)
     out_ref[count:, :] = tail.astype(BF)
+    lower_ref[half:, :] = tail.astype(BF)
 
 
 def normal(tokens):
@@ -207,6 +225,24 @@
     value = value - jnp.mean(value, axis=-1, keepdims=True)
     spread = jnp.mean(value * value, axis=-1, keepdims=True)
     return (value * lax.rsqrt(spread + epsilon)).astype(BF)
+
+
+def unpack(refs, layout):
+    chunks, start = [], 0
+    for parts in layout:
+        chunks.append(refs[start : start + parts])
+        start += parts
+    return chunks
+
+
+def rows_of(chunk):
+    parts = [ref[...] for ref in chunk[:-1]]
+    parts.append(chunk[-1][: chunk[-1].shape[0] - EXTRA, :])
+    return parts[0] if len(parts) == 1 else jnp.concatenate(parts, axis=0)
+
+
+def flags_of(chunk, count):
+    return chunk[-1][chunk[-1].shape[0] - EXTRA :, :count]
 
 
 def lift(joined, normed, keys, values):
@@ -268,70 +304,74 @@
         down = jnp.sum(jnp.where(square, across, 0.0), axis=1, keepdims=True)
         perm_ref[slot * count : (slot + 1) * count, :] = one_hot(labels == down)
     for slot, ref in enumerate(chunk_refs):
-        normed[slot * count : (slot + 1) * count, :] = normal(ref[:count, :])
+        normed[slot * count : (slot + 1) * count, :] = normal(rows_of([ref]))
     for copy in copies:
         copy.wait()
     lift(joined, normed, keys, values)
 
 
-def extend_kernel(perm_ref, joined, normed0, *refs, pieces, chunks, early, swap):
-    chunk_refs = refs[:chunks]
-    weight_refs = refs[chunks : chunks + 2 * pieces]
-    refs = refs[chunks + 2 * pieces :]
-    query, output, keys1, values1, token_ref, picked_ref, on_ref, normed1, sems = refs
+def extend_kernel(perm_ref, joined, normed0, *refs, pieces, layout, early, swap):
+    total = sum(layout)
+    chunks = unpack(refs[:total], layout)
+    query_refs = refs[total : total + pieces]
+    query, keys1, values1, token_ref, picked_ref, on_ref, normed1, sems = refs[total + pieces :]
     count = token_ref.shape[0]
-    copies = []
-    for kind, target in enumerate((query, output)):
-        sources = []
-        for piece in range(pieces):
-            ref = weight_refs[kind * pieces + piece]
-            depth = ref.shape[0]
-            sources.append((ref, block_of(pieces > 1, piece) * depth, 0, depth))
-        copies += collect(sources, target, sems.at[kind])
-    for slot, ref in enumerate(chunk_refs[early:]):
-        normed1[slot * count : (slot + 1) * count, :] = normal(ref[:count, :])
+    copies = collect(weight_rows(query_refs), query, sems)
+    for slot, chunk in enumerate(chunks[early:]):
+        normed1[slot * count : (slot + 1) * count, :] = normal(rows_of(chunk))
     lift(joined, normed1, keys1, values1)
     own = own_rows(perm_ref, count, swap)
-    near = early * count
-    picked_ref[...] = dot(own[:, :near], normed0[...]) + dot(own[:, near : chunks * count], normed1[...])
-    on, token = flags_and_tokens(perm_ref, own, chunk_refs, 0)
+    near, far = early * count, len(layout) * count
+    picked_ref[...] = dot(own[:, :near], normed0[...]) + dot(own[:, near:far], normed1[...])
+    on, token = flags_and_tokens(perm_ref, own, chunks, 0)
     on_ref[...] = on
     token_ref[...] = token
     for copy in copies:
         copy.wait()
 
 
+def weight_rows(refs):
+    sources = []
+    for piece, ref in enumerate(refs):
+        depth = ref.shape[0]
+        sources.append((ref, block_of(len(refs) > 1, piece) * depth, 0, depth))
+    return sources
+
+
 def own_rows(perm_ref, count, swap):
     slot = 0 if swap else lax.axis_index("seq")
     return perm_ref[pl.ds(pl.multiple_of(slot * count, count), count), :]
 
 
-def flags_and_tokens(perm_ref, own, chunk_refs, first):
+def flags_and_tokens(perm_ref, own, chunks, first):
     count = own.shape[0]
     on = token = 0.0
-    for slot, ref in enumerate(chunk_refs):
+    for slot, chunk in enumerate(chunks):
         here = slice((first + slot) * count, (first + slot + 1) * count)
-        on += dot(ref[count:, :count], perm_ref[here, :])
-        token += dot(own[:, here], ref[:count, :])
+        on += dot(flags_of(chunk, count), perm_ref[here, :])
+        token += dot(own[:, here], rows_of(chunk))
     return on, token
 
 
 def finish_kernel(
-    perm_ref, joined, keys0, values0, keys1, values1, query, output, token_ref, picked_ref, on_ref, *refs,
-    chunks, swap
+    perm_ref, joined, keys0, values0, keys1, values1, query, token_ref, picked_ref, on_ref, *refs,
+    pieces, layout, swap
 ):
-    chunk_refs = refs[:chunks]
-    out_ref, normed2, keys2, values2, cap, mixed = refs[chunks:]
+    total = sum(layout)
+    chunks = unpack(refs[:total], layout)
+    output_refs = refs[total : total + pieces]
+    out_ref, output, normed2, keys2, values2, cap, mixed, sems = refs[total + pieces :]
+    copies = collect(weight_rows(output_refs), output, sems)
     count, width = token_ref.shape
-    first = perm_ref.shape[0] // count - chunks
-    for slot, ref in enumerate(chunk_refs):
-        normed2[slot * count : (slot + 1) * count, :] = normal(ref[:count, :])
+    first = perm_ref.shape[0] // count - len(layout)
+    for slot, chunk in enumerate(chunks):
+        normed2[slot * count : (slot + 1) * count, :] = normal(rows_of(chunk))
     lift(joined, normed2, keys2, values2)
     own = own_rows(perm_ref, count, swap)
     picked = (picked_ref[...] + dot(own[:, first * count :], normed2[...])).astype(BF)
     head = width // HEADS
     queries = (dot(picked, query[...]) * head ** (-0.5)).astype(BF)
-    on, token = flags_and_tokens(perm_ref, own, chunk_refs, first)
+    on, token = flags_and_tokens(perm_ref, own, chunks, first)
     on += on_ref[...]
     token += token_ref[...]
     allowed = (own.astype(F32) + jnp.broadcast_to(on[:1], own.shape)) > 0.5
@@ -357,6 +397,8 @@
             part += dot(weights[:, start : start + keys.shape[0]], values[:, here])
             start += keys.shape[0]
         mixed[:, here] = jnp.where(low, part[:count] * scale[0], part[count:] * scale[1]).astype(BF)
+    for copy in copies:
+        copy.wait()
     out_ref[...] = (token + dot(mixed[...], output[...])).astype(BF)
 
 
@@ -432,29 +474,37 @@
     return pl.pallas_call(
         functools.partial(mix_kernel, pieces=len(embeds)),
         out_shape=(array((patch.shape[1], width), F32), array((patch.shape[0], width))),
-        in_specs=[vmem()] + [fixed()] + [vmem()] * (len(embeds) - 1),
+        in_specs=[vmem()] * (1 + len(embeds)),
         out_specs=[vmem()] * 2,
-        scratch_shapes=[
-            pltpu.VMEM((patch.shape[0], width), BF),
-            pltpu.VMEM(embeds[0].shape, BF),
-            pltpu.SemaphoreType.DMA,
-        ],
+        scratch_shapes=[pltpu.VMEM((patch.shape[0], width), BF)],
         compiler_params=params(8),
         name="mix",
     )(patch, *embeds)
 
 
-def back(got, parts, k1, k2, active):
+def blend(patch, token, embed):
+    return pl.pallas_call(
+        blend_kernel,
+        out_shape=(array(token.shape, F32), array((embed.shape[0] // 2, embed.shape[1]))),
+        in_specs=[vmem()] * 3,
+        out_specs=[vmem()] * 2,
+        compiler_params=params(6),
+        name="blend",
+    )(patch, token, embed)
+
+
+def back(got, k1, k2, active, *parts):
     middle = k1.shape[1]
     channels = k1.shape[0] // 9
     length = got.shape[1]
     count = active.shape[1]
-    width = parts[-1].shape[1]
+    half = count // 2
+    width = parts[2].shape[1]
     return pl.pallas_call(
         functools.partial(back_kernel, channels=channels, middle=middle),
-        out_shape=array((count + EXTRA, width)),
+        out_shape=(array((count + EXTRA, width)), array((half, width)), array((half + EXTRA, width))),
         in_specs=[vmem()] * (4 + len(parts)),
-        out_specs=vmem(),
+        out_specs=[vmem()] * 3,
         scratch_shapes=[
             pltpu.VMEM((3 * channels, length), BF),
             pltpu.VMEM((6 * middle, length // 2), BF),
@@ -462,7 +512,7 @@
         ],
         compiler_params=params(8),
         name="back",
-    )(got, *parts, k1, k2, active)
+    )(got, k1, k2, active, *parts)
 
 
 def prepare(order, weights, chunks, swap):
@@ -484,13 +534,14 @@
     joined, normed, _, _, perm = ready
     width = joined.shape[0]
     size = perm.shape[0]
-    count = chunks[0].shape[0] - EXTRA
+    count = chunks[0][0].shape[0] - EXTRA
     far = (len(chunks) - early) * count
-    pieces = len(weights) // 2
-    return pl.pallas_call(
-        functools.partial(extend_kernel, pieces=pieces, chunks=len(chunks), early=early, swap=swap),
+    pieces = len(weights)
+    layout = tuple(len(chunk) for chunk in chunks)
+    flat = [part for chunk in chunks for part in chunk]
+    return pl.pallas_call(
+        functools.partial(extend_kernel, pieces=pieces, layout=layout, early=early, swap=swap),
         out_shape=(
-            array((width, width)),
             array((width, width)),
             array((far, width)),
             array((far, width)),
@@ -498,36 +549,41 @@
             array((count, width), F32),
             array((EXTRA, size), F32),
         ),
-        in_specs=[vmem()] * (3 + len(chunks)) + ([fixed()] + [hbm()] * (pieces - 1)) * 2,
-        out_specs=[vmem()] * 7,
-        scratch_shapes=[pltpu.VMEM((far, width), BF), pltpu.SemaphoreType.DMA((2, pieces))],
+        in_specs=[vmem()] * (3 + len(flat)) + [fixed()] + [hbm()] * (pieces - 1),
+        out_specs=[vmem()] * 6,
+        scratch_shapes=[pltpu.VMEM((far, width), BF), pltpu.SemaphoreType.DMA((pieces,))],
         compiler_params=params(8 + size // 128),
         name="extend",
-    )(perm, joined, normed, *chunks, *weights)
-
-
-def finish(ready, extra, chunks, swap):
+    )(perm, joined, normed, *flat, *weights)
+
+
+def finish(ready, extra, chunks, weights, swap):
     joined, _, keys, values, perm = ready
-    query, output, keys1, values1, token, picked, on = extra
+    query, keys1, values1, token, picked, on = extra
     width = joined.shape[0]
     size = perm.shape[0]
     count = token.shape[0]
     far = len(chunks) * count
-    return pl.pallas_call(
-        functools.partial(finish_kernel, chunks=len(chunks), swap=swap),
+    pieces = len(weights)
+    layout = tuple(len(chunk) for chunk in chunks)
+    flat = [part for chunk in chunks for part in chunk]
+    return pl.pallas_call(
+        functools.partial(finish_kernel, pieces=pieces, layout=layout, swap=swap),
         out_shape=array((count, width)),
-        in_specs=[vmem()] * (11 + len(chunks)),
+        in_specs=[vmem()] * (10 + len(flat)) + [fixed()] + [hbm()] * (pieces - 1),
         out_specs=vmem(),
         scratch_shapes=[
+            pltpu.VMEM((width, width), BF),
             pltpu.VMEM((far, width), BF),
             pltpu.VMEM((far, width), BF),
             pltpu.VMEM((far, width), BF),
             pltpu.VMEM((count, size), F32),
             pltpu.VMEM((count, width), BF),
+            pltpu.SemaphoreType.DMA((pieces,)),
         ],
         compiler_params=params(8 + size // 64),
         name="finish",
-    )(perm, joined, keys, values, keys1, values1, query, output, token, picked, on, *chunks)
+    )(perm, joined, keys, values, keys1, values1, query, token, picked, on, *flat, *weights)
 
 
 def exchanged(value, axis, flip):
@@ -550,8 +606,8 @@
     if paired:
         embed_across = exchanged(embed_weight, "mp", 1)
         embed_beside = exchanged(embed_weight, "section", 1)
+        embed_corner = exchanged(embed_across, "section", 1)
         embeds = [embed_weight, embed_beside, embed_across]
-        embeds.append(exchanged(embed_across, "section", 1))
         msg, rows, k1, k2, near, query = front(rows, k1, k2, wires, (project_weight,))
     else:
         embeds = [lax.all_gather(embed_weight, ("mp", "section"), axis=0, tiled=True)]
@@ -559,13 +615,19 @@
     got = lax.ppermute(msg, "seq", [(i, i + 1) for i in range(shards - 1)])
     first, second, patch = central(msg, rows, k1, k2, wires, count)
     token, low = mix(patch, embeds)
-    tokens = back(got, (first, second, token, low), k1, k2, active)
+    parts = [first, second, token, low]
+    if paired:
+        parts[2], corner_low = blend(patch, token, embed_corner)
+        parts.append(corner_low)
+    tokens, upper, lower = back(got, k1, k2, active, *parts)
     if swap:
-        chunks = [tokens] + [exchanged(tokens, "seq", flip) for flip in (1, 2)]
-        chunks.append(exchanged(chunks[2], "seq", 1))
+        chunks = [[tokens], [exchanged(tokens, "seq", 1)]]
+        chunks.append([exchanged(upper, "seq", 2), exchanged(lower, "seq", 2)])
+        chunks.append([exchanged(chunks[2][0], "seq", 1), exchanged(chunks[2][1], "seq", 1)])
     else:
         everyone = lax.all_gather(tokens, "seq", axis=0, tiled=True)
-        chunks = [everyone[i * (count + EXTRA) : (i + 1) * (count + EXTRA)] for i in range(shards)]
+        each = count + EXTRA
+        chunks = [[everyone[i * each : (i + 1) * each]] for i in range(shards)]
     if paired:
         project_beside = exchanged(project_weight, "section", 1)
         output_beside = exchanged(output_weight, "section", 1)
@@ -576,17 +638,18 @@
         kv_weights = [project_weight, project_beside, near, far]
         kv_weights.append(exchanged(near, "section", 1))
         kv_weights.append(exchanged(far, "section", 1))
-        last_weights = [project_weight, project_beside, query]
-        last_weights.append(exchanged(query, "section", 1))
-        last_weights += [output_weight, output_beside, output_across]
-        last_weights.append(exchanged(output_across, "section", 1))
+        query_weights = [project_weight, project_beside, query]
+        query_weights.append(exchanged(query, "section", 1))
+        output_weights = [output_weight, output_beside, output_across]
+        output_weights.append(exchanged(output_across, "section", 1))
     else:
         kv_weights = [lax.all_gather(project_weight, ("mp", "section"), axis=0, tiled=True)]
-        last_weights = kv_weights + [lax.all_gather(output_weight, ("mp", "section"), axis=0, tiled=True)]
+        query_weights = kv_weights
+        output_weights = [lax.all_gather(output_weight, ("mp", "section"), axis=0, tiled=True)]
     early, later = shards // 2, shards // 2 + shards // 4
-    ready = prepare(order, kv_weights, chunks[:early], swap)
-    extra = extend(ready, chunks[:later], last_weights, early, swap)
-    result = finish(ready, extra, chunks[later:], swap)
+    ready = prepare(order, kv_weights, [chunk[0] for chunk in chunks[:early]], swap)
+    extra = extend(ready, chunks[:later], query_weights, early, swap)
+    result = finish(ready, extra, chunks[later:], output_weights, swap)
     return result[None]
 
 

time: 54.8 us -> 64.5 us (1.18)
  starting transfers between devices: 17.2 us -> 23.1 us
  waiting for transfers between devices: 23.4 us -> 27 us
    ppermute x16 -> x18, starting transfers between devices: 13.3 us -> 19.6 us  [exchanged(): return lax.ppermute(value, axis, [(i, i ^ flip) for i in range(count)])]
    ppermute x1, waiting for transfers between devices: 0.01 us -> 4.4 us  [layer(): got = lax.ppermute(msg, 'seq', [(i, i + 1) for i in range(shards - 1)])]
    ppermute x16 -> x18, waiting for transfers between devices: 23.4 us -> 22.6 us  [exchanged(): return lax.ppermute(value, axis, [(i, i ^ flip) for i in range(count)])]
    pallas_call x2 -> x3, Pallas kernels: 5.54 us -> 6.09 us  [the longest x1 4.46 us: finish(): pl.pallas_call(functools.partial(finish_kernel, pieces=pieces, layout=lay...]
  transfers between devices with their start and end apart: 17 -> 19, of which waited for: 6 -> 6; matrix products, arithmetic and copies ran while one was open for 0% -> 0% of each run, Pallas kernels for 18% -> 15%
where the time goes in v3:
time: 64.5 us; the launch traced here: 64.3 us
  waiting for transfers between devices  27 us (42%)
  starting transfers between devices  23.1 us (36%)
  Pallas kernels  14.1 us (22%)
    ppermute x18, waiting for transfers between devices, exchanged(): return lax.ppermute(value, axis, [(i, i ^ flip) for i in range(count)])  22.6 us
    ppermute x18, starting transfers between devices, exchanged(): return lax.ppermute(value, axis, [(i, i ^ flip) for i in range(count)])  19.6 us
    pallas_call x1, Pallas kernels, finish(): pl.pallas_call(functools.partial(finish_kernel, pieces=pieces, layout=lay...  4.46 us
    ppermute x1, waiting for transfers between devices, layer(): got = lax.ppermute(msg, 'seq', [(i, i + 1) for i in range(shards - 1)])  4.4 us
    ppermute x1, starting transfers between devices, layer(): got = lax.ppermute(msg, 'seq', [(i, i + 1) for i in range(shards - 1)])  3.48 us
    pallas_call x1, Pallas kernels, front(): pl.pallas_call(functools.partial(front_kernel, wires=wires, channels=chan...  2.27 us
    pallas_call x1, Pallas kernels, central(): pl.pallas_call(functools.partial(central_kernel, wires=wires, channels=ch...  2.04 us
    pallas_call x1, Pallas kernels, prepare(): pl.pallas_call(functools.partial(prepare_kernel, pieces=len(weights), chu...  1.53 us
  transfers between devices with their start and end apart: 19, of which 6 were waited for; matrix products, arithmetic and copies ran while one was open for 0% of the time, Pallas kernels for 15%

profile of v3, /device:TPU:0, one launch (start us, length us, event | category | flops | bytes accessed | tf_op | source)
XLA Modules:
  0.0 64.3 jit_solution(6933739809004578307)
XLA Ops:
  0.0 3.0 %collective-permute-start.7 = (bf16[256,768]{1,0:T(8,128)(2,1)}, bf16[256,768]{1,0:T(8,128)(2,1)S(1)}, u32[]{:S(2)}, u32[]{:S(2)}) collective-permute-start(bf16[256,768]{1,0:T(8,128)(2,1)} %refs_0_.4), channel_id=1, source_target_pairs={{0,2},{2,0},{1,3},{3,1},{4,6},{6,4},{5,7},{7,5},{8,10},{10,8},{9,1... | collective-permute-start | bytes 1179656 | tf_op jit(solution)/shard_map/ppermute | solution.py:591
  3.0 2.3 %front.1 = (bf16[256,512]{1,0:T(8,128)(2,1)S(1)}, bf16[512,1024]{1,0:T(8,128)(2,1)S(1)}, bf16[576,128]{1,0:T(8,128)(2,1)S(1)}, bf16[1152,256]{1,0:T(8,128)(2,1)S...) custom-call(bf16[512,1024]{1,0:T(8,128)(2,1)} %bitcast.6, bf16[576,128]{1,0:T(8,128)(2,1)} %bitcast.8, ...), custom_call_target="tpu_custom_call" | custom-call | tf_op jit(solution)/shard_map/front/pallas_call | solution.py:434
  6.0 7.2 %collective-permute-done.7.refs_2_ = bf16[256,768]{1,0:T(8,128)(2,1)S(1)} collective-permute-done((bf16[256,768]{1,0:T(8,128)(2,1)}, bf16[256,768]{1,0:T(8,128)(2,1)S(1)}, u32[]{:S(2)}, u32[]{:S(2)}) %collective-permute-start.7) | collective-permute-done | bytes 393248 | tf_op jit(solution)/shard_map/ppermute | solution.py:591
  13.2 5.5 %collective-permute-done.1.refs_2_ = bf16[96,1536]{1,0:T(8,128)(2,1)S(1)} collective-permute-done((bf16[96,1536]{1,0:T(8,128)(2,1)S(1)}, bf16[96,1536]{1,0:T(8,128)(2,1)S(1)}, u32[]{:S(2)}, u32[]{:S(2)}) %collective-permute-start.1) | collective-permute-done | bytes 294944 | tf_op jit(solution)/shard_map/ppermute | solution.py:591
  18.7 1.8 %collective-permute-start.2 = (bf16[96,1536]{1,0:T(8,128)(2,1)S(1)}, bf16[96,1536]{1,0:T(8,128)(2,1)S(1)}, u32[]{:S(2)}, u32[]{:S(2)}) collective-permute-start(bf16[96,1536]{1,0:T(8,128)(2,1)S(1)} %collective-permute-done.1.refs_2_), channel_id=1, source_target_pairs={{0,16},{16,0},{1,17},{17,1},{2,18},{18,2},{3,19},{19,3},{4,20},{20... | collective-permute-start | bytes 884744 | tf_op jit(solution)/shard_map/ppermute | solution.py:591
  20.5 3.5 %collective-permute-start.5 = (bf16[256,512]{1,0:T(8,128)(2,1)S(1)}, bf16[256,512]{1,0:T(8,128)(2,1)S(1)}, u32[]{:S(2)}, u32[]{:S(2)}) collective-permute-start(bf16[256,512]{1,0:T(8,128)(2,1)S(1)} %get-tuple-element.33.msg_ref), channel_id=1, source_target_pairs={{0,4},{4,8},{8,12},{1,5},{5,9},{9,13},{2,6},{6,10},{10,14},{3,7},{... | collective-permute-start | bytes 786440 | tf_op jit(solution)/shard_map/ppermute | solution.py:615
  23.9 4.4 %collective-permute-done.5.got_ref = bf16[256,512]{1,0:T(8,128)(2,1)S(1)} collective-permute-done((bf16[256,512]{1,0:T(8,128)(2,1)S(1)}, bf16[256,512]{1,0:T(8,128)(2,1)S(1)}, u32[]{:S(2)}, u32[]{:S(2)}) %collective-permute-start.5) | collective-permute-done | bytes 262176 | tf_op jit(solution)/shard_map/ppermute | solution.py:615
  28.3 1.5 %collective-permute-start.12 = (bf16[192,768]{1,0:T(8,128)(2,1)S(1)}, bf16[192,768]{1,0:T(8,128)(2,1)S(1)}, u32[]{:S(2)}, u32[]{:S(2)}) collective-permute-start(bf16[192,768]{1,0:T(8,128)(2,1)S(1)} %get-tuple-element.52), channel_id=1, source_target_pairs={{0,2},{2,0},{1,3},{3,1},{4,6},{6,4},{5,7},{7,5},{8,10},{10,8},{9,1... | collective-permute-start | bytes 884744 | tf_op jit(solution)/shard_map/ppermute | solution.py:591
  29.8 0.5 collective-permute-start.17
  30.4 0.5 collective-permute-start.4
  30.9 2.0 %central.1 = (f32[128,512]{1,0:T(8,128)S(1)}, f32[256,256]{1,0:T(8,128)S(1)}, bf16[512,128]{1,0:T(8,128)(2,1)S(1)}) custom-call(bf16[256,512]{1,0:T(8,128)(2,1)S(1)} %get-tuple-element.33.msg_ref, bf16[512,1024]{1,0:T(8,128)(2,1)S(1)} %get-tuple-element.36.x_ref, bf16[576,128]{1,0:T(8,128)(2,1)S(1)} %get-tuple-element.34.k1_ref, ...), custom_call_target="tpu_custom_call" | custom-call | tf_op jit(solution)/shard_map/central/pallas_call | solution.py:454
  33.0 0.8 %mix.1 = (f32[128,768]{1,0:T(8,128)S(1)}, bf16[512,768]{1,0:T(8,128)(2,1)S(1)}) custom-call(bf16[512,128]{1,0:T(8,128)(2,1)S(1)} %get-tuple-element.39.patch, bf16[256,768]{1,0:T(8,128)(2,1)S(1)} %copy-done.1, bf16[256,768]{1,0:T(8,128)(2,1)S(1)} %collective-permute-done.6.refs_1_, bf16[256,768]{1,0:T(8,128)(2,1)S(1)} %collective-permute-done.7.refs_2_), custom_call_target="tpu_custom_call" | custom-call | tf_op jit(solution)/shard_map/mix/pallas_call | solution.py:474
  34.3 1.3 %back.1 = (bf16[136,768]{1,0:T(8,128)(2,1)S(1)}, bf16[64,768]{1,0:T(8,128)(2,1)S(1)}, bf16[72,768]{1,0:T(8,128)(2,1)S(1)}) custom-call(bf16[256,512]{1,0:T(8,128)(2,1)S(1)} %collective-permute-done.5.got_ref, bf16[576,128]{1,0:T(8,128)(2,1)S(1)} %get-tuple-element.34.k1_ref, bf16[1152,256]{1,0:T(8,128)(2,1)S(1)} %get-tuple-element.35.k2_ref, ...), custom_call_target="tpu_custom_call" | custom-call | tf_op jit(solution)/shard_map/back/pallas_call | solution.py:503
  35.6 2.6 %collective-permute-done.12.refs_6_ = bf16[192,768]{1,0:T(8,128)(2,1)S(1)} collective-permute-done((bf16[192,768]{1,0:T(8,128)(2,1)S(1)}, bf16[192,768]{1,0:T(8,128)(2,1)S(1)}, u32[]{:S(2)}, u32[]{:S(2)}) %collective-permute-start.12) | collective-permute-done | bytes 294944 | tf_op jit(solution)/shard_map/ppermute | solution.py:591
  38.2 3.5 %collective-permute-start.10 = (bf16[64,768]{1,0:T(8,128)(2,1)S(1)}, bf16[64,768]{1,0:T(8,128)(2,1)S(1)}, u32[]{:S(2)}, u32[]{:S(2)}) collective-permute-start(bf16[64,768]{1,0:T(8,128)(2,1)S(1)} %get-tuple-element.50), channel_id=1, source_target_pairs={{0,8},{4,12},{8,0},{12,4},{1,9},{5,13},{9,1},{13,5},{2,10},{6,14},... | collective-permute-start | bytes 294920 | tf_op jit(solution)/shard_map/ppermute | solution.py:591
  41.7 2.2 %collective-permute-start.9 = (bf16[136,768]{1,0:T(8,128)(2,1)S(1)}, bf16[136,768]{1,0:T(8,128)(2,1)S(1)}, u32[]{:S(2)}, u32[]{:S(2)}) collective-permute-start(bf16[136,768]{1,0:T(8,128)(2,1)S(1)} %get-tuple-element.44.refs_6_.refs_0_), channel_id=1, source_target_pairs={{0,4},{4,0},{8,12},{12,8},{1,5},{5,1},{9,13},{13,9},{2,6},{6,2},{1... | collective-permute-start | bytes 626696 | tf_op jit(solution)/shard_map/ppermute | solution.py:591
  43.9 0.5 collective-permute-start.16
  44.5 3.3 %collective-permute-start.11 = (bf16[72,768]{1,0:T(8,128)(2,1)S(1)}, bf16[72,768]{1,0:T(8,128)(2,1)S(1)}, u32[]{:S(2)}, u32[]{:S(2)}) collective-permute-start(bf16[72,768]{1,0:T(8,128)(2,1)S(1)} %get-tuple-element.51), channel_id=1, source_target_pairs={{0,8},{4,12},{8,0},{12,4},{1,9},{5,13},{9,1},{13,5},{2,10},{6,14},... | collective-permute-start | bytes 331784 | tf_op jit(solution)/shard_map/ppermute | solution.py:591
  47.8 5.3 %collective-permute-done.11.refs_3_ = bf16[72,768]{1,0:T(8,128)(2,1)S(1)} collective-permute-done((bf16[72,768]{1,0:T(8,128)(2,1)S(1)}, bf16[72,768]{1,0:T(8,128)(2,1)S(1)}, u32[]{:S(2)}, u32[]{:S(2)}) %collective-permute-start.11) | collective-permute-done | bytes 110624 | tf_op jit(solution)/shard_map/ppermute | solution.py:591
  53.2 1.9 %collective-permute-start.14 = (bf16[64,768]{1,0:T(8,128)(2,1)S(1)}, bf16[64,768]{1,0:T(8,128)(2,1)S(1)}, u32[]{:S(2)}, u32[]{:S(2)}) collective-permute-start(bf16[64,768]{1,0:T(8,128)(2,1)S(1)} %collective-permute-done.10.refs_2_), channel_id=1, source_target_pairs={{0,4},{4,0},{8,12},{12,8},{1,5},{5,1},{9,13},{13,9},{2,6},{6,2},{1... | collective-permute-start | bytes 294920 | tf_op jit(solution)/shard_map/ppermute | solution.py:591
  55.1 1.5 %prepare.1 = (bf16[768,1536]{1,0:T(8,128)(2,1)S(1)}, bf16[256,768]{1,0:T(8,128)(2,1)S(1)}, bf16[256,768]{1,0:T(8,128)(2,1)S(1)}, bf16[256,768]{1,0:T(8,128)(2,1)S(1)}, bf16[512,512]{1,0:T(8,128)(2,1)S(1)}) custom-call(s32[4,128]{1,0:T(4,128)S(1)} %bitcast.5, bf16[192,2304]{1,0:T(8,128)(2,1)S(1)} %copy-done, ...), custom_call_target="tpu_custom_call" | custom-call | tf_op jit(solution)/shard_map/prepare/pallas_call | solution.py:522
  56.7 1.2 %extend.1 = (bf16[768,768]{1,0:T(8,128)(2,1)S(1)}, bf16[128,768]{1,0:T(8,128)(2,1)S(1)}, bf16[128,768]{1,0:T(8,128)(2,1)S(1)}, f32[128,768]{1,0:T(8,128)S(1)}, f...) custom-call(bf16[512,512]{1,0:T(8,128)(2,1)S(1)} %get-tuple-element.45.perm_ref, ...), custom_call_target="tpu_custom_call" | custom-call | tf_op jit(solution)/shard_map/extend/pallas_call | solution.py:542
  57.9 2.0 %collective-permute-done.14.refs_0_ = bf16[64,768]{1,0:T(8,128)(2,1)S(1)} collective-permute-done((bf16[64,768]{1,0:T(8,128)(2,1)S(1)}, bf16[64,768]{1,0:T(8,128)(2,1)S(1)}, u32[]{:S(2)}, u32[]{:S(2)}) %collective-permute-start.14) | collective-permute-done | bytes 98336 | tf_op jit(solution)/shard_map/ppermute | solution.py:591
  59.8 4.5 %finish.1 = bf16[128,768]{1,0:T(8,128)(2,1)} custom-call(bf16[512,512]{1,0:T(8,128)(2,1)S(1)} %get-tuple-element.45.perm_ref, bf16[768,1536]{1,0:T(8,128)(2,1)S(1)} %get-tuple-element.46.joined, bf16[256,768]{1,0:T(8,128)(2,1)S(1)} %get-tuple-element.47.keys0, bf16[256,768]{1,0:T(8,128)(2,1)S(1)} %get-tuple-element.48.values0, ...), custom_call_target="tpu_custom_call" | custom-call | tf_op jit(solution)/shard_map/finish/pallas_call | solution.py:570
  (32 shorter events, 1.4 us)
Async XLA Ops:
  0.0 5.5 %copy-start.1 = (bf16[256,768]{1,0:T(8,128)(2,1)S(1)}, bf16[256,768]{1,0:T(8,128)(2,1)}, u32[]{:S(2)}) copy-start(bf16[256,768]{1,0:T(8,128)(2,1)} %refs_0_.4) | copy-start | bytes 1179652
  0.0 5.5 %copy-start = (bf16[192,2304]{1,0:T(8,128)(2,1)S(1)}, bf16[192,2304]{1,0:T(8,128)(2,1)}, u32[]{:S(2)}) copy-start(bf16[192,2304]{1,0:T(8,128)(2,1)} %refs_4_.1) | copy-start | bytes 2654212
  0.0 29.8 %copy-start.2 = (bf16[192,768]{1,0:T(8,128)(2,1)S(1)}, bf16[192,768]{1,0:T(8,128)(2,1)}, u32[]{:S(2)}) copy-start(bf16[192,768]{1,0:T(8,128)(2,1)} %refs_2_.1) | copy-start | bytes 884740
  0.0 13.2 %collective-permute-start.7 = (bf16[256,768]{1,0:T(8,128)(2,1)}, bf16[256,768]{1,0:T(8,128)(2,1)S(1)}, u32[]{:S(2)}, u32[]{:S(2)}) collective-permute-start(bf16[256,768]{1,0:T(8,128)(2,1)} %refs_0_.4), channel_id=1, source_target_pairs={{0,2},{2,0},{1,3},{3,1},{4,6},{6,4},{5,7},{7,5},{8,10},{10,8},{9,1... | collective-permute-start | bytes 1179656 | tf_op jit(solution)/shard_map/ppermute | solution.py:591
  5.3 28.9 %copy-start.4 = (s32[1,128]{1,0:T(1,128)S(1)}, s32[1,128]{1,0:T(1,128)}, u32[]{:S(2)}) copy-start(s32[1,128]{1,0:T(1,128)} %active_ref.1) | copy-start | bytes 1540
  5.3 13.4 %collective-permute-start.1 = (bf16[96,1536]{1,0:T(8,128)(2,1)S(1)}, bf16[96,1536]{1,0:T(8,128)(2,1)S(1)}, u32[]{:S(2)}, u32[]{:S(2)}) collective-permute-start(bf16[96,1536]{1,0:T(8,128)(2,1)S(1)} %get-tuple-element.32), channel_id=1, source_target_pairs={{0,2},{2,0},{1,3},{3,1},{4,6},{6,4},{5,7},{7,5},{8,10},{10,8},{9,1... | collective-permute-start | bytes 884744 | tf_op jit(solution)/shard_map/ppermute | solution.py:591
  5.5 38.4 %collective-permute-start = (bf16[192,2304]{1,0:T(8,128)(2,1)S(1)}, bf16[192,2304]{1,0:T(8,128)(2,1)S(1)}, u32[]{:S(2)}, u32[]{:S(2)}) collective-permute-start(bf16[192,2304]{1,0:T(8,128)(2,1)S(1)} %copy-done), channel_id=1, source_target_pairs={{0,1},{1,0},{2,3},{3,2},{4,5},{5,4},{6,7},{7,6},{8,9},{9,8},{10,11... | collective-permute-start | bytes 2654216 | tf_op jit(solution)/shard_map/ppermute | solution.py:591
  5.5 24.3 %collective-permute-start.6 = (bf16[256,768]{1,0:T(8,128)(2,1)S(1)}, bf16[256,768]{1,0:T(8,128)(2,1)S(1)}, u32[]{:S(2)}, u32[]{:S(2)}) collective-permute-start(bf16[256,768]{1,0:T(8,128)(2,1)S(1)} %copy-done.1), channel_id=1, source_target_pairs={{0,1},{1,0},{2,3},{3,2},{4,5},{5,4},{6,7},{7,6},{8,9},{9,8},{10,11... | collective-permute-start | bytes 1179656 | tf_op jit(solution)/shard_map/ppermute | solution.py:591
  13.2 17.2 %collective-permute-start.8 = (bf16[256,768]{1,0:T(8,128)(2,1)S(1)}, bf16[256,768]{1,0:T(8,128)(2,1)S(1)}, u32[]{:S(2)}, u32[]{:S(2)}) collective-permute-start(bf16[256,768]{1,0:T(8,128)(2,1)S(1)} %collective-permute-done.7.refs_2_), channel_id=1, source_target_pairs={{0,1},{1,0},{2,3},{3,2},{4,5},{5,4},{6,7},{7,6},{8,9},{9,8},{10,11... | collective-permute-start | bytes 1179656 | tf_op jit(solution)/shard_map/ppermute | solution.py:591
  18.7 11.7 %collective-permute-start.2 = (bf16[96,1536]{1,0:T(8,128)(2,1)S(1)}, bf16[96,1536]{1,0:T(8,128)(2,1)S(1)}, u32[]{:S(2)}, u32[]{:S(2)}) collective-permute-start(bf16[96,1536]{1,0:T(8,128)(2,1)S(1)} %collective-permute-done.1.refs_2_), channel_id=1, source_target_pairs={{0,16},{16,0},{1,17},{17,1},{2,18},{18,2},{3,19},{19,3},{4,20},{20... | collective-permute-start | bytes 884744 | tf_op jit(solution)/shard_map/ppermute | solution.py:591
  20.5 7.9 %collective-permute-start.5 = (bf16[256,512]{1,0:T(8,128)(2,1)S(1)}, bf16[256,512]{1,0:T(8,128)(2,1)S(1)}, u32[]{:S(2)}, u32[]{:S(2)}) collective-permute-start(bf16[256,512]{1,0:T(8,128)(2,1)S(1)} %get-tuple-element.33.msg_ref), channel_id=1, source_target_pairs={{0,4},{4,8},{8,12},{1,5},{5,9},{9,13},{2,6},{6,10},{10,14},{3,7},{... | collective-permute-start | bytes 786440 | tf_op jit(solution)/shard_map/ppermute | solution.py:615
  28.3 9.9 %collective-permute-start.12 = (bf16[192,768]{1,0:T(8,128)(2,1)S(1)}, bf16[192,768]{1,0:T(8,128)(2,1)S(1)}, u32[]{:S(2)}, u32[]{:S(2)}) collective-permute-start(bf16[192,768]{1,0:T(8,128)(2,1)S(1)} %get-tuple-element.52), channel_id=1, source_target_pairs={{0,2},{2,0},{1,3},{3,1},{4,6},{6,4},{5,7},{7,5},{8,10},{10,8},{9,1... | collective-permute-start | bytes 884744 | tf_op jit(solution)/shard_map/ppermute | solution.py:591
  29.8 11.9 %collective-permute-start.17 = (bf16[192,768]{1,0:T(8,128)(2,1)S(1)}, bf16[192,768]{1,0:T(8,128)(2,1)S(1)}, u32[]{:S(2)}, u32[]{:S(2)}) collective-permute-start(bf16[192,768]{1,0:T(8,128)(2,1)S(1)} %copy-done.2), channel_id=1, source_target_pairs={{0,2},{2,0},{1,3},{3,1},{4,6},{6,4},{5,7},{7,5},{8,10},{10,8},{9,1... | collective-permute-start | bytes 884744 | tf_op jit(solution)/shard_map/ppermute | solution.py:591
  30.4 13.5 %collective-permute-start.3 = (bf16[96,1536]{1,0:T(8,128)(2,1)S(1)}, bf16[96,1536]{1,0:T(8,128)(2,1)S(1)}, u32[]{:S(2)}, u32[]{:S(2)}) collective-permute-start(bf16[96,1536]{1,0:T(8,128)(2,1)S(1)} %collective-permute-done.1.refs_2_), channel_id=1, source_target_pairs={{0,1},{1,0},{2,3},{3,2},{4,5},{5,4},{6,7},{7,6},{8,9},{9,8},{10,11... | collective-permute-start | bytes 884744 | tf_op jit(solution)/shard_map/ppermute | solution.py:591
  30.4 14.0 %collective-permute-start.4 = (bf16[96,1536]{1,0:T(8,128)(2,1)S(1)}, bf16[96,1536]{1,0:T(8,128)(2,1)S(1)}, u32[]{:S(2)}, u32[]{:S(2)}) collective-permute-start(bf16[96,1536]{1,0:T(8,128)(2,1)S(1)} %collective-permute-done.2.refs_3_), channel_id=1, source_target_pairs={{0,1},{1,0},{2,3},{3,2},{4,5},{5,4},{6,7},{7,6},{8,9},{9,8},{10,11... | collective-permute-start | bytes 884744 | tf_op jit(solution)/shard_map/ppermute | solution.py:591
  32.9 22.2 %copy-start.3 = (s32[1,512]{1,0:T(1,128)S(1)}, s32[1,512]{1,0:T(1,128)}, u32[]{:S(2)}) copy-start(s32[1,512]{1,0:T(1,128)} %param.14) | copy-start | bytes 6148
  38.2 6.3 %collective-permute-start.10 = (bf16[64,768]{1,0:T(8,128)(2,1)S(1)}, bf16[64,768]{1,0:T(8,128)(2,1)S(1)}, u32[]{:S(2)}, u32[]{:S(2)}) collective-permute-start(bf16[64,768]{1,0:T(8,128)(2,1)S(1)} %get-tuple-element.50), channel_id=1, source_target_pairs={{0,8},{4,12},{8,0},{12,4},{1,9},{5,13},{9,1},{13,5},{2,10},{6,14},... | collective-permute-start | bytes 294920 | tf_op jit(solution)/shard_map/ppermute | solution.py:591
  41.7 11.5 %collective-permute-start.9 = (bf16[136,768]{1,0:T(8,128)(2,1)S(1)}, bf16[136,768]{1,0:T(8,128)(2,1)S(1)}, u32[]{:S(2)}, u32[]{:S(2)}) collective-permute-start(bf16[136,768]{1,0:T(8,128)(2,1)S(1)} %get-tuple-element.44.refs_6_.refs_0_), channel_id=1, source_target_pairs={{0,4},{4,0},{8,12},{12,8},{1,5},{5,1},{9,13},{13,9},{2,6},{6,2},{1... | collective-permute-start | bytes 626696 | tf_op jit(solution)/shard_map/ppermute | solution.py:591
  43.9 12.8 %collective-permute-start.13 = (bf16[192,768]{1,0:T(8,128)(2,1)S(1)}, bf16[192,768]{1,0:T(8,128)(2,1)S(1)}, u32[]{:S(2)}, u32[]{:S(2)}) collective-permute-start(bf16[192,768]{1,0:T(8,128)(2,1)S(1)} %collective-permute-done.12.refs_6_), channel_id=1, source_target_pairs={{0,1},{1,0},{2,3},{3,2},{4,5},{5,4},{6,7},{7,6},{8,9},{9,8},{10,11... | collective-permute-start | bytes 884744 | tf_op jit(solution)/shard_map/ppermute | solution.py:591
  43.9 13.9 %collective-permute-start.16 = (bf16[192,768]{1,0:T(8,128)(2,1)S(1)}, bf16[192,768]{1,0:T(8,128)(2,1)S(1)}, u32[]{:S(2)}, u32[]{:S(2)}) collective-permute-start(bf16[192,768]{1,0:T(8,128)(2,1)S(1)} %copy-done.2), channel_id=1, source_target_pairs={{0,1},{1,0},{2,3},{3,2},{4,5},{5,4},{6,7},{7,6},{8,9},{9,8},{10,11... | collective-permute-start | bytes 884744 | tf_op jit(solution)/shard_map/ppermute | solution.py:591
  44.4 13.4 %collective-permute-start.18 = (bf16[192,768]{1,0:T(8,128)(2,1)S(1)}, bf16[192,768]{1,0:T(8,128)(2,1)S(1)}, u32[]{:S(2)}, u32[]{:S(2)}) collective-permute-start(bf16[192,768]{1,0:T(8,128)(2,1)S(1)} %collective-permute-done.17.refs_4_), channel_id=1, source_target_pairs={{0,1},{1,0},{2,3},{3,2},{4,5},{5,4},{6,7},{7,6},{8,9},{9,8},{10,11... | collective-permute-start | bytes 884744 | tf_op jit(solution)/shard_map/ppermute | solution.py:591
  44.5 8.6 %collective-permute-start.11 = (bf16[72,768]{1,0:T(8,128)(2,1)S(1)}, bf16[72,768]{1,0:T(8,128)(2,1)S(1)}, u32[]{:S(2)}, u32[]{:S(2)}) collective-permute-start(bf16[72,768]{1,0:T(8,128)(2,1)S(1)} %get-tuple-element.51), channel_id=1, source_target_pairs={{0,8},{4,12},{8,0},{12,4},{1,9},{5,13},{9,1},{13,5},{2,10},{6,14},... | collective-permute-start | bytes 331784 | tf_op jit(solution)/shard_map/ppermute | solution.py:591
  53.1 6.7 %collective-permute-start.15 = (bf16[72,768]{1,0:T(8,128)(2,1)S(1)}, bf16[72,768]{1,0:T(8,128)(2,1)S(1)}, u32[]{:S(2)}, u32[]{:S(2)}) collective-permute-start(bf16[72,768]{1,0:T(8,128)(2,1)S(1)} %collective-permute-done.11.refs_3_), channel_id=1, source_target_pairs={{0,4},{4,0},{8,12},{12,8},{1,5},{5,1},{9,13},{13,9},{2,6},{6,2},{1... | collective-permute-start | bytes 331784 | tf_op jit(solution)/shard_map/ppermute | solution.py:591
  53.2 6.6 %collective-permute-start.14 = (bf16[64,768]{1,0:T(8,128)(2,1)S(1)}, bf16[64,768]{1,0:T(8,128)(2,1)S(1)}, u32[]{:S(2)}, u32[]{:S(2)}) collective-permute-start(bf16[64,768]{1,0:T(8,128)(2,1)S(1)} %collective-permute-done.10.refs_2_), channel_id=1, source_target_pairs={{0,4},{4,0},{8,12},{12,8},{1,5},{5,1},{9,13},{13,9},{2,6},{6,2},{1... | collective-permute-start | bytes 294920 | tf_op jit(solution)/shard_map/ppermute | solution.py:591

commit v4 on v3

--- a/solution.py
+++ b/solution.py
@@ -192,7 +192,7 @@
 def back_kernel(
     got_ref, k1_ref, k2_ref, active_ref, first_ref, second_ref, token_ref, low_ref, *refs, channels, middle
 ):
-    out_ref, upper_ref, lower_ref, all1, all2, patch = refs[-6:]
+    out_ref, all1, all2, patch = refs[-4:]
     splitter = split_matrix()
     odd = got_ref[channels : 2 * channels, :].astype(F32)
     all1[:channels, :] = later(odd).astype(BF)
@@ -205,19 +205,14 @@
     out = silu(second_ref[...] + dot(k2_ref[: 6 * middle, :], all2[...], 0, 0)).astype(BF)
     store_patch(patch, out, splitter)
     total = token_ref[...] + dot(patch[...], low_ref[...], 0, 0)
-    if len(refs) > 6:
+    if len(refs) > 4:
         base = pl.multiple_of(block_of(True, 3) * 128, 128)
         total += dot(patch[pl.ds(base, 128), :], refs[0][...], 0, 0)
     count, width = total.shape
-    total = total.astype(BF)
-    half = count // 2
-    out_ref[:count, :] = total
-    upper_ref[...] = total[:half]
-    lower_ref[:half, :] = total[half:]
+    out_ref[:count, :] = total.astype(BF)
     tail = jnp.broadcast_to(active_ref[...].astype(F32), (EXTRA, count))
     tail = jnp.concatenate([tail, jnp.zeros((EXTRA, width - count), F32)], axis=1)
     out_ref[count:, :] = tail.astype(BF)
-    lower_ref[half:, :] = tail.astype(BF)
 
 
 def normal(tokens):
@@ -225,24 +220,6 @@
     value = value - jnp.mean(value, axis=-1, keepdims=True)
     spread = jnp.mean(value * value, axis=-1, keepdims=True)
     return (value * lax.rsqrt(spread + epsilon)).astype(BF)
-
-
-def unpack(refs, layout):
-    chunks, start = [], 0
-    for parts in layout:
-        chunks.append(refs[start : start + parts])
-        start += parts
-    return chunks
-
-
-def rows_of(chunk):
-    parts = [ref[...] for ref in chunk[:-1]]
-    parts.append(chunk[-1][: chunk[-1].shape[0] - EXTRA, :])
-    return parts[0] if len(parts) == 1 else jnp.concatenate(parts, axis=0)
-
-
-def flags_of(chunk, count):
-    return chunk[-1][chunk[-1].shape[0] - EXTRA :, :count]
 
 
 def lift(joined, normed, keys, values):
@@ -304,26 +281,25 @@
         down = jnp.sum(jnp.where(square, across, 0.0), axis=1, keepdims=True)
         perm_ref[slot * count : (slot + 1) * count, :] = one_hot(labels == down)
     for slot, ref in enumerate(chunk_refs):
-        normed[slot * count : (slot + 1) * count, :] = normal(rows_of([ref]))
+        normed[slot * count : (slot + 1) * count, :] = normal(ref[:count, :])
     for copy in copies:
         copy.wait()
     lift(joined, normed, keys, values)
 
 
-def extend_kernel(perm_ref, joined, normed0, *refs, pieces, layout, early, swap):
-    total = sum(layout)
-    chunks = unpack(refs[:total], layout)
-    query_refs = refs[total : total + pieces]
-    query, keys1, values1, token_ref, picked_ref, on_ref, normed1, sems = refs[total + pieces :]
+def extend_kernel(perm_ref, joined, normed0, *refs, pieces, chunks, early, swap):
+    chunk_refs = refs[:chunks]
+    query_refs = refs[chunks : chunks + pieces]
+    query, keys1, values1, token_ref, picked_ref, on_ref, normed1, sems = refs[chunks + pieces :]
     count = token_ref.shape[0]
     copies = collect(weight_rows(query_refs), query, sems)
-    for slot, chunk in enumerate(chunks[early:]):
-        normed1[slot * count : (slot + 1) * count, :] = normal(rows_of(chunk))
+    for slot, ref in enumerate(chunk_refs[early:]):
+        normed1[slot * count : (slot + 1) * count, :] = normal(ref[:count, :])
     lift(joined, normed1, keys1, values1)
     own = own_rows(perm_ref, count, swap)
-    near, far = early * count, len(layout) * count
+    near, far = early * count, chunks * count
     picked_ref[...] = dot(own[:, :near], normed0[...]) + dot(own[:, near:far], normed1[...])
-    on, token = flags_and_tokens(perm_ref, own, chunks, 0)
+    on, token = flags_and_tokens(perm_ref, own, chunk_refs, 0)
     on_ref[...] = on
     token_ref[...] = token
     for copy in copies:
@@ -343,35 +319,34 @@
     return perm_ref[pl.ds(pl.multiple_of(slot * count, count), count), :]
 
 
-def flags_and_tokens(perm_ref, own, chunks, first):
+def flags_and_tokens(perm_ref, own, chunk_refs, first):
     count = own.shape[0]
     on = token = 0.0
-    for slot, chunk in enumerate(chunks):
+    for slot, ref in enumerate(chunk_refs):
         here = slice((first + slot) * count, (first + slot + 1) * count)
-        on += dot(flags_of(chunk, count), perm_ref[here, :])
-        token += dot(own[:, here], rows_of(chunk))
+        on += dot(ref[count:, :count], perm_ref[here, :])
+        token += dot(own[:, here], ref[:count, :])
     return on, token
 
 
 def finish_kernel(
     perm_ref, joined, keys0, values0, keys1, values1, query, token_ref, picked_ref, on_ref, *refs,
-    pieces, layout, swap
+    pieces, chunks, swap
 ):
-    total = sum(layout)
-    chunks = unpack(refs[:total], layout)
-    output_refs = refs[total : total + pieces]
-    out_ref, output, normed2, keys2, values2, cap, mixed, sems = refs[total + pieces :]
+    chunk_refs = refs[:chunks]
+    output_refs = refs[chunks : chunks + pieces]
+    out_ref, output, normed2, keys2, values2, cap, mixed, sems = refs[chunks + pieces :]
     copies = collect(weight_rows(output_refs), output, sems)
     count, width = token_ref.shape
-    first = perm_ref.shape[0] // count - len(layout)
-    for slot, chunk in enumerate(chunks):
-        normed2[slot * count : (slot + 1) * count, :] = normal(rows_of(chunk))
+    first = perm_ref.shape[0] // count - chunks
+    for slot, ref in enumerate(chunk_refs):
+        normed2[slot * count : (slot + 1) * count, :] = normal(ref[:count, :])
     lift(joined, normed2, keys2, values2)
     own = own_rows(perm_ref, count, swap)
     picked = (picked_ref[...] + dot(own[:, first * count :], normed2[...])).astype(BF)
     head = width // HEADS
     queries = (dot(picked, query[...]) * head ** (-0.5)).astype(BF)
-    on, token = flags_and_tokens(perm_ref, own, chunks, first)
+    on, token = flags_and_tokens(perm_ref, own, chunk_refs, first)
     on += on_ref[...]
     token += token_ref[...]
     allowed = (own.astype(F32) + jnp.broadcast_to(on[:1], own.shape)) > 0.5
@@ -498,13 +473,12 @@
     channels = k1.shape[0] // 9
     length = got.shape[1]
     count = active.shape[1]
-    half = count // 2
     width = parts[2].shape[1]
     return pl.pallas_call(
         functools.partial(back_kernel, channels=channels, middle=middle),
-        out_shape=(array((count + EXTRA, width)), array((half, width)), array((half + EXTRA, width))),
+        out_shape=array((count + EXTRA, width)),
         in_specs=[vmem()] * (4 + len(parts)),
-        out_specs=[vmem()] * 3,
+        out_specs=vmem(),
         scratch_shapes=[
             pltpu.VMEM((3 * channels, length), BF),
             pltpu.VMEM((6 * middle, length // 2), BF),
@@ -534,13 +508,11 @@
     joined, normed, _, _, perm = ready
     width = joined.shape[0]
     size = perm.shape[0]
-    count = chunks[0][0].shape[0] - EXTRA
+    count = chunks[0].shape[0] - EXTRA
     far = (len(chunks) - early) * count
     pieces = len(weights)
-    layout = tuple(len(chunk) for chunk in chunks)
-    flat = [part for chunk in chunks for part in chunk]
-    return pl.pallas_call(
-        functools.partial(extend_kernel, pieces=pieces, layout=layout, early=early, swap=swap),
+    return pl.pallas_call(
+        functools.partial(extend_kernel, pieces=pieces, chunks=len(chunks), early=early, swap=swap),
         out_shape=(
             array((width, width)),
             array((far, width)),
@@ -549,12 +521,12 @@
             array((count, width), F32),
             array((EXTRA, size), F32),
         ),
-        in_specs=[vmem()] * (3 + len(flat)) + [fixed()] + [hbm()] * (pieces - 1),
+        in_specs=[vmem()] * (3 + len(chunks)) + [fixed()] + [hbm()] * (pieces - 1),
         out_specs=[vmem()] * 6,
         scratch_shapes=[pltpu.VMEM((far, width), BF), pltpu.SemaphoreType.DMA((pieces,))],
         compiler_params=params(8 + size // 128),
         name="extend",
-    )(perm, joined, normed, *flat, *weights)
+    )(perm, joined, normed, *chunks, *weights)
 
 
 def finish(ready, extra, chunks, weights, swap):
@@ -565,12 +537,10 @@
     count = token.shape[0]
     far = len(chunks) * count
     pieces = len(weights)
-    layout = tuple(len(chunk) for chunk in chunks)
-    flat = [part for chunk in chunks for part in chunk]
-    return pl.pallas_call(
-        functools.partial(finish_kernel, pieces=pieces, layout=layout, swap=swap),
+    return pl.pallas_call(
+        functools.partial(finish_kernel, pieces=pieces, chunks=len(chunks), swap=swap),
         out_shape=array((count, width)),
-        in_specs=[vmem()] * (10 + len(flat)) + [fixed()] + [hbm()] * (pieces - 1),
+        in_specs=[vmem()] * (10 + len(chunks)) + [fixed()] + [hbm()] * (pieces - 1),
         out_specs=vmem(),
         scratch_shapes=[
             pltpu.VMEM((width, width), BF),
@@ -583,7 +553,7 @@
         ],
         compiler_params=params(8 + size // 64),
         name="finish",
-    )(perm, joined, keys, values, keys1, values1, query, token, picked, on, *flat, *weights)
+    )(perm, joined, keys, values, keys1, values1, query, token, picked, on, *chunks, *weights)
 
 
 def exchanged(value, axis, flip):
@@ -619,15 +589,14 @@
     if paired:
         parts[2], corner_low = blend(patch, token, embed_corner)
         parts.append(corner_low)
-    tokens, upper, lower = back(got, k1, k2, active, *parts)
+    tokens = back(got, k1, k2, active, *parts)
     if swap:
-        chunks = [[tokens], [exchanged(tokens, "seq", 1)]]
-        chunks.append([exchanged(upper, "seq", 2), exchanged(lower, "seq", 2)])
-        chunks.append([exchanged(chunks[2][0], "seq", 1), exchanged(chunks[2][1], "seq", 1)])
+        chunks = [tokens] + [exchanged(tokens, "seq", flip) for flip in (1, 2)]
+        chunks.append(exchanged(chunks[2], "seq", 1))
     else:
         everyone = lax.all_gather(tokens, "seq", axis=0, tiled=True)
         each = count + EXTRA
-        chunks = [[everyone[i * each : (i + 1) * each]] for i in range(shards)]
+        chunks = [everyone[i * each : (i + 1) * each] for i in range(shards)]
     if paired:
         project_beside = exchanged(project_weight, "section", 1)
         output_beside = exchanged(output_weight, "section", 1)
@@ -647,7 +616,7 @@
         query_weights = kv_weights
         output_weights = [lax.all_gather(output_weight, ("mp", "section"), axis=0, tiled=True)]
     early, later = shards // 2, shards // 2 + shards // 4
-    ready = prepare(order, kv_weights, [chunk[0] for chunk in chunks[:early]], swap)
+    ready = prepare(order, kv_weights, chunks[:early], swap)
     extra = extend(ready, chunks[:later], query_weights, early, swap)
     result = finish(ready, extra, chunks[later:], output_weights, swap)
     return result[None]

time: 64.5 us -> 55.5 us (0.86)
  starting transfers between devices: 23.1 us -> 17.3 us
  waiting for transfers between devices: 27 us -> 23.8 us
    ppermute x18 -> x16, starting transfers between devices: 19.6 us -> 13.4 us  [exchanged(): return lax.ppermute(value, axis, [(i, i ^ flip) for i in range(count)])]
    ppermute x1, waiting for transfers between devices: 4.4 us -> 0.01 us  [layer(): got = lax.ppermute(msg, 'seq', [(i, i + 1) for i in range(shards - 1)])]
    ppermute x18 -> x16, waiting for transfers between devices: 22.6 us -> 23.8 us  [exchanged(): return lax.ppermute(value, axis, [(i, i ^ flip) for i in range(count)])]
  transfers between devices with their start and end apart: 19 -> 17, of which waited for: 6 -> 6; matrix products, arithmetic and copies ran while one was open for 0% -> 0% of each run, Pallas kernels for 15% -> 17%
where the time goes in v4:
time: 55.5 us; the launch traced here: 55.3 us
  waiting for transfers between devices  23.8 us (43%)
  starting transfers between devices  17.3 us (31%)
  Pallas kernels  14.1 us (25%)
    ppermute x16, waiting for transfers between devices, exchanged(): return lax.ppermute(value, axis, [(i, i ^ flip) for i in range(count)])  23.8 us
    ppermute x16, starting transfers between devices, exchanged(): return lax.ppermute(value, axis, [(i, i ^ flip) for i in range(count)])  13.4 us
    pallas_call x1, Pallas kernels, finish(): pl.pallas_call(functools.partial(finish_kernel, pieces=pieces, chunks=len...  4.46 us
    ppermute x1, starting transfers between devices, layer(): got = lax.ppermute(msg, 'seq', [(i, i + 1) for i in range(shards - 1)])  3.9 us
    pallas_call x1, Pallas kernels, front(): pl.pallas_call(functools.partial(front_kernel, wires=wires, channels=chan...  2.27 us
    pallas_call x1, Pallas kernels, central(): pl.pallas_call(functools.partial(central_kernel, wires=wires, channels=ch...  2.05 us
    pallas_call x1, Pallas kernels, prepare(): pl.pallas_call(functools.partial(prepare_kernel, pieces=len(weights), chu...  1.53 us
    pallas_call x1, Pallas kernels, back(): pl.pallas_call(functools.partial(back_kernel, channels=channels, middle=m...  1.32 us
  transfers between devices with their start and end apart: 17, of which 6 were waited for; matrix products, arithmetic and copies ran while one was open for 0% of the time, Pallas kernels for 17%

profile of v4, /device:TPU:0, one launch (start us, length us, event | category | flops | bytes accessed | tf_op | source)
XLA Modules:
  0.0 55.3 jit_solution(67568749945967392)
XLA Ops:
  0.0 3.0 %collective-permute-start.7 = (bf16[256,768]{1,0:T(8,128)(2,1)}, bf16[256,768]{1,0:T(8,128)(2,1)S(1)}, u32[]{:S(2)}, u32[]{:S(2)}) collective-permute-start(bf16[256,768]{1,0:T(8,128)(2,1)} %refs_0_.4), channel_id=1, source_target_pairs={{0,2},{2,0},{1,3},{3,1},{4,6},{6,4},{5,7},{7,5},{8,10},{10,8},{9,1... | collective-permute-start | bytes 1179656 | tf_op jit(solution)/shard_map/ppermute | solution.py:561
  3.0 2.3 %front.1 = (bf16[256,512]{1,0:T(8,128)(2,1)S(1)}, bf16[512,1024]{1,0:T(8,128)(2,1)S(1)}, bf16[576,128]{1,0:T(8,128)(2,1)S(1)}, bf16[1152,256]{1,0:T(8,128)(2,1)S...) custom-call(bf16[512,1024]{1,0:T(8,128)(2,1)} %bitcast.6, bf16[576,128]{1,0:T(8,128)(2,1)} %bitcast.8, ...), custom_call_target="tpu_custom_call" | custom-call | tf_op jit(solution)/shard_map/front/pallas_call | solution.py:409
  5.5 0.5 collective-permute-start.6
  6.0 3.9 %collective-permute-start.5 = (bf16[256,512]{1,0:T(8,128)(2,1)S(1)}, bf16[256,512]{1,0:T(8,128)(2,1)S(1)}, u32[]{:S(2)}, u32[]{:S(2)}) collective-permute-start(bf16[256,512]{1,0:T(8,128)(2,1)S(1)} %get-tuple-element.30.msg_ref), channel_id=1, source_target_pairs={{0,4},{4,8},{8,12},{1,5},{5,9},{9,13},{2,6},{6,10},{10,14},{3,7},{... | collective-permute-start | bytes 786440 | tf_op jit(solution)/shard_map/ppermute | solution.py:585
  9.9 3.3 %collective-permute-done.7.refs_2_ = bf16[256,768]{1,0:T(8,128)(2,1)S(1)} collective-permute-done((bf16[256,768]{1,0:T(8,128)(2,1)}, bf16[256,768]{1,0:T(8,128)(2,1)S(1)}, u32[]{:S(2)}, u32[]{:S(2)}) %collective-permute-start.7) | collective-permute-done | bytes 393248 | tf_op jit(solution)/shard_map/ppermute | solution.py:561
  13.2 5.5 %collective-permute-done.1.refs_2_ = bf16[96,1536]{1,0:T(8,128)(2,1)S(1)} collective-permute-done((bf16[96,1536]{1,0:T(8,128)(2,1)S(1)}, bf16[96,1536]{1,0:T(8,128)(2,1)S(1)}, u32[]{:S(2)}, u32[]{:S(2)}) %collective-permute-start.1) | collective-permute-done | bytes 294944 | tf_op jit(solution)/shard_map/ppermute | solution.py:561
  18.7 1.8 %collective-permute-start.2 = (bf16[96,1536]{1,0:T(8,128)(2,1)S(1)}, bf16[96,1536]{1,0:T(8,128)(2,1)S(1)}, u32[]{:S(2)}, u32[]{:S(2)}) collective-permute-start(bf16[96,1536]{1,0:T(8,128)(2,1)S(1)} %collective-permute-done.1.refs_2_), channel_id=1, source_target_pairs={{0,16},{16,0},{1,17},{17,1},{2,18},{18,2},{3,19},{19,3},{4,20},{20... | collective-permute-start | bytes 884744 | tf_op jit(solution)/shard_map/ppermute | solution.py:561
  20.5 1.5 %collective-permute-start.11 = (bf16[192,768]{1,0:T(8,128)(2,1)S(1)}, bf16[192,768]{1,0:T(8,128)(2,1)S(1)}, u32[]{:S(2)}, u32[]{:S(2)}) collective-permute-start(bf16[192,768]{1,0:T(8,128)(2,1)S(1)} %get-tuple-element.46), channel_id=1, source_target_pairs={{0,2},{2,0},{1,3},{3,1},{4,6},{6,4},{5,7},{7,5},{8,10},{10,8},{9,1... | collective-permute-start | bytes 884744 | tf_op jit(solution)/shard_map/ppermute | solution.py:561
  22.0 0.5 collective-permute-start.15
  22.5 4.4 %collective-permute-done.2.refs_3_ = bf16[96,1536]{1,0:T(8,128)(2,1)S(1)} collective-permute-done((bf16[96,1536]{1,0:T(8,128)(2,1)S(1)}, bf16[96,1536]{1,0:T(8,128)(2,1)S(1)}, u32[]{:S(2)}, u32[]{:S(2)}) %collective-permute-start.2) | collective-permute-done | bytes 294944 | tf_op jit(solution)/shard_map/ppermute | solution.py:561
  26.9 0.5 collective-permute-start.4
  27.4 2.0 %central.1 = (f32[128,512]{1,0:T(8,128)S(1)}, f32[256,256]{1,0:T(8,128)S(1)}, bf16[512,128]{1,0:T(8,128)(2,1)S(1)}) custom-call(bf16[256,512]{1,0:T(8,128)(2,1)S(1)} %get-tuple-element.30.msg_ref, bf16[512,1024]{1,0:T(8,128)(2,1)S(1)} %get-tuple-element.33.x_ref, bf16[576,128]{1,0:T(8,128)(2,1)S(1)} %get-tuple-element.31.k1_ref, ...), custom_call_target="tpu_custom_call" | custom-call | tf_op jit(solution)/shard_map/central/pallas_call | solution.py:429
  29.4 0.8 %mix.1 = (f32[128,768]{1,0:T(8,128)S(1)}, bf16[512,768]{1,0:T(8,128)(2,1)S(1)}) custom-call(bf16[512,128]{1,0:T(8,128)(2,1)S(1)} %get-tuple-element.36.patch, bf16[256,768]{1,0:T(8,128)(2,1)S(1)} %copy-done.1, bf16[256,768]{1,0:T(8,128)(2,1)S(1)} %collective-permute-done.6.refs_1_, bf16[256,768]{1,0:T(8,128)(2,1)S(1)} %collective-permute-done.7.refs_2_), custom_call_target="tpu_custom_call" | custom-call | tf_op jit(solution)/shard_map/mix/pallas_call | solution.py:449
  30.7 1.3 %back.1.refs_6_.refs_0_ = bf16[136,768]{1,0:T(8,128)(2,1)S(1)} custom-call(bf16[256,512]{1,0:T(8,128)(2,1)S(1)} %collective-permute-done.5.got_ref, bf16[576,128]{1,0:T(8,128)(2,1)S(1)} %get-tuple-element.31.k1_ref, bf16[1152,256]{1,0:T(8,128)(2,1)S(1)} %get-tuple-element.32.k2_ref, s32[1,128]{1,0:T(1,128)S(1)} %copy-done.4, ...), custom_call_target="tpu_custom_call" | custom-call | tf_op jit(solution)/shard_map/back/pallas_call | solution.py:477
  32.1 2.6 %collective-permute-start.10 = (bf16[136,768]{1,0:T(8,128)(2,1)S(1)}, bf16[136,768]{1,0:T(8,128)(2,1)S(1)}, u32[]{:S(2)}, u32[]{:S(2)}) collective-permute-start(bf16[136,768]{1,0:T(8,128)(2,1)S(1)} %back.1.refs_6_.refs_0_), channel_id=1, source_target_pairs={{0,8},{4,12},{8,0},{12,4},{1,9},{5,13},{9,1},{13,5},{2,10},{6,14},... | collective-permute-start | bytes 626696 | tf_op jit(solution)/shard_map/ppermute | solution.py:561
  34.7 0.5 collective-permute-start.14
  35.3 1.6 %collective-permute-start.9 = (bf16[136,768]{1,0:T(8,128)(2,1)S(1)}, bf16[136,768]{1,0:T(8,128)(2,1)S(1)}, u32[]{:S(2)}, u32[]{:S(2)}) collective-permute-start(bf16[136,768]{1,0:T(8,128)(2,1)S(1)} %back.1.refs_6_.refs_0_), channel_id=1, source_target_pairs={{0,4},{4,0},{8,12},{12,8},{1,5},{5,1},{9,13},{13,9},{2,6},{6,2},{1... | collective-permute-start | bytes 626696 | tf_op jit(solution)/shard_map/ppermute | solution.py:561
  36.9 7.8 %collective-permute-done.10.refs_2_ = bf16[136,768]{1,0:T(8,128)(2,1)S(1)} collective-permute-done((bf16[136,768]{1,0:T(8,128)(2,1)S(1)}, bf16[136,768]{1,0:T(8,128)(2,1)S(1)}, u32[]{:S(2)}, u32[]{:S(2)}) %collective-permute-start.10) | collective-permute-done | bytes 208928 | tf_op jit(solution)/shard_map/ppermute | solution.py:561
  44.7 0.6 %collective-permute-start.13 = (bf16[136,768]{1,0:T(8,128)(2,1)S(1)}, bf16[136,768]{1,0:T(8,128)(2,1)S(1)}, u32[]{:S(2)}, u32[]{:S(2)}) collective-permute-start(bf16[136,768]{1,0:T(8,128)(2,1)S(1)} %collective-permute-done.10.refs_2_), channel_id=1, source_target_pairs={{0,4},{4,0},{8,12},{12,8},{1,5},{5,1},{9,13},{13,9},{2,6},{6,2},{1... | collective-permute-start | bytes 626696 | tf_op jit(solution)/shard_map/ppermute | solution.py:561
  45.3 0.9 %collective-permute-done.9.refs_7_.refs_1_ = bf16[136,768]{1,0:T(8,128)(2,1)S(1)} collective-permute-done((bf16[136,768]{1,0:T(8,128)(2,1)S(1)}, bf16[136,768]{1,0:T(8,128)(2,1)S(1)}, u32[]{:S(2)}, u32[]{:S(2)}) %collective-permute-start.9) | collective-permute-done | bytes 208928 | tf_op jit(solution)/shard_map/ppermute | solution.py:561
  46.2 1.5 %prepare.1 = (bf16[768,1536]{1,0:T(8,128)(2,1)S(1)}, bf16[256,768]{1,0:T(8,128)(2,1)S(1)}, bf16[256,768]{1,0:T(8,128)(2,1)S(1)}, bf16[256,768]{1,0:T(8,128)(2,1)S(1)}, bf16[512,512]{1,0:T(8,128)(2,1)S(1)}) custom-call(s32[4,128]{1,0:T(4,128)S(1)} %bitcast.5, bf16[192,2304]{1,0:T(8,128)(2,1)S(1)} %copy-done, ...), custom_call_target="tpu_custom_call" | custom-call | tf_op jit(solution)/shard_map/prepare/pallas_call | solution.py:496
  47.7 1.2 %extend.1 = (bf16[768,768]{1,0:T(8,128)(2,1)S(1)}, bf16[128,768]{1,0:T(8,128)(2,1)S(1)}, bf16[128,768]{1,0:T(8,128)(2,1)S(1)}, f32[128,768]{1,0:T(8,128)S(1)}, f...) custom-call(bf16[512,512]{1,0:T(8,128)(2,1)S(1)} %get-tuple-element.41.perm_ref, ...), custom_call_target="tpu_custom_call" | custom-call | tf_op jit(solution)/shard_map/extend/pallas_call | solution.py:514
  48.9 1.9 %collective-permute-done.13.refs_0_ = bf16[136,768]{1,0:T(8,128)(2,1)S(1)} collective-permute-done((bf16[136,768]{1,0:T(8,128)(2,1)S(1)}, bf16[136,768]{1,0:T(8,128)(2,1)S(1)}, u32[]{:S(2)}, u32[]{:S(2)}) %collective-permute-start.13) | collective-permute-done | bytes 208928 | tf_op jit(solution)/shard_map/ppermute | solution.py:561
  50.8 4.5 %finish.1 = bf16[128,768]{1,0:T(8,128)(2,1)} custom-call(bf16[512,512]{1,0:T(8,128)(2,1)S(1)} %get-tuple-element.41.perm_ref, bf16[768,1536]{1,0:T(8,128)(2,1)S(1)} %get-tuple-element.42.joined, bf16[256,768]{1,0:T(8,128)(2,1)S(1)} %get-tuple-element.43.keys0, bf16[256,768]{1,0:T(8,128)(2,1)S(1)} %get-tuple-element.44.values0, ...), custom_call_target="tpu_custom_call" | custom-call | tf_op jit(solution)/shard_map/finish/pallas_call | solution.py:540
  (28 shorter events, 0.8 us)
Async XLA Ops:
  0.0 5.5 %copy-start.1 = (bf16[256,768]{1,0:T(8,128)(2,1)S(1)}, bf16[256,768]{1,0:T(8,128)(2,1)}, u32[]{:S(2)}) copy-start(bf16[256,768]{1,0:T(8,128)(2,1)} %refs_0_.4) | copy-start | bytes 1179652
  0.0 5.5 %copy-start = (bf16[192,2304]{1,0:T(8,128)(2,1)S(1)}, bf16[192,2304]{1,0:T(8,128)(2,1)}, u32[]{:S(2)}) copy-start(bf16[192,2304]{1,0:T(8,128)(2,1)} %refs_3_.1) | copy-start | bytes 2654212
  0.0 22.0 %copy-start.2 = (bf16[192,768]{1,0:T(8,128)(2,1)S(1)}, bf16[192,768]{1,0:T(8,128)(2,1)}, u32[]{:S(2)}) copy-start(bf16[192,768]{1,0:T(8,128)(2,1)} %refs_1_.1) | copy-start | bytes 884740
  0.0 13.2 %collective-permute-start.7 = (bf16[256,768]{1,0:T(8,128)(2,1)}, bf16[256,768]{1,0:T(8,128)(2,1)S(1)}, u32[]{:S(2)}, u32[]{:S(2)}) collective-permute-start(bf16[256,768]{1,0:T(8,128)(2,1)} %refs_0_.4), channel_id=1, source_target_pairs={{0,2},{2,0},{1,3},{3,1},{4,6},{6,4},{5,7},{7,5},{8,10},{10,8},{9,1... | collective-permute-start | bytes 1179656 | tf_op jit(solution)/shard_map/ppermute | solution.py:561
  5.3 25.4 %copy-start.4 = (s32[1,128]{1,0:T(1,128)S(1)}, s32[1,128]{1,0:T(1,128)}, u32[]{:S(2)}) copy-start(s32[1,128]{1,0:T(1,128)} %active_ref.1) | copy-start | bytes 1540
  5.3 13.4 %collective-permute-start.1 = (bf16[96,1536]{1,0:T(8,128)(2,1)S(1)}, bf16[96,1536]{1,0:T(8,128)(2,1)S(1)}, u32[]{:S(2)}, u32[]{:S(2)}) collective-permute-start(bf16[96,1536]{1,0:T(8,128)(2,1)S(1)} %get-tuple-element.29), channel_id=1, source_target_pairs={{0,2},{2,0},{1,3},{3,1},{4,6},{6,4},{5,7},{7,5},{8,10},{10,8},{9,1... | collective-permute-start | bytes 884744 | tf_op jit(solution)/shard_map/ppermute | solution.py:561
  5.5 29.7 %collective-permute-start = (bf16[192,2304]{1,0:T(8,128)(2,1)S(1)}, bf16[192,2304]{1,0:T(8,128)(2,1)S(1)}, u32[]{:S(2)}, u32[]{:S(2)}) collective-permute-start(bf16[192,2304]{1,0:T(8,128)(2,1)S(1)} %copy-done), channel_id=1, source_target_pairs={{0,1},{1,0},{2,3},{3,2},{4,5},{5,4},{6,7},{7,6},{8,9},{9,8},{10,11... | collective-permute-start | bytes 2654216 | tf_op jit(solution)/shard_map/ppermute | solution.py:561
  5.5 16.4 %collective-permute-start.6 = (bf16[256,768]{1,0:T(8,128)(2,1)S(1)}, bf16[256,768]{1,0:T(8,128)(2,1)S(1)}, u32[]{:S(2)}, u32[]{:S(2)}) collective-permute-start(bf16[256,768]{1,0:T(8,128)(2,1)S(1)} %copy-done.1), channel_id=1, source_target_pairs={{0,1},{1,0},{2,3},{3,2},{4,5},{5,4},{6,7},{7,6},{8,9},{9,8},{10,11... | collective-permute-start | bytes 1179656 | tf_op jit(solution)/shard_map/ppermute | solution.py:561
  6.0 14.4 %collective-permute-start.5 = (bf16[256,512]{1,0:T(8,128)(2,1)S(1)}, bf16[256,512]{1,0:T(8,128)(2,1)S(1)}, u32[]{:S(2)}, u32[]{:S(2)}) collective-permute-start(bf16[256,512]{1,0:T(8,128)(2,1)S(1)} %get-tuple-element.30.msg_ref), channel_id=1, source_target_pairs={{0,4},{4,8},{8,12},{1,5},{5,9},{9,13},{2,6},{6,10},{10,14},{3,7},{... | collective-permute-start | bytes 786440 | tf_op jit(solution)/shard_map/ppermute | solution.py:585
  13.2 13.6 %collective-permute-start.8 = (bf16[256,768]{1,0:T(8,128)(2,1)S(1)}, bf16[256,768]{1,0:T(8,128)(2,1)S(1)}, u32[]{:S(2)}, u32[]{:S(2)}) collective-permute-start(bf16[256,768]{1,0:T(8,128)(2,1)S(1)} %collective-permute-done.7.refs_2_), channel_id=1, source_target_pairs={{0,1},{1,0},{2,3},{3,2},{4,5},{5,4},{6,7},{7,6},{8,9},{9,8},{10,11... | collective-permute-start | bytes 1179656 | tf_op jit(solution)/shard_map/ppermute | solution.py:561
  18.7 8.2 %collective-permute-start.2 = (bf16[96,1536]{1,0:T(8,128)(2,1)S(1)}, bf16[96,1536]{1,0:T(8,128)(2,1)S(1)}, u32[]{:S(2)}, u32[]{:S(2)}) collective-permute-start(bf16[96,1536]{1,0:T(8,128)(2,1)S(1)} %collective-permute-done.1.refs_2_), channel_id=1, source_target_pairs={{0,16},{16,0},{1,17},{17,1},{2,18},{18,2},{3,19},{19,3},{4,20},{20... | collective-permute-start | bytes 884744 | tf_op jit(solution)/shard_map/ppermute | solution.py:561
  20.5 11.6 %collective-permute-start.11 = (bf16[192,768]{1,0:T(8,128)(2,1)S(1)}, bf16[192,768]{1,0:T(8,128)(2,1)S(1)}, u32[]{:S(2)}, u32[]{:S(2)}) collective-permute-start(bf16[192,768]{1,0:T(8,128)(2,1)S(1)} %get-tuple-element.46), channel_id=1, source_target_pairs={{0,2},{2,0},{1,3},{3,1},{4,6},{6,4},{5,7},{7,5},{8,10},{10,8},{9,1... | collective-permute-start | bytes 884744 | tf_op jit(solution)/shard_map/ppermute | solution.py:561
  22.0 12.7 %collective-permute-start.15 = (bf16[192,768]{1,0:T(8,128)(2,1)S(1)}, bf16[192,768]{1,0:T(8,128)(2,1)S(1)}, u32[]{:S(2)}, u32[]{:S(2)}) collective-permute-start(bf16[192,768]{1,0:T(8,128)(2,1)S(1)} %copy-done.2), channel_id=1, source_target_pairs={{0,2},{2,0},{1,3},{3,1},{4,6},{6,4},{5,7},{7,5},{8,10},{10,8},{9,1... | collective-permute-start | bytes 884744 | tf_op jit(solution)/shard_map/ppermute | solution.py:561
  26.9 7.8 %collective-permute-start.3 = (bf16[96,1536]{1,0:T(8,128)(2,1)S(1)}, bf16[96,1536]{1,0:T(8,128)(2,1)S(1)}, u32[]{:S(2)}, u32[]{:S(2)}) collective-permute-start(bf16[96,1536]{1,0:T(8,128)(2,1)S(1)} %collective-permute-done.1.refs_2_), channel_id=1, source_target_pairs={{0,1},{1,0},{2,3},{3,2},{4,5},{5,4},{6,7},{7,6},{8,9},{9,8},{10,11... | collective-permute-start | bytes 884744 | tf_op jit(solution)/shard_map/ppermute | solution.py:561
  26.9 8.4 %collective-permute-start.4 = (bf16[96,1536]{1,0:T(8,128)(2,1)S(1)}, bf16[96,1536]{1,0:T(8,128)(2,1)S(1)}, u32[]{:S(2)}, u32[]{:S(2)}) collective-permute-start(bf16[96,1536]{1,0:T(8,128)(2,1)S(1)} %collective-permute-done.2.refs_3_), channel_id=1, source_target_pairs={{0,1},{1,0},{2,3},{3,2},{4,5},{5,4},{6,7},{7,6},{8,9},{9,8},{10,11... | collective-permute-start | bytes 884744 | tf_op jit(solution)/shard_map/ppermute | solution.py:561
  29.4 16.8 %copy-start.3 = (s32[1,512]{1,0:T(1,128)S(1)}, s32[1,512]{1,0:T(1,128)}, u32[]{:S(2)}) copy-start(s32[1,512]{1,0:T(1,128)} %param.14) | copy-start | bytes 6148
  32.1 12.6 %collective-permute-start.10 = (bf16[136,768]{1,0:T(8,128)(2,1)S(1)}, bf16[136,768]{1,0:T(8,128)(2,1)S(1)}, u32[]{:S(2)}, u32[]{:S(2)}) collective-permute-start(bf16[136,768]{1,0:T(8,128)(2,1)S(1)} %back.1.refs_6_.refs_0_), channel_id=1, source_target_pairs={{0,8},{4,12},{8,0},{12,4},{1,9},{5,13},{9,1},{13,5},{2,10},{6,14},... | collective-permute-start | bytes 626696 | tf_op jit(solution)/shard_map/ppermute | solution.py:561
  34.7 13.1 %collective-permute-start.12 = (bf16[192,768]{1,0:T(8,128)(2,1)S(1)}, bf16[192,768]{1,0:T(8,128)(2,1)S(1)}, u32[]{:S(2)}, u32[]{:S(2)}) collective-permute-start(bf16[192,768]{1,0:T(8,128)(2,1)S(1)} %collective-permute-done.11.refs_5_), channel_id=1, source_target_pairs={{0,1},{1,0},{2,3},{3,2},{4,5},{5,4},{6,7},{7,6},{8,9},{9,8},{10,11... | collective-permute-start | bytes 884744 | tf_op jit(solution)/shard_map/ppermute | solution.py:561
  34.7 14.2 %collective-permute-start.14 = (bf16[192,768]{1,0:T(8,128)(2,1)S(1)}, bf16[192,768]{1,0:T(8,128)(2,1)S(1)}, u32[]{:S(2)}, u32[]{:S(2)}) collective-permute-start(bf16[192,768]{1,0:T(8,128)(2,1)S(1)} %copy-done.2), channel_id=1, source_target_pairs={{0,1},{1,0},{2,3},{3,2},{4,5},{5,4},{6,7},{7,6},{8,9},{9,8},{10,11... | collective-permute-start | bytes 884744 | tf_op jit(solution)/shard_map/ppermute | solution.py:561
  35.2 13.7 %collective-permute-start.16 = (bf16[192,768]{1,0:T(8,128)(2,1)S(1)}, bf16[192,768]{1,0:T(8,128)(2,1)S(1)}, u32[]{:S(2)}, u32[]{:S(2)}) collective-permute-start(bf16[192,768]{1,0:T(8,128)(2,1)S(1)} %collective-permute-done.15.refs_3_), channel_id=1, source_target_pairs={{0,1},{1,0},{2,3},{3,2},{4,5},{5,4},{6,7},{7,6},{8,9},{9,8},{10,11... | collective-permute-start | bytes 884744 | tf_op jit(solution)/shard_map/ppermute | solution.py:561
  35.3 10.9 %collective-permute-start.9 = (bf16[136,768]{1,0:T(8,128)(2,1)S(1)}, bf16[136,768]{1,0:T(8,128)(2,1)S(1)}, u32[]{:S(2)}, u32[]{:S(2)}) collective-permute-start(bf16[136,768]{1,0:T(8,128)(2,1)S(1)} %back.1.refs_6_.refs_0_), channel_id=1, source_target_pairs={{0,4},{4,0},{8,12},{12,8},{1,5},{5,1},{9,13},{13,9},{2,6},{6,2},{1... | collective-permute-start | bytes 626696 | tf_op jit(solution)/shard_map/ppermute | solution.py:561
  44.7 6.2 %collective-permute-start.13 = (bf16[136,768]{1,0:T(8,128)(2,1)S(1)}, bf16[136,768]{1,0:T(8,128)(2,1)S(1)}, u32[]{:S(2)}, u32[]{:S(2)}) collective-permute-start(bf16[136,768]{1,0:T(8,128)(2,1)S(1)} %collective-permute-done.10.refs_2_), channel_id=1, source_target_pairs={{0,4},{4,0},{8,12},{12,8},{1,5},{5,1},{9,13},{13,9},{2,6},{6,2},{1... | collective-permute-start | bytes 626696 | tf_op jit(solution)/shard_map/ppermute | solution.py:561

commit v5 on v4

--- a/solution.py
+++ b/solution.py
@@ -209,10 +209,21 @@
         base = pl.multiple_of(block_of(True, 3) * 128, 128)
         total += dot(patch[pl.ds(base, 128), :], refs[0][...], 0, 0)
     count, width = total.shape
-    out_ref[:count, :] = total.astype(BF)
-    tail = jnp.broadcast_to(active_ref[...].astype(F32), (EXTRA, count))
-    tail = jnp.concatenate([tail, jnp.zeros((EXTRA, width - count), F32)], axis=1)
-    out_ref[count:, :] = tail.astype(BF)
+    total = total.astype(BF)
+    for start in range(0, width, count):
+        out_ref[start : start + count, :] = total[:, start : start + count]
+    out_ref[width:, :] = jnp.broadcast_to(active_ref[...].astype(F32), (EXTRA, count)).astype(BF)
+
+
+def tokens_of(ref):
+    count = ref.shape[1]
+    return jnp.concatenate(
+        [ref[start : start + count, :] for start in range(0, ref.shape[0] - EXTRA, count)], axis=1
+    )
+
+
+def flags_of(ref):
+    return ref[ref.shape[0] - EXTRA :, :]
 
 
 def normal(tokens):
@@ -281,7 +292,7 @@
         down = jnp.sum(jnp.where(square, across, 0.0), axis=1, keepdims=True)
         perm_ref[slot * count : (slot + 1) * count, :] = one_hot(labels == down)
     for slot, ref in enumerate(chunk_refs):
-        normed[slot * count : (slot + 1) * count, :] = normal(ref[:count, :])
+        normed[slot * count : (slot + 1) * count, :] = normal(tokens_of(ref))
     for copy in copies:
         copy.wait()
     lift(joined, normed, keys, values)
@@ -294,7 +305,7 @@
     count = token_ref.shape[0]
     copies = collect(weight_rows(query_refs), query, sems)
     for slot, ref in enumerate(chunk_refs[early:]):
-        normed1[slot * count : (slot + 1) * count, :] = normal(ref[:count, :])
+        normed1[slot * count : (slot + 1) * count, :] = normal(tokens_of(ref))
     lift(joined, normed1, keys1, values1)
     own = own_rows(perm_ref, count, swap)
     near, far = early * count, chunks * count
@@ -324,8 +335,8 @@
     on = token = 0.0
     for slot, ref in enumerate(chunk_refs):
         here = slice((first + slot) * count, (first + slot + 1) * count)
-        on += dot(ref[count:, :count], perm_ref[here, :])
-        token += dot(own[:, here], ref[:count, :])
+        on += dot(flags_of(ref), perm_ref[here, :])
+        token += dot(own[:, here], tokens_of(ref))
     return on, token
 
 
@@ -340,7 +351,7 @@
     count, width = token_ref.shape
     first = perm_ref.shape[0] // count - chunks
     for slot, ref in enumerate(chunk_refs):
-        normed2[slot * count : (slot + 1) * count, :] = normal(ref[:count, :])
+        normed2[slot * count : (slot + 1) * count, :] = normal(tokens_of(ref))
     lift(joined, normed2, keys2, values2)
     own = own_rows(perm_ref, count, swap)
     picked = (picked_ref[...] + dot(own[:, first * count :], normed2[...])).astype(BF)
@@ -476,7 +487,7 @@
     width = parts[2].shape[1]
     return pl.pallas_call(
         functools.partial(back_kernel, channels=channels, middle=middle),
-        out_shape=array((count + EXTRA, width)),
+        out_shape=array((width + EXTRA, count)),
         in_specs=[vmem()] * (4 + len(parts)),
         out_specs=vmem(),
         scratch_shapes=[
@@ -491,7 +502,7 @@
 
 def prepare(order, weights, chunks, swap):
     shards, count = order.shape
-    width = chunks[0].shape[1]
+    width = chunks[0].shape[0] - EXTRA
     size, near = shards * count, len(chunks) * count
     return pl.pallas_call(
         functools.partial(prepare_kernel, pieces=len(weights), chunks=len(chunks), swap=swap),
@@ -508,7 +519,7 @@
     joined, normed, _, _, perm = ready
     width = joined.shape[0]
     size = perm.shape[0]
-    count = chunks[0].shape[0] - EXTRA
+    count = chunks[0].shape[1]
     far = (len(chunks) - early) * count
     pieces = len(weights)
     return pl.pallas_call(
@@ -595,7 +606,7 @@
         chunks.append(exchanged(chunks[2], "seq", 1))
     else:
         everyone = lax.all_gather(tokens, "seq", axis=0, tiled=True)
-        each = count + EXTRA
+        each = everyone.shape[0] // shards
         chunks = [everyone[i * each : (i + 1) * each] for i in range(shards)]
     if paired:
         project_beside = exchanged(project_weight, "section", 1)

time: 55.5 us -> 54.8 us (0.987)
  waiting for transfers between devices: 23.8 us -> 23.1 us
    ppermute x16, waiting for transfers between devices: 23.8 us -> 23.1 us  [exchanged(): return lax.ppermute(value, axis, [(i, i ^ flip) for i in range(count)])]
  transfers between devices with their start and end apart: 17 -> 17, of which waited for: 6 -> 6; matrix products, arithmetic and copies ran while one was open for 0% -> 0% of each run, Pallas kernels for 17% -> 18%
where the time goes in v5:
time: 54.8 us; the launch traced here: 54.6 us
  waiting for transfers between devices  23.1 us (42%)
  starting transfers between devices  17.3 us (32%)
  Pallas kernels  14.1 us (26%)
    ppermute x16, waiting for transfers between devices, exchanged(): return lax.ppermute(value, axis, [(i, i ^ flip) for i in range(count)])  23.1 us
    ppermute x16, starting transfers between devices, exchanged(): return lax.ppermute(value, axis, [(i, i ^ flip) for i in range(count)])  13.4 us
    pallas_call x1, Pallas kernels, finish(): pl.pallas_call(functools.partial(finish_kernel, pieces=pieces, chunks=len...  4.45 us
    ppermute x1, starting transfers between devices, layer(): got = lax.ppermute(msg, 'seq', [(i, i + 1) for i in range(shards - 1)])  3.9 us
    pallas_call x1, Pallas kernels, front(): pl.pallas_call(functools.partial(front_kernel, wires=wires, channels=chan...  2.27 us
    pallas_call x1, Pallas kernels, central(): pl.pallas_call(functools.partial(central_kernel, wires=wires, channels=ch...  2.05 us
    pallas_call x1, Pallas kernels, prepare(): pl.pallas_call(functools.partial(prepare_kernel, pieces=len(weights), chu...  1.53 us
    pallas_call x1, Pallas kernels, back(): pl.pallas_call(functools.partial(back_kernel, channels=channels, middle=m...  1.32 us
  transfers between devices with their start and end apart: 17, of which 6 were waited for; matrix products, arithmetic and copies ran while one was open for 0% of the time, Pallas kernels for 18%

profile of v5, /device:TPU:0, one launch (start us, length us, event | category | flops | bytes accessed | tf_op | source)
XLA Modules:
  0.0 54.6 jit_solution(10244681357509114356)
XLA Ops:
  0.0 3.0 %collective-permute-start.7 = (bf16[256,768]{1,0:T(8,128)(2,1)}, bf16[256,768]{1,0:T(8,128)(2,1)S(1)}, u32[]{:S(2)}, u32[]{:S(2)}) collective-permute-start(bf16[256,768]{1,0:T(8,128)(2,1)} %refs_0_.4), channel_id=1, source_target_pairs={{0,2},{2,0},{1,3},{3,1},{4,6},{6,4},{5,7},{7,5},{8,10},{10,8},{9,1... | collective-permute-start | bytes 1179656 | tf_op jit(solution)/shard_map/ppermute | solution.py:572
  3.0 2.3 %front.1 = (bf16[256,512]{1,0:T(8,128)(2,1)S(1)}, bf16[512,1024]{1,0:T(8,128)(2,1)S(1)}, bf16[576,128]{1,0:T(8,128)(2,1)S(1)}, bf16[1152,256]{1,0:T(8,128)(2,1)S...) custom-call(bf16[512,1024]{1,0:T(8,128)(2,1)} %bitcast.6, bf16[576,128]{1,0:T(8,128)(2,1)} %bitcast.8, ...), custom_call_target="tpu_custom_call" | custom-call | tf_op jit(solution)/shard_map/front/pallas_call | solution.py:420
  5.5 0.5 collective-permute-start.6
  6.0 3.9 %collective-permute-start.5 = (bf16[256,512]{1,0:T(8,128)(2,1)S(1)}, bf16[256,512]{1,0:T(8,128)(2,1)S(1)}, u32[]{:S(2)}, u32[]{:S(2)}) collective-permute-start(bf16[256,512]{1,0:T(8,128)(2,1)S(1)} %get-tuple-element.30.msg_ref), channel_id=1, source_target_pairs={{0,4},{4,8},{8,12},{1,5},{5,9},{9,13},{2,6},{6,10},{10,14},{3,7},{... | collective-permute-start | bytes 786440 | tf_op jit(solution)/shard_map/ppermute | solution.py:596
  9.9 3.3 %collective-permute-done.7.refs_2_ = bf16[256,768]{1,0:T(8,128)(2,1)S(1)} collective-permute-done((bf16[256,768]{1,0:T(8,128)(2,1)}, bf16[256,768]{1,0:T(8,128)(2,1)S(1)}, u32[]{:S(2)}, u32[]{:S(2)}) %collective-permute-start.7) | collective-permute-done | bytes 393248 | tf_op jit(solution)/shard_map/ppermute | solution.py:572
  13.2 5.5 %collective-permute-done.1.refs_2_ = bf16[96,1536]{1,0:T(8,128)(2,1)S(1)} collective-permute-done((bf16[96,1536]{1,0:T(8,128)(2,1)S(1)}, bf16[96,1536]{1,0:T(8,128)(2,1)S(1)}, u32[]{:S(2)}, u32[]{:S(2)}) %collective-permute-start.1) | collective-permute-done | bytes 294944 | tf_op jit(solution)/shard_map/ppermute | solution.py:572
  18.7 1.8 %collective-permute-start.2 = (bf16[96,1536]{1,0:T(8,128)(2,1)S(1)}, bf16[96,1536]{1,0:T(8,128)(2,1)S(1)}, u32[]{:S(2)}, u32[]{:S(2)}) collective-permute-start(bf16[96,1536]{1,0:T(8,128)(2,1)S(1)} %collective-permute-done.1.refs_2_), channel_id=1, source_target_pairs={{0,16},{16,0},{1,17},{17,1},{2,18},{18,2},{3,19},{19,3},{4,20},{20... | collective-permute-start | bytes 884744 | tf_op jit(solution)/shard_map/ppermute | solution.py:572
  20.5 1.5 %collective-permute-start.11 = (bf16[192,768]{1,0:T(8,128)(2,1)S(1)}, bf16[192,768]{1,0:T(8,128)(2,1)S(1)}, u32[]{:S(2)}, u32[]{:S(2)}) collective-permute-start(bf16[192,768]{1,0:T(8,128)(2,1)S(1)} %get-tuple-element.46), channel_id=1, source_target_pairs={{0,2},{2,0},{1,3},{3,1},{4,6},{6,4},{5,7},{7,5},{8,10},{10,8},{9,1... | collective-permute-start | bytes 884744 | tf_op jit(solution)/shard_map/ppermute | solution.py:572
  22.0 0.5 collective-permute-start.15
  22.5 4.4 %collective-permute-done.2.refs_3_ = bf16[96,1536]{1,0:T(8,128)(2,1)S(1)} collective-permute-done((bf16[96,1536]{1,0:T(8,128)(2,1)S(1)}, bf16[96,1536]{1,0:T(8,128)(2,1)S(1)}, u32[]{:S(2)}, u32[]{:S(2)}) %collective-permute-start.2) | collective-permute-done | bytes 294944 | tf_op jit(solution)/shard_map/ppermute | solution.py:572
  26.9 0.5 collective-permute-start.4
  27.4 2.0 %central.1 = (f32[128,512]{1,0:T(8,128)S(1)}, f32[256,256]{1,0:T(8,128)S(1)}, bf16[512,128]{1,0:T(8,128)(2,1)S(1)}) custom-call(bf16[256,512]{1,0:T(8,128)(2,1)S(1)} %get-tuple-element.30.msg_ref, bf16[512,1024]{1,0:T(8,128)(2,1)S(1)} %get-tuple-element.33.x_ref, bf16[576,128]{1,0:T(8,128)(2,1)S(1)} %get-tuple-element.31.k1_ref, ...), custom_call_target="tpu_custom_call" | custom-call | tf_op jit(solution)/shard_map/central/pallas_call | solution.py:440
  29.4 0.8 %mix.1 = (f32[128,768]{1,0:T(8,128)S(1)}, bf16[512,768]{1,0:T(8,128)(2,1)S(1)}) custom-call(bf16[512,128]{1,0:T(8,128)(2,1)S(1)} %get-tuple-element.36.patch, bf16[256,768]{1,0:T(8,128)(2,1)S(1)} %copy-done.1, bf16[256,768]{1,0:T(8,128)(2,1)S(1)} %collective-permute-done.6.refs_1_, bf16[256,768]{1,0:T(8,128)(2,1)S(1)} %collective-permute-done.7.refs_2_), custom_call_target="tpu_custom_call" | custom-call | tf_op jit(solution)/shard_map/mix/pallas_call | solution.py:460
  30.7 1.3 %back.1.refs_6_.refs_0_ = bf16[776,128]{1,0:T(8,128)(2,1)S(1)} custom-call(bf16[256,512]{1,0:T(8,128)(2,1)S(1)} %collective-permute-done.5.got_ref, bf16[576,128]{1,0:T(8,128)(2,1)S(1)} %get-tuple-element.31.k1_ref, bf16[1152,256]{1,0:T(8,128)(2,1)S(1)} %get-tuple-element.32.k2_ref, s32[1,128]{1,0:T(1,128)S(1)} %copy-done.4, ...), custom_call_target="tpu_custom_call" | custom-call | tf_op jit(solution)/shard_map/back/pallas_call | solution.py:488
  32.1 2.6 %collective-permute-start.10 = (bf16[776,128]{1,0:T(8,128)(2,1)S(1)}, bf16[776,128]{1,0:T(8,128)(2,1)S(1)}, u32[]{:S(2)}, u32[]{:S(2)}) collective-permute-start(bf16[776,128]{1,0:T(8,128)(2,1)S(1)} %back.1.refs_6_.refs_0_), channel_id=1, source_target_pairs={{0,8},{4,12},{8,0},{12,4},{1,9},{5,13},{9,1},{13,5},{2,10},{6,14},... | collective-permute-start | bytes 595976 | tf_op jit(solution)/shard_map/ppermute | solution.py:572
  34.7 0.5 collective-permute-start.14
  35.3 1.6 %collective-permute-start.9 = (bf16[776,128]{1,0:T(8,128)(2,1)S(1)}, bf16[776,128]{1,0:T(8,128)(2,1)S(1)}, u32[]{:S(2)}, u32[]{:S(2)}) collective-permute-start(bf16[776,128]{1,0:T(8,128)(2,1)S(1)} %back.1.refs_6_.refs_0_), channel_id=1, source_target_pairs={{0,4},{4,0},{8,12},{12,8},{1,5},{5,1},{9,13},{13,9},{2,6},{6,2},{1... | collective-permute-start | bytes 595976 | tf_op jit(solution)/shard_map/ppermute | solution.py:572
  36.9 7.4 %collective-permute-done.10.refs_2_ = bf16[776,128]{1,0:T(8,128)(2,1)S(1)} collective-permute-done((bf16[776,128]{1,0:T(8,128)(2,1)S(1)}, bf16[776,128]{1,0:T(8,128)(2,1)S(1)}, u32[]{:S(2)}, u32[]{:S(2)}) %collective-permute-start.10) | collective-permute-done | bytes 198688 | tf_op jit(solution)/shard_map/ppermute | solution.py:572
  44.2 0.6 %collective-permute-start.13 = (bf16[776,128]{1,0:T(8,128)(2,1)S(1)}, bf16[776,128]{1,0:T(8,128)(2,1)S(1)}, u32[]{:S(2)}, u32[]{:S(2)}) collective-permute-start(bf16[776,128]{1,0:T(8,128)(2,1)S(1)} %collective-permute-done.10.refs_2_), channel_id=1, source_target_pairs={{0,4},{4,0},{8,12},{12,8},{1,5},{5,1},{9,13},{13,9},{2,6},{6,2},{1... | collective-permute-start | bytes 595976 | tf_op jit(solution)/shard_map/ppermute | solution.py:572
  44.8 0.9 %collective-permute-done.9.refs_7_.refs_1_ = bf16[776,128]{1,0:T(8,128)(2,1)S(1)} collective-permute-done((bf16[776,128]{1,0:T(8,128)(2,1)S(1)}, bf16[776,128]{1,0:T(8,128)(2,1)S(1)}, u32[]{:S(2)}, u32[]{:S(2)}) %collective-permute-start.9) | collective-permute-done | bytes 198688 | tf_op jit(solution)/shard_map/ppermute | solution.py:572
  45.8 1.5 %prepare.1 = (bf16[768,1536]{1,0:T(8,128)(2,1)S(1)}, bf16[256,768]{1,0:T(8,128)(2,1)S(1)}, bf16[256,768]{1,0:T(8,128)(2,1)S(1)}, bf16[256,768]{1,0:T(8,128)(2,1)S(1)}, bf16[512,512]{1,0:T(8,128)(2,1)S(1)}) custom-call(s32[4,128]{1,0:T(4,128)S(1)} %bitcast.5, bf16[192,2304]{1,0:T(8,128)(2,1)S(1)} %copy-done, ...), custom_call_target="tpu_custom_call" | custom-call | tf_op jit(solution)/shard_map/prepare/pallas_call | solution.py:507
  47.3 1.2 %extend.1 = (bf16[768,768]{1,0:T(8,128)(2,1)S(1)}, bf16[128,768]{1,0:T(8,128)(2,1)S(1)}, bf16[128,768]{1,0:T(8,128)(2,1)S(1)}, f32[128,768]{1,0:T(8,128)S(1)}, f...) custom-call(bf16[512,512]{1,0:T(8,128)(2,1)S(1)} %get-tuple-element.41.perm_ref, ...), custom_call_target="tpu_custom_call" | custom-call | tf_op jit(solution)/shard_map/extend/pallas_call | solution.py:525
  48.5 1.7 %collective-permute-done.13.refs_0_ = bf16[776,128]{1,0:T(8,128)(2,1)S(1)} collective-permute-done((bf16[776,128]{1,0:T(8,128)(2,1)S(1)}, bf16[776,128]{1,0:T(8,128)(2,1)S(1)}, u32[]{:S(2)}, u32[]{:S(2)}) %collective-permute-start.13) | collective-permute-done | bytes 198688 | tf_op jit(solution)/shard_map/ppermute | solution.py:572
  50.2 4.5 %finish.1 = bf16[128,768]{1,0:T(8,128)(2,1)} custom-call(bf16[512,512]{1,0:T(8,128)(2,1)S(1)} %get-tuple-element.41.perm_ref, bf16[768,1536]{1,0:T(8,128)(2,1)S(1)} %get-tuple-element.42.joined, bf16[256,768]{1,0:T(8,128)(2,1)S(1)} %get-tuple-element.43.keys0, bf16[256,768]{1,0:T(8,128)(2,1)S(1)} %get-tuple-element.44.values0, ...), custom_call_target="tpu_custom_call" | custom-call | tf_op jit(solution)/shard_map/finish/pallas_call | solution.py:551
  (28 shorter events, 0.8 us)
Async XLA Ops:
  0.0 5.5 %copy-start.1 = (bf16[256,768]{1,0:T(8,128)(2,1)S(1)}, bf16[256,768]{1,0:T(8,128)(2,1)}, u32[]{:S(2)}) copy-start(bf16[256,768]{1,0:T(8,128)(2,1)} %refs_0_.4) | copy-start | bytes 1179652
  0.0 5.5 %copy-start = (bf16[192,2304]{1,0:T(8,128)(2,1)S(1)}, bf16[192,2304]{1,0:T(8,128)(2,1)}, u32[]{:S(2)}) copy-start(bf16[192,2304]{1,0:T(8,128)(2,1)} %refs_3_.1) | copy-start | bytes 2654212
  0.0 22.0 %copy-start.2 = (bf16[192,768]{1,0:T(8,128)(2,1)S(1)}, bf16[192,768]{1,0:T(8,128)(2,1)}, u32[]{:S(2)}) copy-start(bf16[192,768]{1,0:T(8,128)(2,1)} %refs_1_.1) | copy-start | bytes 884740
  0.0 13.2 %collective-permute-start.7 = (bf16[256,768]{1,0:T(8,128)(2,1)}, bf16[256,768]{1,0:T(8,128)(2,1)S(1)}, u32[]{:S(2)}, u32[]{:S(2)}) collective-permute-start(bf16[256,768]{1,0:T(8,128)(2,1)} %refs_0_.4), channel_id=1, source_target_pairs={{0,2},{2,0},{1,3},{3,1},{4,6},{6,4},{5,7},{7,5},{8,10},{10,8},{9,1... | collective-permute-start | bytes 1179656 | tf_op jit(solution)/shard_map/ppermute | solution.py:572
  5.3 25.4 %copy-start.4 = (s32[1,128]{1,0:T(1,128)S(1)}, s32[1,128]{1,0:T(1,128)}, u32[]{:S(2)}) copy-start(s32[1,128]{1,0:T(1,128)} %active_ref.1) | copy-start | bytes 1540
  5.3 13.4 %collective-permute-start.1 = (bf16[96,1536]{1,0:T(8,128)(2,1)S(1)}, bf16[96,1536]{1,0:T(8,128)(2,1)S(1)}, u32[]{:S(2)}, u32[]{:S(2)}) collective-permute-start(bf16[96,1536]{1,0:T(8,128)(2,1)S(1)} %get-tuple-element.29), channel_id=1, source_target_pairs={{0,2},{2,0},{1,3},{3,1},{4,6},{6,4},{5,7},{7,5},{8,10},{10,8},{9,1... | collective-permute-start | bytes 884744 | tf_op jit(solution)/shard_map/ppermute | solution.py:572
  5.5 29.7 %collective-permute-start = (bf16[192,2304]{1,0:T(8,128)(2,1)S(1)}, bf16[192,2304]{1,0:T(8,128)(2,1)S(1)}, u32[]{:S(2)}, u32[]{:S(2)}) collective-permute-start(bf16[192,2304]{1,0:T(8,128)(2,1)S(1)} %copy-done), channel_id=1, source_target_pairs={{0,1},{1,0},{2,3},{3,2},{4,5},{5,4},{6,7},{7,6},{8,9},{9,8},{10,11... | collective-permute-start | bytes 2654216 | tf_op jit(solution)/shard_map/ppermute | solution.py:572
  5.5 16.4 %collective-permute-start.6 = (bf16[256,768]{1,0:T(8,128)(2,1)S(1)}, bf16[256,768]{1,0:T(8,128)(2,1)S(1)}, u32[]{:S(2)}, u32[]{:S(2)}) collective-permute-start(bf16[256,768]{1,0:T(8,128)(2,1)S(1)} %copy-done.1), channel_id=1, source_target_pairs={{0,1},{1,0},{2,3},{3,2},{4,5},{5,4},{6,7},{7,6},{8,9},{9,8},{10,11... | collective-permute-start | bytes 1179656 | tf_op jit(solution)/shard_map/ppermute | solution.py:572
  6.0 14.4 %collective-permute-start.5 = (bf16[256,512]{1,0:T(8,128)(2,1)S(1)}, bf16[256,512]{1,0:T(8,128)(2,1)S(1)}, u32[]{:S(2)}, u32[]{:S(2)}) collective-permute-start(bf16[256,512]{1,0:T(8,128)(2,1)S(1)} %get-tuple-element.30.msg_ref), channel_id=1, source_target_pairs={{0,4},{4,8},{8,12},{1,5},{5,9},{9,13},{2,6},{6,10},{10,14},{3,7},{... | collective-permute-start | bytes 786440 | tf_op jit(solution)/shard_map/ppermute | solution.py:596
  13.2 13.6 %collective-permute-start.8 = (bf16[256,768]{1,0:T(8,128)(2,1)S(1)}, bf16[256,768]{1,0:T(8,128)(2,1)S(1)}, u32[]{:S(2)}, u32[]{:S(2)}) collective-permute-start(bf16[256,768]{1,0:T(8,128)(2,1)S(1)} %collective-permute-done.7.refs_2_), channel_id=1, source_target_pairs={{0,1},{1,0},{2,3},{3,2},{4,5},{5,4},{6,7},{7,6},{8,9},{9,8},{10,11... | collective-permute-start | bytes 1179656 | tf_op jit(solution)/shard_map/ppermute | solution.py:572
  18.7 8.2 %collective-permute-start.2 = (bf16[96,1536]{1,0:T(8,128)(2,1)S(1)}, bf16[96,1536]{1,0:T(8,128)(2,1)S(1)}, u32[]{:S(2)}, u32[]{:S(2)}) collective-permute-start(bf16[96,1536]{1,0:T(8,128)(2,1)S(1)} %collective-permute-done.1.refs_2_), channel_id=1, source_target_pairs={{0,16},{16,0},{1,17},{17,1},{2,18},{18,2},{3,19},{19,3},{4,20},{20... | collective-permute-start | bytes 884744 | tf_op jit(solution)/shard_map/ppermute | solution.py:572
  20.5 11.6 %collective-permute-start.11 = (bf16[192,768]{1,0:T(8,128)(2,1)S(1)}, bf16[192,768]{1,0:T(8,128)(2,1)S(1)}, u32[]{:S(2)}, u32[]{:S(2)}) collective-permute-start(bf16[192,768]{1,0:T(8,128)(2,1)S(1)} %get-tuple-element.46), channel_id=1, source_target_pairs={{0,2},{2,0},{1,3},{3,1},{4,6},{6,4},{5,7},{7,5},{8,10},{10,8},{9,1... | collective-permute-start | bytes 884744 | tf_op jit(solution)/shard_map/ppermute | solution.py:572
  22.0 12.7 %collective-permute-start.15 = (bf16[192,768]{1,0:T(8,128)(2,1)S(1)}, bf16[192,768]{1,0:T(8,128)(2,1)S(1)}, u32[]{:S(2)}, u32[]{:S(2)}) collective-permute-start(bf16[192,768]{1,0:T(8,128)(2,1)S(1)} %copy-done.2), channel_id=1, source_target_pairs={{0,2},{2,0},{1,3},{3,1},{4,6},{6,4},{5,7},{7,5},{8,10},{10,8},{9,1... | collective-permute-start | bytes 884744 | tf_op jit(solution)/shard_map/ppermute | solution.py:572
  26.9 7.8 %collective-permute-start.3 = (bf16[96,1536]{1,0:T(8,128)(2,1)S(1)}, bf16[96,1536]{1,0:T(8,128)(2,1)S(1)}, u32[]{:S(2)}, u32[]{:S(2)}) collective-permute-start(bf16[96,1536]{1,0:T(8,128)(2,1)S(1)} %collective-permute-done.1.refs_2_), channel_id=1, source_target_pairs={{0,1},{1,0},{2,3},{3,2},{4,5},{5,4},{6,7},{7,6},{8,9},{9,8},{10,11... | collective-permute-start | bytes 884744 | tf_op jit(solution)/shard_map/ppermute | solution.py:572
  26.9 8.4 %collective-permute-start.4 = (bf16[96,1536]{1,0:T(8,128)(2,1)S(1)}, bf16[96,1536]{1,0:T(8,128)(2,1)S(1)}, u32[]{:S(2)}, u32[]{:S(2)}) collective-permute-start(bf16[96,1536]{1,0:T(8,128)(2,1)S(1)} %collective-permute-done.2.refs_3_), channel_id=1, source_target_pairs={{0,1},{1,0},{2,3},{3,2},{4,5},{5,4},{6,7},{7,6},{8,9},{9,8},{10,11... | collective-permute-start | bytes 884744 | tf_op jit(solution)/shard_map/ppermute | solution.py:572
  29.4 16.3 %copy-start.3 = (s32[1,512]{1,0:T(1,128)S(1)}, s32[1,512]{1,0:T(1,128)}, u32[]{:S(2)}) copy-start(s32[1,512]{1,0:T(1,128)} %param.14) | copy-start | bytes 6148
  32.1 12.2 %collective-permute-start.10 = (bf16[776,128]{1,0:T(8,128)(2,1)S(1)}, bf16[776,128]{1,0:T(8,128)(2,1)S(1)}, u32[]{:S(2)}, u32[]{:S(2)}) collective-permute-start(bf16[776,128]{1,0:T(8,128)(2,1)S(1)} %back.1.refs_6_.refs_0_), channel_id=1, source_target_pairs={{0,8},{4,12},{8,0},{12,4},{1,9},{5,13},{9,1},{13,5},{2,10},{6,14},... | collective-permute-start | bytes 595976 | tf_op jit(solution)/shard_map/ppermute | solution.py:572
  34.7 12.6 %collective-permute-start.12 = (bf16[192,768]{1,0:T(8,128)(2,1)S(1)}, bf16[192,768]{1,0:T(8,128)(2,1)S(1)}, u32[]{:S(2)}, u32[]{:S(2)}) collective-permute-start(bf16[192,768]{1,0:T(8,128)(2,1)S(1)} %collective-permute-done.11.refs_5_), channel_id=1, source_target_pairs={{0,1},{1,0},{2,3},{3,2},{4,5},{5,4},{6,7},{7,6},{8,9},{9,8},{10,11... | collective-permute-start | bytes 884744 | tf_op jit(solution)/shard_map/ppermute | solution.py:572
  34.7 13.8 %collective-permute-start.14 = (bf16[192,768]{1,0:T(8,128)(2,1)S(1)}, bf16[192,768]{1,0:T(8,128)(2,1)S(1)}, u32[]{:S(2)}, u32[]{:S(2)}) collective-permute-start(bf16[192,768]{1,0:T(8,128)(2,1)S(1)} %copy-done.2), channel_id=1, source_target_pairs={{0,1},{1,0},{2,3},{3,2},{4,5},{5,4},{6,7},{7,6},{8,9},{9,8},{10,11... | collective-permute-start | bytes 884744 | tf_op jit(solution)/shard_map/ppermute | solution.py:572
  35.2 13.3 %collective-permute-start.16 = (bf16[192,768]{1,0:T(8,128)(2,1)S(1)}, bf16[192,768]{1,0:T(8,128)(2,1)S(1)}, u32[]{:S(2)}, u32[]{:S(2)}) collective-permute-start(bf16[192,768]{1,0:T(8,128)(2,1)S(1)} %collective-permute-done.15.refs_3_), channel_id=1, source_target_pairs={{0,1},{1,0},{2,3},{3,2},{4,5},{5,4},{6,7},{7,6},{8,9},{9,8},{10,11... | collective-permute-start | bytes 884744 | tf_op jit(solution)/shard_map/ppermute | solution.py:572
  35.3 10.5 %collective-permute-start.9 = (bf16[776,128]{1,0:T(8,128)(2,1)S(1)}, bf16[776,128]{1,0:T(8,128)(2,1)S(1)}, u32[]{:S(2)}, u32[]{:S(2)}) collective-permute-start(bf16[776,128]{1,0:T(8,128)(2,1)S(1)} %back.1.refs_6_.refs_0_), channel_id=1, source_target_pairs={{0,4},{4,0},{8,12},{12,8},{1,5},{5,1},{9,13},{13,9},{2,6},{6,2},{1... | collective-permute-start | bytes 595976 | tf_op jit(solution)/shard_map/ppermute | solution.py:572
  44.2 5.9 %collective-permute-start.13 = (bf16[776,128]{1,0:T(8,128)(2,1)S(1)}, bf16[776,128]{1,0:T(8,128)(2,1)S(1)}, u32[]{:S(2)}, u32[]{:S(2)}) collective-permute-start(bf16[776,128]{1,0:T(8,128)(2,1)S(1)} %collective-permute-done.10.refs_2_), channel_id=1, source_target_pairs={{0,4},{4,0},{8,12},{12,8},{1,5},{5,1},{9,13},{13,9},{2,6},{6,2},{1... | collective-permute-start | bytes 595976 | tf_op jit(solution)/shard_map/ppermute | solution.py:572

commit v6 on v5

--- a/solution.py
+++ b/solution.py
@@ -237,7 +237,10 @@
     width = joined.shape[0]
     rows = normed[...]
     keys[...] = dot(rows, joined[:, :width]).astype(BF)
-    values[...] = dot(rows, joined[:, width:]).astype(BF)
+    lifted = dot(rows, joined[:, width:]).astype(BF)
+    for start in range(0, width, 128):
+        values[:, 2 * start : 2 * start + 128] = lifted[:, start : start + 128]
+        values[:, 2 * start + 128 : 2 * start + 256] = jnp.ones((rows.shape[0], 128), BF)
 
 
 def collect(sources, target, sems):
@@ -317,6 +320,12 @@
         copy.wait()
 
 
+def gather_kernel(*refs):
+    output, sems = refs[-2:]
+    for copy in collect(weight_rows(refs[:-2]), output, sems):
+        copy.wait()
+
+
 def weight_rows(refs):
     sources = []
     for piece, ref in enumerate(refs):
@@ -341,13 +350,11 @@
 
 
 def finish_kernel(
-    perm_ref, joined, keys0, values0, keys1, values1, query, token_ref, picked_ref, on_ref, *refs,
-    pieces, chunks, swap
+    perm_ref, joined, keys0, values0, keys1, values1, query, output, token_ref, picked_ref, on_ref,
+    *refs, chunks, swap
 ):
     chunk_refs = refs[:chunks]
-    output_refs = refs[chunks : chunks + pieces]
-    out_ref, output, normed2, keys2, values2, cap, mixed, sems = refs[chunks + pieces :]
-    copies = collect(weight_rows(output_refs), output, sems)
+    out_ref, normed2, keys2, values2, cap, mixed = refs[chunks:]
     count, width = token_ref.shape
     first = perm_ref.shape[0] // count - chunks
     for slot, ref in enumerate(chunk_refs):
@@ -371,20 +378,18 @@
         both = [jnp.where(low, part_query, zero), jnp.where(low, zero, part_query)]
         both = jnp.concatenate(both, axis=0)
         scores = jnp.concatenate([dot(both, keys[:, here], 1, 1) for keys, _ in groups], axis=1)
-        weights, scale = [], []
+        weights = []
         for half in range(2):
             score = jnp.minimum(scores[half * count : (half + 1) * count], cap[...])
-            weight = jnp.exp(score - jnp.max(score, axis=-1, keepdims=True))
-            scale.append(1.0 / jnp.sum(weight, axis=-1, keepdims=True))
-            weights.append(weight.astype(BF))
+            weights.append(jnp.exp(score - jnp.max(score, axis=-1, keepdims=True)).astype(BF))
         weights = jnp.concatenate(weights, axis=0)
         part, start = 0.0, 0
+        there = slice(2 * pair * 2 * head, 2 * (pair + 1) * 2 * head)
         for keys, values in groups:
-            part += dot(weights[:, start : start + keys.shape[0]], values[:, here])
+            part += dot(weights[:, start : start + keys.shape[0]], values[:, there])
             start += keys.shape[0]
-        mixed[:, here] = jnp.where(low, part[:count] * scale[0], part[count:] * scale[1]).astype(BF)
-    for copy in copies:
-        copy.wait()
+        part = part[:, : 2 * head] / part[:, 2 * head :]
+        mixed[:, here] = jnp.where(low, part[:count], part[count:]).astype(BF)
     out_ref[...] = (token + dot(mixed[...], output[...])).astype(BF)
 
 
@@ -506,7 +511,7 @@
     size, near = shards * count, len(chunks) * count
     return pl.pallas_call(
         functools.partial(prepare_kernel, pieces=len(weights), chunks=len(chunks), swap=swap),
-        out_shape=(array((width, 2 * width)),) + (array((near, width)),) * 3 + (array((size, size)),),
+        out_shape=(array((width, 2 * width)),) + (array((near, width)),) * 2 + (array((near, 2 * width)), array((size, size))),
         in_specs=[vmem()] + [fixed()] + [hbm()] * (len(weights) - 1) + [vmem()] * len(chunks),
         out_specs=[vmem()] * 5,
         scratch_shapes=[pltpu.SemaphoreType.DMA((len(weights),))],
@@ -527,7 +532,7 @@
         out_shape=(
             array((width, width)),
             array((far, width)),
-            array((far, width)),
+            array((far, 2 * width)),
             array((count, width), F32),
             array((count, width), F32),
             array((EXTRA, size), F32),
@@ -540,31 +545,41 @@
     )(perm, joined, normed, *chunks, *weights)
 
 
-def finish(ready, extra, chunks, weights, swap):
+def gather(weights):
+    width = weights[0].shape[1]
+    return pl.pallas_call(
+        gather_kernel,
+        out_shape=array((width, width)),
+        in_specs=[fixed()] + [hbm()] * (len(weights) - 1),
+        out_specs=vmem(),
+        scratch_shapes=[pltpu.SemaphoreType.DMA((len(weights),))],
+        compiler_params=params(4),
+        name="gather",
+    )(*weights)
+
+
+def finish(ready, extra, output, chunks, swap):
     joined, _, keys, values, perm = ready
     query, keys1, values1, token, picked, on = extra
     width = joined.shape[0]
     size = perm.shape[0]
     count = token.shape[0]
     far = len(chunks) * count
-    pieces = len(weights)
-    return pl.pallas_call(
-        functools.partial(finish_kernel, pieces=pieces, chunks=len(chunks), swap=swap),
+    return pl.pallas_call(
+        functools.partial(finish_kernel, chunks=len(chunks), swap=swap),
         out_shape=array((count, width)),
-        in_specs=[vmem()] * (10 + len(chunks)) + [fixed()] + [hbm()] * (pieces - 1),
+        in_specs=[vmem()] * (11 + len(chunks)),
         out_specs=vmem(),
         scratch_shapes=[
-            pltpu.VMEM((width, width), BF),
             pltpu.VMEM((far, width), BF),
             pltpu.VMEM((far, width), BF),
-            pltpu.VMEM((far, width), BF),
+            pltpu.VMEM((far, 2 * width), BF),
             pltpu.VMEM((count, size), F32),
             pltpu.VMEM((count, width), BF),
-            pltpu.SemaphoreType.DMA((pieces,)),
         ],
         compiler_params=params(8 + size // 64),
         name="finish",
-    )(perm, joined, keys, values, keys1, values1, query, token, picked, on, *chunks, *weights)
+    )(perm, joined, keys, values, keys1, values1, query, output, token, picked, on, *chunks)
 
 
 def exchanged(value, axis, flip):
@@ -629,7 +644,8 @@
     early, later = shards // 2, shards // 2 + shards // 4
     ready = prepare(order, kv_weights, chunks[:early], swap)
     extra = extend(ready, chunks[:later], query_weights, early, swap)
-    result = finish(ready, extra, chunks[later:], output_weights, swap)
+    output = gather(output_weights)
+    result = finish(ready, extra, output, chunks[later:], swap)
     return result[None]
 
 

time: 54.8 us -> 60.4 us (1.10)
  waiting for transfers between devices: 23.1 us -> 28.6 us
    ppermute x16, waiting for transfers between devices: 23.1 us -> 27.3 us  [exchanged(): return lax.ppermute(value, axis, [(i, i ^ flip) for i in range(count)])]
    ppermute x1, waiting for transfers between devices: 0.01 us -> 1.29 us  [layer(): got = lax.ppermute(msg, 'seq', [(i, i + 1) for i in range(shards - 1)])]
    pallas_call x1 -> x2, Pallas kernels: 4.45 us -> 4.07 us  [the longest x1 3.79 us: finish(): pl.pallas_call(functools.partial(finish_kernel, chunks=len(chunks), swap=...]
  transfers between devices with their start and end apart: 17 -> 17, of which waited for: 6 -> 8; matrix products, arithmetic and copies ran while one was open for 0% -> 0% of each run, Pallas kernels for 18% -> 17%
where the time goes in v6:
time: 60.4 us; the launch traced here: 60.3 us
  waiting for transfers between devices  28.6 us (47%)
  starting transfers between devices  17.7 us (29%)
  Pallas kernels  13.8 us (23%)
    ppermute x16, waiting for transfers between devices, exchanged(): return lax.ppermute(value, axis, [(i, i ^ flip) for i in range(count)])  27.3 us
    ppermute x16, starting transfers between devices, exchanged(): return lax.ppermute(value, axis, [(i, i ^ flip) for i in range(count)])  13.7 us
    ppermute x1, starting transfers between devices, layer(): got = lax.ppermute(msg, 'seq', [(i, i + 1) for i in range(shards - 1)])  4 us
    pallas_call x1, Pallas kernels, finish(): pl.pallas_call(functools.partial(finish_kernel, chunks=len(chunks), swap=...  3.79 us
    pallas_call x1, Pallas kernels, front(): pl.pallas_call(functools.partial(front_kernel, wires=wires, channels=chan...  2.39 us
    pallas_call x1, Pallas kernels, central(): pl.pallas_call(functools.partial(central_kernel, wires=wires, channels=ch...  2.03 us
    pallas_call x1, Pallas kernels, prepare(): pl.pallas_call(functools.partial(prepare_kernel, pieces=len(weights), chu...  1.54 us
    pallas_call x1, Pallas kernels, back(): pl.pallas_call(functools.partial(back_kernel, channels=channels, middle=m...  1.32 us
  transfers between devices with their start and end apart: 17, of which 8 were waited for; matrix products, arithmetic and copies ran while one was open for 0% of the time, Pallas kernels for 17%

profile of v6, /device:TPU:0, one launch (start us, length us, event | category | flops | bytes accessed | tf_op | source)
XLA Modules:
  0.0 60.3 jit_solution(16000901501494328717)
XLA Ops:
  0.0 3.0 %collective-permute-start.7 = (bf16[256,768]{1,0:T(8,128)(2,1)}, bf16[256,768]{1,0:T(8,128)(2,1)S(1)}, u32[]{:S(2)}, u32[]{:S(2)}) collective-permute-start(bf16[256,768]{1,0:T(8,128)(2,1)} %refs_0_.5), channel_id=1, source_target_pairs={{0,2},{2,0},{1,3},{3,1},{4,6},{6,4},{5,7},{7,5},{8,10},{10,8},{9,1... | collective-permute-start | bytes 1179656 | tf_op jit(solution)/shard_map/ppermute | solution.py:587
  3.0 2.4 %front.1 = (bf16[256,512]{1,0:T(8,128)(2,1)S(1)}, bf16[512,1024]{1,0:T(8,128)(2,1)S(1)}, bf16[576,128]{1,0:T(8,128)(2,1)S(1)}, bf16[1152,256]{1,0:T(8,128)(2,1)S...) custom-call(bf16[512,1024]{1,0:T(8,128)(2,1)} %bitcast.6, bf16[576,128]{1,0:T(8,128)(2,1)} %bitcast.8, ...), custom_call_target="tpu_custom_call" | custom-call | tf_op jit(solution)/shard_map/front/pallas_call | solution.py:425
  5.5 4.0 %collective-permute-start.5 = (bf16[256,512]{1,0:T(8,128)(2,1)S(1)}, bf16[256,512]{1,0:T(8,128)(2,1)S(1)}, u32[]{:S(2)}, u32[]{:S(2)}) collective-permute-start(bf16[256,512]{1,0:T(8,128)(2,1)S(1)} %get-tuple-element.30.msg_ref), channel_id=1, source_target_pairs={{0,4},{4,8},{8,12},{1,5},{5,9},{9,13},{2,6},{6,10},{10,14},{3,7},{... | collective-permute-start | bytes 786440 | tf_op jit(solution)/shard_map/ppermute | solution.py:611
  9.5 1.6 %collective-permute-start.11 = (bf16[192,768]{1,0:T(8,128)(2,1)S(1)}, bf16[192,768]{1,0:T(8,128)(2,1)S(1)}, u32[]{:S(2)}, u32[]{:S(2)}) collective-permute-start(bf16[192,768]{1,0:T(8,128)(2,1)S(1)} %get-tuple-element.46), channel_id=1, source_target_pairs={{0,2},{2,0},{1,3},{3,1},{4,6},{6,4},{5,7},{7,5},{8,10},{10,8},{9,1... | collective-permute-start | bytes 884744 | tf_op jit(solution)/shard_map/ppermute | solution.py:587
  11.0 2.1 %collective-permute-done.7.refs_2_ = bf16[256,768]{1,0:T(8,128)(2,1)S(1)} collective-permute-done((bf16[256,768]{1,0:T(8,128)(2,1)}, bf16[256,768]{1,0:T(8,128)(2,1)S(1)}, u32[]{:S(2)}, u32[]{:S(2)}) %collective-permute-start.7) | collective-permute-done | bytes 393248 | tf_op jit(solution)/shard_map/ppermute | solution.py:587
  13.1 1.3 %collective-permute-done.5.got_ref = bf16[256,512]{1,0:T(8,128)(2,1)S(1)} collective-permute-done((bf16[256,512]{1,0:T(8,128)(2,1)S(1)}, bf16[256,512]{1,0:T(8,128)(2,1)S(1)}, u32[]{:S(2)}, u32[]{:S(2)}) %collective-permute-start.5) | collective-permute-done | bytes 262176 | tf_op jit(solution)/shard_map/ppermute | solution.py:611
  14.4 1.5 %collective-permute-start.14 = (bf16[192,768]{1,0:T(8,128)(2,1)S(1)}, bf16[192,768]{1,0:T(8,128)(2,1)S(1)}, u32[]{:S(2)}, u32[]{:S(2)}) collective-permute-start(bf16[192,768]{1,0:T(8,128)(2,1)S(1)} %copy-done.2), channel_id=1, source_target_pairs={{0,2},{2,0},{1,3},{3,1},{4,6},{6,4},{5,7},{7,5},{8,10},{10,8},{9,1... | collective-permute-start | bytes 884744 | tf_op jit(solution)/shard_map/ppermute | solution.py:587
  15.9 3.5 %collective-permute-done.1.refs_2_ = bf16[96,1536]{1,0:T(8,128)(2,1)S(1)} collective-permute-done((bf16[96,1536]{1,0:T(8,128)(2,1)S(1)}, bf16[96,1536]{1,0:T(8,128)(2,1)S(1)}, u32[]{:S(2)}, u32[]{:S(2)}) %collective-permute-start.1) | collective-permute-done | bytes 294944 | tf_op jit(solution)/shard_map/ppermute | solution.py:587
  19.5 6.3 %collective-permute-done.11.refs_5_ = bf16[192,768]{1,0:T(8,128)(2,1)S(1)} collective-permute-done((bf16[192,768]{1,0:T(8,128)(2,1)S(1)}, bf16[192,768]{1,0:T(8,128)(2,1)S(1)}, u32[]{:S(2)}, u32[]{:S(2)}) %collective-permute-start.11) | collective-permute-done | bytes 294944 | tf_op jit(solution)/shard_map/ppermute | solution.py:587
  25.8 5.5 %collective-permute-done.14.refs_2_ = bf16[192,768]{1,0:T(8,128)(2,1)S(1)} collective-permute-done((bf16[192,768]{1,0:T(8,128)(2,1)S(1)}, bf16[192,768]{1,0:T(8,128)(2,1)S(1)}, u32[]{:S(2)}, u32[]{:S(2)}) %collective-permute-start.14) | collective-permute-done | bytes 294944 | tf_op jit(solution)/shard_map/ppermute | solution.py:587
  31.2 1.8 %collective-permute-start.2 = (bf16[96,1536]{1,0:T(8,128)(2,1)S(1)}, bf16[96,1536]{1,0:T(8,128)(2,1)S(1)}, u32[]{:S(2)}, u32[]{:S(2)}) collective-permute-start(bf16[96,1536]{1,0:T(8,128)(2,1)S(1)} %collective-permute-done.1.refs_2_), channel_id=1, source_target_pairs={{0,16},{16,0},{1,17},{17,1},{2,18},{18,2},{3,19},{19,3},{4,20},{20... | collective-permute-start | bytes 884744 | tf_op jit(solution)/shard_map/ppermute | solution.py:587
  33.0 0.5 collective-permute-start.15
  33.5 2.0 %central.1 = (f32[128,512]{1,0:T(8,128)S(1)}, f32[256,256]{1,0:T(8,128)S(1)}, bf16[512,128]{1,0:T(8,128)(2,1)S(1)}) custom-call(bf16[256,512]{1,0:T(8,128)(2,1)S(1)} %get-tuple-element.30.msg_ref, bf16[512,1024]{1,0:T(8,128)(2,1)S(1)} %get-tuple-element.33.x_ref, bf16[576,128]{1,0:T(8,128)(2,1)S(1)} %get-tuple-element.31.k1_ref, ...), custom_call_target="tpu_custom_call" | custom-call | tf_op jit(solution)/shard_map/central/pallas_call | solution.py:445
  35.6 0.8 %mix.1 = (f32[128,768]{1,0:T(8,128)S(1)}, bf16[512,768]{1,0:T(8,128)(2,1)S(1)}) custom-call(bf16[512,128]{1,0:T(8,128)(2,1)S(1)} %get-tuple-element.36.patch, bf16[256,768]{1,0:T(8,128)(2,1)S(1)} %copy-done.1, bf16[256,768]{1,0:T(8,128)(2,1)S(1)} %collective-permute-done.6.refs_1_, bf16[256,768]{1,0:T(8,128)(2,1)S(1)} %collective-permute-done.7.refs_2_), custom_call_target="tpu_custom_call" | custom-call | tf_op jit(solution)/shard_map/mix/pallas_call | solution.py:465
  36.9 1.3 %back.1.refs_6_.refs_0_ = bf16[776,128]{1,0:T(8,128)(2,1)S(1)} custom-call(bf16[256,512]{1,0:T(8,128)(2,1)S(1)} %collective-permute-done.5.got_ref, bf16[576,128]{1,0:T(8,128)(2,1)S(1)} %get-tuple-element.31.k1_ref, bf16[1152,256]{1,0:T(8,128)(2,1)S(1)} %get-tuple-element.32.k2_ref, s32[1,128]{1,0:T(1,128)S(1)} %copy-done.4, ...), custom_call_target="tpu_custom_call" | custom-call | tf_op jit(solution)/shard_map/back/pallas_call | solution.py:493
  38.2 2.7 %collective-permute-start.10 = (bf16[776,128]{1,0:T(8,128)(2,1)S(1)}, bf16[776,128]{1,0:T(8,128)(2,1)S(1)}, u32[]{:S(2)}, u32[]{:S(2)}) collective-permute-start(bf16[776,128]{1,0:T(8,128)(2,1)S(1)} %back.1.refs_6_.refs_0_), channel_id=1, source_target_pairs={{0,8},{4,12},{8,0},{12,4},{1,9},{5,13},{9,1},{13,5},{2,10},{6,14},... | collective-permute-start | bytes 595976 | tf_op jit(solution)/shard_map/ppermute | solution.py:587
  40.9 0.5 collective-permute-start.12
  41.4 1.6 %collective-permute-start.9 = (bf16[776,128]{1,0:T(8,128)(2,1)S(1)}, bf16[776,128]{1,0:T(8,128)(2,1)S(1)}, u32[]{:S(2)}, u32[]{:S(2)}) collective-permute-start(bf16[776,128]{1,0:T(8,128)(2,1)S(1)} %back.1.refs_6_.refs_0_), channel_id=1, source_target_pairs={{0,4},{4,0},{8,12},{12,8},{1,5},{5,1},{9,13},{13,9},{2,6},{6,2},{1... | collective-permute-start | bytes 595976 | tf_op jit(solution)/shard_map/ppermute | solution.py:587
  43.0 7.5 %collective-permute-done.10.refs_2_ = bf16[776,128]{1,0:T(8,128)(2,1)S(1)} collective-permute-done((bf16[776,128]{1,0:T(8,128)(2,1)S(1)}, bf16[776,128]{1,0:T(8,128)(2,1)S(1)}, u32[]{:S(2)}, u32[]{:S(2)}) %collective-permute-start.10) | collective-permute-done | bytes 198688 | tf_op jit(solution)/shard_map/ppermute | solution.py:587
  50.5 0.6 %collective-permute-start.16 = (bf16[776,128]{1,0:T(8,128)(2,1)S(1)}, bf16[776,128]{1,0:T(8,128)(2,1)S(1)}, u32[]{:S(2)}, u32[]{:S(2)}) collective-permute-start(bf16[776,128]{1,0:T(8,128)(2,1)S(1)} %collective-permute-done.10.refs_2_), channel_id=1, source_target_pairs={{0,4},{4,0},{8,12},{12,8},{1,5},{5,1},{9,13},{13,9},{2,6},{6,2},{1... | collective-permute-start | bytes 595976 | tf_op jit(solution)/shard_map/ppermute | solution.py:587
  51.5 1.5 %prepare.1 = (bf16[768,1536]{1,0:T(8,128)(2,1)S(1)}, bf16[256,768]{1,0:T(8,128)(2,1)S(1)}, bf16[256,768]{1,0:T(8,128)(2,1)S(1)}, bf16[256,1536]{1,0:T(8,128)(2,1)S(1)}, bf16[512,512]{1,0:T(8,128)(2,1)S(1)}) custom-call(s32[4,128]{1,0:T(4,128)S(1)} %bitcast.5, bf16[192,2304]{1,0:T(8,128)(2,1)S(1)} %copy-done, ...), custom_call_target="tpu_custom_call" | custom-call | tf_op jit(solution)/shard_map/prepare/pallas_call | solution.py:512
  53.0 1.2 %extend.1 = (bf16[768,768]{1,0:T(8,128)(2,1)S(1)}, bf16[128,768]{1,0:T(8,128)(2,1)S(1)}, bf16[128,1536]{1,0:T(8,128)(2,1)S(1)}, f32[128,768]{1,0:T(8,128)S(1)}, ...) custom-call(bf16[512,512]{1,0:T(8,128)(2,1)S(1)} %get-tuple-element.41.perm_ref, ...), custom_call_target="tpu_custom_call" | custom-call | tf_op jit(solution)/shard_map/extend/pallas_call | solution.py:530
  54.2 2.3 %collective-permute-done.16.refs_0_ = bf16[776,128]{1,0:T(8,128)(2,1)S(1)} collective-permute-done((bf16[776,128]{1,0:T(8,128)(2,1)S(1)}, bf16[776,128]{1,0:T(8,128)(2,1)S(1)}, u32[]{:S(2)}, u32[]{:S(2)}) %collective-permute-start.16) | collective-permute-done | bytes 198688 | tf_op jit(solution)/shard_map/ppermute | solution.py:587
  56.5 3.8 %finish.1 = bf16[128,768]{1,0:T(8,128)(2,1)} custom-call(bf16[512,512]{1,0:T(8,128)(2,1)S(1)} %get-tuple-element.41.perm_ref, bf16[768,1536]{1,0:T(8,128)(2,1)S(1)} %get-tuple-element.42.joined, bf16[256,768]{1,0:T(8,128)(2,1)S(1)} %get-tuple-element.43.keys0, bf16[256,1536]{1,0:T(8,128)(2,1)S(1)} %get-tuple-element.44.values0, ...), custom_call_target="tpu_custom_call" | custom-call | tf_op jit(solution)/shard_map/finish/pallas_call | solution.py:568
  (29 shorter events, 1.0 us)
Async XLA Ops:
  0.0 13.1 %collective-permute-start.7 = (bf16[256,768]{1,0:T(8,128)(2,1)}, bf16[256,768]{1,0:T(8,128)(2,1)S(1)}, u32[]{:S(2)}, u32[]{:S(2)}) collective-permute-start(bf16[256,768]{1,0:T(8,128)(2,1)} %refs_0_.5), channel_id=1, source_target_pairs={{0,2},{2,0},{1,3},{3,1},{4,6},{6,4},{5,7},{7,5},{8,10},{10,8},{9,1... | collective-permute-start | bytes 1179656 | tf_op jit(solution)/shard_map/ppermute | solution.py:587
  3.0 8.1 %copy-start.1 = (bf16[256,768]{1,0:T(8,128)(2,1)S(1)}, bf16[256,768]{1,0:T(8,128)(2,1)}, u32[]{:S(2)}) copy-start(bf16[256,768]{1,0:T(8,128)(2,1)} %refs_0_.5) | copy-start | bytes 1179652
  3.0 11.5 %copy-start.2 = (bf16[192,768]{1,0:T(8,128)(2,1)S(1)}, bf16[192,768]{1,0:T(8,128)(2,1)}, u32[]{:S(2)}) copy-start(bf16[192,768]{1,0:T(8,128)(2,1)} %refs_0_.7) | copy-start | bytes 884740
  3.0 16.5 %copy-start = (bf16[192,2304]{1,0:T(8,128)(2,1)S(1)}, bf16[192,2304]{1,0:T(8,128)(2,1)}, u32[]{:S(2)}) copy-start(bf16[192,2304]{1,0:T(8,128)(2,1)} %refs_3_.1) | copy-start | bytes 2654212
  5.4 14.1 %collective-permute-start.1 = (bf16[96,1536]{1,0:T(8,128)(2,1)S(1)}, bf16[96,1536]{1,0:T(8,128)(2,1)S(1)}, u32[]{:S(2)}, u32[]{:S(2)}) collective-permute-start(bf16[96,1536]{1,0:T(8,128)(2,1)S(1)} %get-tuple-element.29), channel_id=1, source_target_pairs={{0,2},{2,0},{1,3},{3,1},{4,6},{6,4},{5,7},{7,5},{8,10},{10,8},{9,1... | collective-permute-start | bytes 884744 | tf_op jit(solution)/shard_map/ppermute | solution.py:587
  5.5 9.0 %collective-permute-start.5 = (bf16[256,512]{1,0:T(8,128)(2,1)S(1)}, bf16[256,512]{1,0:T(8,128)(2,1)S(1)}, u32[]{:S(2)}, u32[]{:S(2)}) collective-permute-start(bf16[256,512]{1,0:T(8,128)(2,1)S(1)} %get-tuple-element.30.msg_ref), channel_id=1, source_target_pairs={{0,4},{4,8},{8,12},{1,5},{5,9},{9,13},{2,6},{6,10},{10,14},{3,7},{... | collective-permute-start | bytes 786440 | tf_op jit(solution)/shard_map/ppermute | solution.py:611
  9.5 16.3 %collective-permute-start.11 = (bf16[192,768]{1,0:T(8,128)(2,1)S(1)}, bf16[192,768]{1,0:T(8,128)(2,1)S(1)}, u32[]{:S(2)}, u32[]{:S(2)}) collective-permute-start(bf16[192,768]{1,0:T(8,128)(2,1)S(1)} %get-tuple-element.46), channel_id=1, source_target_pairs={{0,2},{2,0},{1,3},{3,1},{4,6},{6,4},{5,7},{7,5},{8,10},{10,8},{9,1... | collective-permute-start | bytes 884744 | tf_op jit(solution)/shard_map/ppermute | solution.py:587
  11.0 22.0 %collective-permute-start.6 = (bf16[256,768]{1,0:T(8,128)(2,1)S(1)}, bf16[256,768]{1,0:T(8,128)(2,1)S(1)}, u32[]{:S(2)}, u32[]{:S(2)}) collective-permute-start(bf16[256,768]{1,0:T(8,128)(2,1)S(1)} %copy-done.1), channel_id=1, source_target_pairs={{0,1},{1,0},{2,3},{3,2},{4,5},{5,4},{6,7},{7,6},{8,9},{9,8},{10,11... | collective-permute-start | bytes 1179656 | tf_op jit(solution)/shard_map/ppermute | solution.py:587
  13.1 19.9 %collective-permute-start.8 = (bf16[256,768]{1,0:T(8,128)(2,1)S(1)}, bf16[256,768]{1,0:T(8,128)(2,1)S(1)}, u32[]{:S(2)}, u32[]{:S(2)}) collective-permute-start(bf16[256,768]{1,0:T(8,128)(2,1)S(1)} %collective-permute-done.7.refs_2_), channel_id=1, source_target_pairs={{0,1},{1,0},{2,3},{3,2},{4,5},{5,4},{6,7},{7,6},{8,9},{9,8},{10,11... | collective-permute-start | bytes 1179656 | tf_op jit(solution)/shard_map/ppermute | solution.py:587
  14.4 16.8 %collective-permute-start.14 = (bf16[192,768]{1,0:T(8,128)(2,1)S(1)}, bf16[192,768]{1,0:T(8,128)(2,1)S(1)}, u32[]{:S(2)}, u32[]{:S(2)}) collective-permute-start(bf16[192,768]{1,0:T(8,128)(2,1)S(1)} %copy-done.2), channel_id=1, source_target_pairs={{0,2},{2,0},{1,3},{3,1},{4,6},{6,4},{5,7},{7,5},{8,10},{10,8},{9,1... | collective-permute-start | bytes 884744 | tf_op jit(solution)/shard_map/ppermute | solution.py:587
  19.5 31.9 %collective-permute-start = (bf16[192,2304]{1,0:T(8,128)(2,1)S(1)}, bf16[192,2304]{1,0:T(8,128)(2,1)S(1)}, u32[]{:S(2)}, u32[]{:S(2)}) collective-permute-start(bf16[192,2304]{1,0:T(8,128)(2,1)S(1)} %copy-done), channel_id=1, source_target_pairs={{0,1},{1,0},{2,3},{3,2},{4,5},{5,4},{6,7},{7,6},{8,9},{9,8},{10,11... | collective-permute-start | bytes 2654216 | tf_op jit(solution)/shard_map/ppermute | solution.py:587
  25.8 12.4 %collective-permute-start.13 = (bf16[192,768]{1,0:T(8,128)(2,1)S(1)}, bf16[192,768]{1,0:T(8,128)(2,1)S(1)}, u32[]{:S(2)}, u32[]{:S(2)}) collective-permute-start(bf16[192,768]{1,0:T(8,128)(2,1)S(1)} %copy-done.2), channel_id=1, source_target_pairs={{0,1},{1,0},{2,3},{3,2},{4,5},{5,4},{6,7},{7,6},{8,9},{9,8},{10,11... | collective-permute-start | bytes 884744 | tf_op jit(solution)/shard_map/ppermute | solution.py:587
  31.2 9.7 %collective-permute-start.2 = (bf16[96,1536]{1,0:T(8,128)(2,1)S(1)}, bf16[96,1536]{1,0:T(8,128)(2,1)S(1)}, u32[]{:S(2)}, u32[]{:S(2)}) collective-permute-start(bf16[96,1536]{1,0:T(8,128)(2,1)S(1)} %collective-permute-done.1.refs_2_), channel_id=1, source_target_pairs={{0,16},{16,0},{1,17},{17,1},{2,18},{18,2},{3,19},{19,3},{4,20},{20... | collective-permute-start | bytes 884744 | tf_op jit(solution)/shard_map/ppermute | solution.py:587
  33.0 7.9 %collective-permute-start.3 = (bf16[96,1536]{1,0:T(8,128)(2,1)S(1)}, bf16[96,1536]{1,0:T(8,128)(2,1)S(1)}, u32[]{:S(2)}, u32[]{:S(2)}) collective-permute-start(bf16[96,1536]{1,0:T(8,128)(2,1)S(1)} %collective-permute-done.1.refs_2_), channel_id=1, source_target_pairs={{0,1},{1,0},{2,3},{3,2},{4,5},{5,4},{6,7},{7,6},{8,9},{9,8},{10,11... | collective-permute-start | bytes 884744 | tf_op jit(solution)/shard_map/ppermute | solution.py:587
  33.0 8.4 %collective-permute-start.15 = (bf16[192,768]{1,0:T(8,128)(2,1)S(1)}, bf16[192,768]{1,0:T(8,128)(2,1)S(1)}, u32[]{:S(2)}, u32[]{:S(2)}) collective-permute-start(bf16[192,768]{1,0:T(8,128)(2,1)S(1)} %collective-permute-done.14.refs_2_), channel_id=1, source_target_pairs={{0,1},{1,0},{2,3},{3,2},{4,5},{5,4},{6,7},{7,6},{8,9},{9,8},{10,11... | collective-permute-start | bytes 884744 | tf_op jit(solution)/shard_map/ppermute | solution.py:587
  35.6 1.3 %copy-start.4 = (s32[1,128]{1,0:T(1,128)S(1)}, s32[1,128]{1,0:T(1,128)}, u32[]{:S(2)}) copy-start(s32[1,128]{1,0:T(1,128)} %active_ref.1) | copy-start | bytes 1540
  38.2 13.3 %copy-start.3 = (s32[1,512]{1,0:T(1,128)S(1)}, s32[1,512]{1,0:T(1,128)}, u32[]{:S(2)}) copy-start(s32[1,512]{1,0:T(1,128)} %param.14) | copy-start | bytes 6148
  38.2 12.3 %collective-permute-start.10 = (bf16[776,128]{1,0:T(8,128)(2,1)S(1)}, bf16[776,128]{1,0:T(8,128)(2,1)S(1)}, u32[]{:S(2)}, u32[]{:S(2)}) collective-permute-start(bf16[776,128]{1,0:T(8,128)(2,1)S(1)} %back.1.refs_6_.refs_0_), channel_id=1, source_target_pairs={{0,8},{4,12},{8,0},{12,4},{1,9},{5,13},{9,1},{13,5},{2,10},{6,14},... | collective-permute-start | bytes 595976 | tf_op jit(solution)/shard_map/ppermute | solution.py:587
  40.9 10.5 %collective-permute-start.4 = (bf16[96,1536]{1,0:T(8,128)(2,1)S(1)}, bf16[96,1536]{1,0:T(8,128)(2,1)S(1)}, u32[]{:S(2)}, u32[]{:S(2)}) collective-permute-start(bf16[96,1536]{1,0:T(8,128)(2,1)S(1)} %collective-permute-done.2.refs_3_), channel_id=1, source_target_pairs={{0,1},{1,0},{2,3},{3,2},{4,5},{5,4},{6,7},{7,6},{8,9},{9,8},{10,11... | collective-permute-start | bytes 884744 | tf_op jit(solution)/shard_map/ppermute | solution.py:587
  40.9 12.1 %collective-permute-start.12 = (bf16[192,768]{1,0:T(8,128)(2,1)S(1)}, bf16[192,768]{1,0:T(8,128)(2,1)S(1)}, u32[]{:S(2)}, u32[]{:S(2)}) collective-permute-start(bf16[192,768]{1,0:T(8,128)(2,1)S(1)} %collective-permute-done.11.refs_5_), channel_id=1, source_target_pairs={{0,1},{1,0},{2,3},{3,2},{4,5},{5,4},{6,7},{7,6},{8,9},{9,8},{10,11... | collective-permute-start | bytes 884744 | tf_op jit(solution)/shard_map/ppermute | solution.py:587
  41.4 10.1 %collective-permute-start.9 = (bf16[776,128]{1,0:T(8,128)(2,1)S(1)}, bf16[776,128]{1,0:T(8,128)(2,1)S(1)}, u32[]{:S(2)}, u32[]{:S(2)}) collective-permute-start(bf16[776,128]{1,0:T(8,128)(2,1)S(1)} %back.1.refs_6_.refs_0_), channel_id=1, source_target_pairs={{0,4},{4,0},{8,12},{12,8},{1,5},{5,1},{9,13},{13,9},{2,6},{6,2},{1... | collective-permute-start | bytes 595976 | tf_op jit(solution)/shard_map/ppermute | solution.py:587
  50.5 6.0 %collective-permute-start.16 = (bf16[776,128]{1,0:T(8,128)(2,1)S(1)}, bf16[776,128]{1,0:T(8,128)(2,1)S(1)}, u32[]{:S(2)}, u32[]{:S(2)}) collective-permute-start(bf16[776,128]{1,0:T(8,128)(2,1)S(1)} %collective-permute-done.10.refs_2_), channel_id=1, source_target_pairs={{0,4},{4,0},{8,12},{12,8},{1,5},{5,1},{9,13},{13,9},{2,6},{6,2},{1... | collective-permute-start | bytes 595976 | tf_op jit(solution)/shard_map/ppermute | solution.py:587

commit v7 on v6

--- a/solution.py
+++ b/solution.py
@@ -194,10 +194,11 @@
 ):
     out_ref, all1, all2, patch = refs[-4:]
     splitter = split_matrix()
-    odd = got_ref[channels : 2 * channels, :].astype(F32)
-    all1[:channels, :] = later(odd).astype(BF)
-    all1[channels:, :] = got_ref[: 2 * channels, :]
-    even, odd = split_time(got_ref[2 * channels :, :], splitter)
+    got = got_ref[...]
+    got = jnp.where(lax.axis_index("seq") > 0, got, jnp.zeros_like(got))
+    all1[:channels, :] = later(got[channels : 2 * channels].astype(F32)).astype(BF)
+    all1[channels:, :] = got[: 2 * channels]
+    even, odd = split_time(got[2 * channels :], splitter)
     store_taps(all2, 0, even, odd)
     first = silu(first_ref[...] + dot(k1_ref[: 3 * channels, :], all1[...], 0, 0)).astype(BF)
     even, odd = split_time(first, splitter)
@@ -301,12 +302,10 @@
     lift(joined, normed, keys, values)
 
 
-def extend_kernel(perm_ref, joined, normed0, *refs, pieces, chunks, early, swap):
+def extend_kernel(perm_ref, joined, normed0, *refs, chunks, early, swap):
     chunk_refs = refs[:chunks]
-    query_refs = refs[chunks : chunks + pieces]
-    query, keys1, values1, token_ref, picked_ref, on_ref, normed1, sems = refs[chunks + pieces :]
+    keys1, values1, token_ref, picked_ref, on_ref, normed1 = refs[chunks:]
     count = token_ref.shape[0]
-    copies = collect(weight_rows(query_refs), query, sems)
     for slot, ref in enumerate(chunk_refs[early:]):
         normed1[slot * count : (slot + 1) * count, :] = normal(tokens_of(ref))
     lift(joined, normed1, keys1, values1)
@@ -316,13 +315,14 @@
     on, token = flags_and_tokens(perm_ref, own, chunk_refs, 0)
     on_ref[...] = on
     token_ref[...] = token
+
+
+def gather_kernel(*refs):
+    query, output, sems = refs[-3:]
+    pieces = len(refs) // 2 - 1
+    copies = collect(weight_rows(refs[:pieces]), query, sems.at[0])
+    copies += collect(weight_rows(refs[pieces : 2 * pieces]), output, sems.at[1])
     for copy in copies:
-        copy.wait()
-
-
-def gather_kernel(*refs):
-    output, sems = refs[-2:]
-    for copy in collect(weight_rows(refs[:-2]), output, sems):
         copy.wait()
 
 
@@ -520,47 +520,46 @@
     )(order, *weights, *chunks)
 
 
-def extend(ready, chunks, weights, early, swap):
+def extend(ready, chunks, early, swap):
     joined, normed, _, _, perm = ready
     width = joined.shape[0]
     size = perm.shape[0]
     count = chunks[0].shape[1]
     far = (len(chunks) - early) * count
-    pieces = len(weights)
-    return pl.pallas_call(
-        functools.partial(extend_kernel, pieces=pieces, chunks=len(chunks), early=early, swap=swap),
+    return pl.pallas_call(
+        functools.partial(extend_kernel, chunks=len(chunks), early=early, swap=swap),
         out_shape=(
-            array((width, width)),
             array((far, width)),
             array((far, 2 * width)),
             array((count, width), F32),
             array((count, width), F32),
             array((EXTRA, size), F32),
         ),
-        in_specs=[vmem()] * (3 + len(chunks)) + [fixed()] + [hbm()] * (pieces - 1),
-        out_specs=[vmem()] * 6,
-        scratch_shapes=[pltpu.VMEM((far, width), BF), pltpu.SemaphoreType.DMA((pieces,))],
+        in_specs=[vmem()] * (3 + len(chunks)),
+        out_specs=[vmem()] * 5,
+        scratch_shapes=[pltpu.VMEM((far, width), BF)],
         compiler_params=params(8 + size // 128),
         name="extend",
-    )(perm, joined, normed, *chunks, *weights)
-
-
-def gather(weights):
-    width = weights[0].shape[1]
+    )(perm, joined, normed, *chunks)
+
+
+def gather(query_weights, output_weights):
+    width = output_weights[0].shape[1]
+    pieces = len(output_weights)
     return pl.pallas_call(
         gather_kernel,
-        out_shape=array((width, width)),
-        in_specs=[fixed()] + [hbm()] * (len(weights) - 1),
-        out_specs=vmem(),
-        scratch_shapes=[pltpu.SemaphoreType.DMA((len(weights),))],
+        out_shape=(array((width, width)), array((width, width))),
+        in_specs=([fixed()] + [hbm()] * (pieces - 1)) * 2,
+        out_specs=[vmem()] * 2,
+        scratch_shapes=[pltpu.SemaphoreType.DMA((2, pieces))],
         compiler_params=params(4),
         name="gather",
-    )(*weights)
-
-
-def finish(ready, extra, output, chunks, swap):
+    )(*query_weights, *output_weights)
+
+
+def finish(ready, extra, weights, chunks, swap):
     joined, _, keys, values, perm = ready
-    query, keys1, values1, token, picked, on = extra
+    keys1, values1, token, picked, on = extra
     width = joined.shape[0]
     size = perm.shape[0]
     count = token.shape[0]
@@ -579,7 +578,7 @@
         ],
         compiler_params=params(8 + size // 64),
         name="finish",
-    )(perm, joined, keys, values, keys1, values1, query, output, token, picked, on, *chunks)
+    )(perm, joined, keys, values, keys1, values1, *weights, token, picked, on, *chunks)
 
 
 def exchanged(value, axis, flip):
@@ -608,7 +607,7 @@
     else:
         embeds = [lax.all_gather(embed_weight, ("mp", "section"), axis=0, tiled=True)]
         msg, rows, k1, k2 = front(rows, k1, k2, wires, ())
-    got = lax.ppermute(msg, "seq", [(i, i + 1) for i in range(shards - 1)])
+    got = lax.ppermute(msg, "seq", [(i, (i + 1) % shards) for i in range(shards)])
     first, second, patch = central(msg, rows, k1, k2, wires, count)
     token, low = mix(patch, embeds)
     parts = [first, second, token, low]
@@ -643,9 +642,9 @@
         output_weights = [lax.all_gather(output_weight, ("mp", "section"), axis=0, tiled=True)]
     early, later = shards // 2, shards // 2 + shards // 4
     ready = prepare(order, kv_weights, chunks[:early], swap)
-    extra = extend(ready, chunks[:later], query_weights, early, swap)
-    output = gather(output_weights)
-    result = finish(ready, extra, output, chunks[later:], swap)
+    extra = extend(ready, chunks[:later], early, swap)
+    weights = gather(query_weights, output_weights)
+    result = finish(ready, extra, weights, chunks[later:], swap)
     return result[None]
 
 

time: 60.4 us -> 60.5 us (level)
  waiting for transfers between devices: 28.6 us -> 31 us
  starting transfers between devices: 17.7 us -> 15.4 us
    ppermute x1, starting transfers between devices: 4 us -> 2.14 us  [layer(): lax.ppermute(msg, 'seq', [(i, (i + 1) % shards) for i in range(shards)])]
    ppermute x16, waiting for transfers between devices: 27.3 us -> 28.9 us  [exchanged(): return lax.ppermute(value, axis, [(i, i ^ flip) for i in range(count)])]
    ppermute x1, waiting for transfers between devices: 1.29 us -> 2.16 us  [layer(): lax.ppermute(msg, 'seq', [(i, (i + 1) % shards) for i in range(shards)])]
where the time goes in v7:
time: 60.5 us; the launch traced here: 60.4 us
  waiting for transfers between devices  31 us (51%)
  starting transfers between devices  15.4 us (25%)
  Pallas kernels  13.8 us (23%)
    ppermute x16, waiting for transfers between devices, exchanged(): return lax.ppermute(value, axis, [(i, i ^ flip) for i in range(count)])  28.9 us
    ppermute x16, starting transfers between devices, exchanged(): return lax.ppermute(value, axis, [(i, i ^ flip) for i in range(count)])  13.3 us
    pallas_call x1, Pallas kernels, finish(): pl.pallas_call(functools.partial(finish_kernel, chunks=len(chunks), swap=...  3.75 us
    pallas_call x1, Pallas kernels, front(): pl.pallas_call(functools.partial(front_kernel, wires=wires, channels=chan...  2.39 us
    ppermute x1, waiting for transfers between devices, layer(): lax.ppermute(msg, 'seq', [(i, (i + 1) % shards) for i in range(shards)])  2.16 us
    ppermute x1, starting transfers between devices, layer(): lax.ppermute(msg, 'seq', [(i, (i + 1) % shards) for i in range(shards)])  2.14 us
    pallas_call x1, Pallas kernels, central(): pl.pallas_call(functools.partial(central_kernel, wires=wires, channels=ch...  2.04 us
    pallas_call x1, Pallas kernels, prepare(): pl.pallas_call(functools.partial(prepare_kernel, pieces=len(weights), chu...  1.57 us
  transfers between devices with their start and end apart: 17, of which 8 were waited for; matrix products, arithmetic and copies ran while one was open for 0% of the time, Pallas kernels for 17%

profile of v7, /device:TPU:0, one launch (start us, length us, event | category | flops | bytes accessed | tf_op | source)
XLA Modules:
  0.0 60.4 jit_solution(10297188189986755393)
XLA Ops:
  0.0 3.0 %collective-permute-start.7 = (bf16[256,768]{1,0:T(8,128)(2,1)}, bf16[256,768]{1,0:T(8,128)(2,1)S(1)}, u32[]{:S(2)}, u32[]{:S(2)}) collective-permute-start(bf16[256,768]{1,0:T(8,128)(2,1)} %refs_0_.5), channel_id=1, source_target_pairs={{0,2},{2,0},{1,3},{3,1},{4,6},{6,4},{5,7},{7,5},{8,10},{10,8},{9,1... | collective-permute-start | bytes 1179656 | tf_op jit(solution)/shard_map/ppermute | solution.py:586
  3.0 2.4 %front.1 = (bf16[256,512]{1,0:T(8,128)(2,1)S(1)}, bf16[512,1024]{1,0:T(8,128)(2,1)S(1)}, bf16[576,128]{1,0:T(8,128)(2,1)S(1)}, bf16[1152,256]{1,0:T(8,128)(2,1)S...) custom-call(bf16[512,1024]{1,0:T(8,128)(2,1)} %bitcast.6, bf16[576,128]{1,0:T(8,128)(2,1)} %bitcast.8, ...), custom_call_target="tpu_custom_call" | custom-call | tf_op jit(solution)/shard_map/front/pallas_call | solution.py:425
  5.4 2.1 %collective-permute-start.5 = (bf16[256,512]{1,0:T(8,128)(2,1)S(1)}, bf16[256,512]{1,0:T(8,128)(2,1)S(1)}, u32[]{:S(2)}, u32[]{:S(2)}) collective-permute-start(bf16[256,512]{1,0:T(8,128)(2,1)S(1)} %get-tuple-element.31.msg_ref), channel_id=1, source_target_pairs={{0,4},{4,8},{8,12},{12,0},{1,5},{5,9},{9,13},{13,1},{2,6},{6,10},{... | collective-permute-start | bytes 786440 | tf_op jit(solution)/shard_map/ppermute | solution.py:610
  7.5 1.5 %collective-permute-start.1 = (bf16[96,1536]{1,0:T(8,128)(2,1)S(1)}, bf16[96,1536]{1,0:T(8,128)(2,1)S(1)}, u32[]{:S(2)}, u32[]{:S(2)}) collective-permute-start(bf16[96,1536]{1,0:T(8,128)(2,1)S(1)} %get-tuple-element.30), channel_id=1, source_target_pairs={{0,2},{2,0},{1,3},{3,1},{4,6},{6,4},{5,7},{7,5},{8,10},{10,8},{9,1... | collective-permute-start | bytes 884744 | tf_op jit(solution)/shard_map/ppermute | solution.py:586
  9.0 4.1 %collective-permute-done.7.refs_2_ = bf16[256,768]{1,0:T(8,128)(2,1)S(1)} collective-permute-done((bf16[256,768]{1,0:T(8,128)(2,1)}, bf16[256,768]{1,0:T(8,128)(2,1)S(1)}, u32[]{:S(2)}, u32[]{:S(2)}) %collective-permute-start.7) | collective-permute-done | bytes 393248 | tf_op jit(solution)/shard_map/ppermute | solution.py:586
  13.1 2.2 %collective-permute-done.5.got_ref = bf16[256,512]{1,0:T(8,128)(2,1)S(1)} collective-permute-done((bf16[256,512]{1,0:T(8,128)(2,1)S(1)}, bf16[256,512]{1,0:T(8,128)(2,1)S(1)}, u32[]{:S(2)}, u32[]{:S(2)}) %collective-permute-start.5) | collective-permute-done | bytes 262176 | tf_op jit(solution)/shard_map/ppermute | solution.py:610
  15.3 1.5 %collective-permute-start.11 = (bf16[192,768]{1,0:T(8,128)(2,1)S(1)}, bf16[192,768]{1,0:T(8,128)(2,1)S(1)}, u32[]{:S(2)}, u32[]{:S(2)}) collective-permute-start(bf16[192,768]{1,0:T(8,128)(2,1)S(1)} %get-tuple-element.49), channel_id=1, source_target_pairs={{0,2},{2,0},{1,3},{3,1},{4,6},{6,4},{5,7},{7,5},{8,10},{10,8},{9,1... | collective-permute-start | bytes 884744 | tf_op jit(solution)/shard_map/ppermute | solution.py:586
  16.8 2.7 %collective-permute-done.14.refs_6_ = bf16[192,768]{1,0:T(8,128)(2,1)S(1)} collective-permute-done((bf16[192,768]{1,0:T(8,128)(2,1)}, bf16[192,768]{1,0:T(8,128)(2,1)S(1)}, u32[]{:S(2)}, u32[]{:S(2)}) %collective-permute-start.14) | collective-permute-done | bytes 294944 | tf_op jit(solution)/shard_map/ppermute | solution.py:586
  19.5 6.3 %collective-permute-done.1.refs_2_ = bf16[96,1536]{1,0:T(8,128)(2,1)S(1)} collective-permute-done((bf16[96,1536]{1,0:T(8,128)(2,1)S(1)}, bf16[96,1536]{1,0:T(8,128)(2,1)S(1)}, u32[]{:S(2)}, u32[]{:S(2)}) %collective-permute-start.1) | collective-permute-done | bytes 294944 | tf_op jit(solution)/shard_map/ppermute | solution.py:586
  25.8 5.5 %collective-permute-done.11.refs_2_ = bf16[192,768]{1,0:T(8,128)(2,1)S(1)} collective-permute-done((bf16[192,768]{1,0:T(8,128)(2,1)S(1)}, bf16[192,768]{1,0:T(8,128)(2,1)S(1)}, u32[]{:S(2)}, u32[]{:S(2)}) %collective-permute-start.11) | collective-permute-done | bytes 294944 | tf_op jit(solution)/shard_map/ppermute | solution.py:586
  31.3 1.8 %collective-permute-start.2 = (bf16[96,1536]{1,0:T(8,128)(2,1)S(1)}, bf16[96,1536]{1,0:T(8,128)(2,1)S(1)}, u32[]{:S(2)}, u32[]{:S(2)}) collective-permute-start(bf16[96,1536]{1,0:T(8,128)(2,1)S(1)} %collective-permute-done.1.refs_2_), channel_id=1, source_target_pairs={{0,16},{16,0},{1,17},{17,1},{2,18},{18,2},{3,19},{19,3},{4,20},{20... | collective-permute-start | bytes 884744 | tf_op jit(solution)/shard_map/ppermute | solution.py:586
  33.3 2.0 %central.1 = (f32[128,512]{1,0:T(8,128)S(1)}, f32[256,256]{1,0:T(8,128)S(1)}, bf16[512,128]{1,0:T(8,128)(2,1)S(1)}) custom-call(bf16[256,512]{1,0:T(8,128)(2,1)S(1)} %get-tuple-element.31.msg_ref, bf16[512,1024]{1,0:T(8,128)(2,1)S(1)} %get-tuple-element.34.x_ref, bf16[576,128]{1,0:T(8,128)(2,1)S(1)} %get-tuple-element.32.k1_ref, ...), custom_call_target="tpu_custom_call" | custom-call | tf_op jit(solution)/shard_map/central/pallas_call | solution.py:445
  35.3 0.8 %mix.1 = (f32[128,768]{1,0:T(8,128)S(1)}, bf16[512,768]{1,0:T(8,128)(2,1)S(1)}) custom-call(bf16[512,128]{1,0:T(8,128)(2,1)S(1)} %get-tuple-element.37.patch, bf16[256,768]{1,0:T(8,128)(2,1)S(1)} %copy-done.1, bf16[256,768]{1,0:T(8,128)(2,1)S(1)} %collective-permute-done.6.refs_1_, bf16[256,768]{1,0:T(8,128)(2,1)S(1)} %collective-permute-done.7.refs_2_), custom_call_target="tpu_custom_call" | custom-call | tf_op jit(solution)/shard_map/mix/pallas_call | solution.py:465
  36.1 0.4 blend.1
  36.6 1.3 %back.1.refs_6_.refs_0_ = bf16[776,128]{1,0:T(8,128)(2,1)S(1)} custom-call(bf16[256,512]{1,0:T(8,128)(2,1)S(1)} %collective-permute-done.5.got_ref, bf16[576,128]{1,0:T(8,128)(2,1)S(1)} %get-tuple-element.32.k1_ref, bf16[1152,256]{1,0:T(8,128)(2,1)S(1)} %get-tuple-element.33.k2_ref, s32[1,128]{1,0:T(1,128)S(1)} %copy-done.4, ...), custom_call_target="tpu_custom_call" | custom-call | tf_op jit(solution)/shard_map/back/pallas_call | solution.py:493
  38.0 2.7 %collective-permute-start.10 = (bf16[776,128]{1,0:T(8,128)(2,1)S(1)}, bf16[776,128]{1,0:T(8,128)(2,1)S(1)}, u32[]{:S(2)}, u32[]{:S(2)}) collective-permute-start(bf16[776,128]{1,0:T(8,128)(2,1)S(1)} %back.1.refs_6_.refs_0_), channel_id=1, source_target_pairs={{0,8},{4,12},{8,0},{12,4},{1,9},{5,13},{9,1},{13,5},{2,10},{6,14},... | collective-permute-start | bytes 595976 | tf_op jit(solution)/shard_map/ppermute | solution.py:586
  41.1 1.6 %collective-permute-start.9 = (bf16[776,128]{1,0:T(8,128)(2,1)S(1)}, bf16[776,128]{1,0:T(8,128)(2,1)S(1)}, u32[]{:S(2)}, u32[]{:S(2)}) collective-permute-start(bf16[776,128]{1,0:T(8,128)(2,1)S(1)} %back.1.refs_6_.refs_0_), channel_id=1, source_target_pairs={{0,4},{4,0},{8,12},{12,8},{1,5},{5,1},{9,13},{13,9},{2,6},{6,2},{1... | collective-permute-start | bytes 595976 | tf_op jit(solution)/shard_map/ppermute | solution.py:586
  42.7 7.7 %collective-permute-done.10.refs_2_ = bf16[776,128]{1,0:T(8,128)(2,1)S(1)} collective-permute-done((bf16[776,128]{1,0:T(8,128)(2,1)S(1)}, bf16[776,128]{1,0:T(8,128)(2,1)S(1)}, u32[]{:S(2)}, u32[]{:S(2)}) %collective-permute-start.10) | collective-permute-done | bytes 198688 | tf_op jit(solution)/shard_map/ppermute | solution.py:586
  50.4 0.6 %collective-permute-start.16 = (bf16[776,128]{1,0:T(8,128)(2,1)S(1)}, bf16[776,128]{1,0:T(8,128)(2,1)S(1)}, u32[]{:S(2)}, u32[]{:S(2)}) collective-permute-start(bf16[776,128]{1,0:T(8,128)(2,1)S(1)} %collective-permute-done.10.refs_2_), channel_id=1, source_target_pairs={{0,4},{4,0},{8,12},{12,8},{1,5},{5,1},{9,13},{13,9},{2,6},{6,2},{1... | collective-permute-start | bytes 595976 | tf_op jit(solution)/shard_map/ppermute | solution.py:586
  51.0 0.5 gather.1
  51.6 1.6 %prepare.1 = (bf16[768,1536]{1,0:T(8,128)(2,1)S(1)}, bf16[256,768]{1,0:T(8,128)(2,1)S(1)}, bf16[256,768]{1,0:T(8,128)(2,1)S(1)}, bf16[256,1536]{1,0:T(8,128)(2,1)S(1)}, bf16[512,512]{1,0:T(8,128)(2,1)S(1)}) custom-call(s32[4,128]{1,0:T(4,128)S(1)} %bitcast.5, bf16[192,2304]{1,0:T(8,128)(2,1)S(1)} %copy-done, ...), custom_call_target="tpu_custom_call" | custom-call | tf_op jit(solution)/shard_map/prepare/pallas_call | solution.py:512
  53.2 1.0 %extend.1 = (bf16[128,768]{1,0:T(8,128)(2,1)S(1)}, bf16[128,1536]{1,0:T(8,128)(2,1)S(1)}, f32[128,768]{1,0:T(8,128)S(1)}, f32[128,768]{1,0:T(8,128)S(1)}, f32[8,512]{1,0:T(8,128)S(1)}) custom-call(bf16[512,512]{1,0:T(8,128)(2,1)S(1)} %get-tuple-element.42.perm_ref, bf16[768,1536]{1,0:T(8,128)(2,1)S(1)} %get-tuple-element.43.joined, ...), custom_call_target="tpu_custom_call" | custom-call | tf_op jit(solution)/shard_map/extend/pallas_call | solution.py:529
  54.1 2.5 %collective-permute-done.16.refs_0_ = bf16[776,128]{1,0:T(8,128)(2,1)S(1)} collective-permute-done((bf16[776,128]{1,0:T(8,128)(2,1)S(1)}, bf16[776,128]{1,0:T(8,128)(2,1)S(1)}, u32[]{:S(2)}, u32[]{:S(2)}) %collective-permute-start.16) | collective-permute-done | bytes 198688 | tf_op jit(solution)/shard_map/ppermute | solution.py:586
  56.6 3.8 %finish.1 = bf16[128,768]{1,0:T(8,128)(2,1)} custom-call(bf16[512,512]{1,0:T(8,128)(2,1)S(1)} %get-tuple-element.42.perm_ref, bf16[768,1536]{1,0:T(8,128)(2,1)S(1)} %get-tuple-element.43.joined, bf16[256,768]{1,0:T(8,128)(2,1)S(1)} %get-tuple-element.44.keys0, bf16[256,1536]{1,0:T(8,128)(2,1)S(1)} %get-tuple-element.45.values0, ...), custom_call_target="tpu_custom_call" | custom-call | tf_op jit(solution)/shard_map/finish/pallas_call | solution.py:567
  (29 shorter events, 0.8 us)
Async XLA Ops:
  0.0 13.1 %collective-permute-start.7 = (bf16[256,768]{1,0:T(8,128)(2,1)}, bf16[256,768]{1,0:T(8,128)(2,1)S(1)}, u32[]{:S(2)}, u32[]{:S(2)}) collective-permute-start(bf16[256,768]{1,0:T(8,128)(2,1)} %refs_0_.5), channel_id=1, source_target_pairs={{0,2},{2,0},{1,3},{3,1},{4,6},{6,4},{5,7},{7,5},{8,10},{10,8},{9,1... | collective-permute-start | bytes 1179656 | tf_op jit(solution)/shard_map/ppermute | solution.py:586
  3.0 16.5 %collective-permute-start.14 = (bf16[192,768]{1,0:T(8,128)(2,1)}, bf16[192,768]{1,0:T(8,128)(2,1)S(1)}, u32[]{:S(2)}, u32[]{:S(2)}) collective-permute-start(bf16[192,768]{1,0:T(8,128)(2,1)} %refs_4_.1), channel_id=1, source_target_pairs={{0,2},{2,0},{1,3},{3,1},{4,6},{6,4},{5,7},{7,5},{8,10},{10,8},{9,1... | collective-permute-start | bytes 884744 | tf_op jit(solution)/shard_map/ppermute | solution.py:586
  3.0 6.0 %copy-start.1 = (bf16[256,768]{1,0:T(8,128)(2,1)S(1)}, bf16[256,768]{1,0:T(8,128)(2,1)}, u32[]{:S(2)}) copy-start(bf16[256,768]{1,0:T(8,128)(2,1)} %refs_0_.5) | copy-start | bytes 1179652
  3.0 16.5 %copy-start = (bf16[192,2304]{1,0:T(8,128)(2,1)S(1)}, bf16[192,2304]{1,0:T(8,128)(2,1)}, u32[]{:S(2)}) copy-start(bf16[192,2304]{1,0:T(8,128)(2,1)} %refs_0_.7) | copy-start | bytes 2654212
  3.0 22.8 %copy-start.2 = (bf16[192,768]{1,0:T(8,128)(2,1)S(1)}, bf16[192,768]{1,0:T(8,128)(2,1)}, u32[]{:S(2)}) copy-start(bf16[192,768]{1,0:T(8,128)(2,1)} %refs_4_.1) | copy-start | bytes 884740
  5.4 9.9 %collective-permute-start.5 = (bf16[256,512]{1,0:T(8,128)(2,1)S(1)}, bf16[256,512]{1,0:T(8,128)(2,1)S(1)}, u32[]{:S(2)}, u32[]{:S(2)}) collective-permute-start(bf16[256,512]{1,0:T(8,128)(2,1)S(1)} %get-tuple-element.31.msg_ref), channel_id=1, source_target_pairs={{0,4},{4,8},{8,12},{12,0},{1,5},{5,9},{9,13},{13,1},{2,6},{6,10},{... | collective-permute-start | bytes 786440 | tf_op jit(solution)/shard_map/ppermute | solution.py:610
  7.5 18.2 %collective-permute-start.1 = (bf16[96,1536]{1,0:T(8,128)(2,1)S(1)}, bf16[96,1536]{1,0:T(8,128)(2,1)S(1)}, u32[]{:S(2)}, u32[]{:S(2)}) collective-permute-start(bf16[96,1536]{1,0:T(8,128)(2,1)S(1)} %get-tuple-element.30), channel_id=1, source_target_pairs={{0,2},{2,0},{1,3},{3,1},{4,6},{6,4},{5,7},{7,5},{8,10},{10,8},{9,1... | collective-permute-start | bytes 884744 | tf_op jit(solution)/shard_map/ppermute | solution.py:586
  9.0 22.2 %collective-permute-start.6 = (bf16[256,768]{1,0:T(8,128)(2,1)S(1)}, bf16[256,768]{1,0:T(8,128)(2,1)S(1)}, u32[]{:S(2)}, u32[]{:S(2)}) collective-permute-start(bf16[256,768]{1,0:T(8,128)(2,1)S(1)} %copy-done.1), channel_id=1, source_target_pairs={{0,1},{1,0},{2,3},{3,2},{4,5},{5,4},{6,7},{7,6},{8,9},{9,8},{10,11... | collective-permute-start | bytes 1179656 | tf_op jit(solution)/shard_map/ppermute | solution.py:586
  13.1 19.9 %collective-permute-start.8 = (bf16[256,768]{1,0:T(8,128)(2,1)S(1)}, bf16[256,768]{1,0:T(8,128)(2,1)S(1)}, u32[]{:S(2)}, u32[]{:S(2)}) collective-permute-start(bf16[256,768]{1,0:T(8,128)(2,1)S(1)} %collective-permute-done.7.refs_2_), channel_id=1, source_target_pairs={{0,1},{1,0},{2,3},{3,2},{4,5},{5,4},{6,7},{7,6},{8,9},{9,8},{10,11... | collective-permute-start | bytes 1179656 | tf_op jit(solution)/shard_map/ppermute | solution.py:586
  15.3 15.9 %collective-permute-start.11 = (bf16[192,768]{1,0:T(8,128)(2,1)S(1)}, bf16[192,768]{1,0:T(8,128)(2,1)S(1)}, u32[]{:S(2)}, u32[]{:S(2)}) collective-permute-start(bf16[192,768]{1,0:T(8,128)(2,1)S(1)} %get-tuple-element.49), channel_id=1, source_target_pairs={{0,2},{2,0},{1,3},{3,1},{4,6},{6,4},{5,7},{7,5},{8,10},{10,8},{9,1... | collective-permute-start | bytes 884744 | tf_op jit(solution)/shard_map/ppermute | solution.py:586
  19.5 31.6 %collective-permute-start = (bf16[192,2304]{1,0:T(8,128)(2,1)S(1)}, bf16[192,2304]{1,0:T(8,128)(2,1)S(1)}, u32[]{:S(2)}, u32[]{:S(2)}) collective-permute-start(bf16[192,2304]{1,0:T(8,128)(2,1)S(1)} %copy-done), channel_id=1, source_target_pairs={{0,1},{1,0},{2,3},{3,2},{4,5},{5,4},{6,7},{7,6},{8,9},{9,8},{10,11... | collective-permute-start | bytes 2654216 | tf_op jit(solution)/shard_map/ppermute | solution.py:586
  25.8 12.2 %collective-permute-start.13 = (bf16[192,768]{1,0:T(8,128)(2,1)S(1)}, bf16[192,768]{1,0:T(8,128)(2,1)S(1)}, u32[]{:S(2)}, u32[]{:S(2)}) collective-permute-start(bf16[192,768]{1,0:T(8,128)(2,1)S(1)} %copy-done.2), channel_id=1, source_target_pairs={{0,1},{1,0},{2,3},{3,2},{4,5},{5,4},{6,7},{7,6},{8,9},{9,8},{10,11... | collective-permute-start | bytes 884744 | tf_op jit(solution)/shard_map/ppermute | solution.py:586
  31.2 9.4 %collective-permute-start.15 = (bf16[192,768]{1,0:T(8,128)(2,1)S(1)}, bf16[192,768]{1,0:T(8,128)(2,1)S(1)}, u32[]{:S(2)}, u32[]{:S(2)}) collective-permute-start(bf16[192,768]{1,0:T(8,128)(2,1)S(1)} %collective-permute-done.14.refs_6_), channel_id=1, source_target_pairs={{0,1},{1,0},{2,3},{3,2},{4,5},{5,4},{6,7},{7,6},{8,9},{9,8},{10,11... | collective-permute-start | bytes 884744 | tf_op jit(solution)/shard_map/ppermute | solution.py:586
  31.3 9.4 %collective-permute-start.2 = (bf16[96,1536]{1,0:T(8,128)(2,1)S(1)}, bf16[96,1536]{1,0:T(8,128)(2,1)S(1)}, u32[]{:S(2)}, u32[]{:S(2)}) collective-permute-start(bf16[96,1536]{1,0:T(8,128)(2,1)S(1)} %collective-permute-done.1.refs_2_), channel_id=1, source_target_pairs={{0,16},{16,0},{1,17},{17,1},{2,18},{18,2},{3,19},{19,3},{4,20},{20... | collective-permute-start | bytes 884744 | tf_op jit(solution)/shard_map/ppermute | solution.py:586
  33.0 8.1 %collective-permute-start.12 = (bf16[192,768]{1,0:T(8,128)(2,1)S(1)}, bf16[192,768]{1,0:T(8,128)(2,1)S(1)}, u32[]{:S(2)}, u32[]{:S(2)}) collective-permute-start(bf16[192,768]{1,0:T(8,128)(2,1)S(1)} %collective-permute-done.11.refs_2_), channel_id=1, source_target_pairs={{0,1},{1,0},{2,3},{3,2},{4,5},{5,4},{6,7},{7,6},{8,9},{9,8},{10,11... | collective-permute-start | bytes 884744 | tf_op jit(solution)/shard_map/ppermute | solution.py:586
  35.3 1.3 %copy-start.4 = (s32[1,128]{1,0:T(1,128)S(1)}, s32[1,128]{1,0:T(1,128)}, u32[]{:S(2)}) copy-start(s32[1,128]{1,0:T(1,128)} %active_ref.1) | copy-start | bytes 1540
  37.9 13.6 %copy-start.3 = (s32[1,512]{1,0:T(1,128)S(1)}, s32[1,512]{1,0:T(1,128)}, u32[]{:S(2)}) copy-start(s32[1,512]{1,0:T(1,128)} %param.14) | copy-start | bytes 6148
  38.0 12.5 %collective-permute-start.10 = (bf16[776,128]{1,0:T(8,128)(2,1)S(1)}, bf16[776,128]{1,0:T(8,128)(2,1)S(1)}, u32[]{:S(2)}, u32[]{:S(2)}) collective-permute-start(bf16[776,128]{1,0:T(8,128)(2,1)S(1)} %back.1.refs_6_.refs_0_), channel_id=1, source_target_pairs={{0,8},{4,12},{8,0},{12,4},{1,9},{5,13},{9,1},{13,5},{2,10},{6,14},... | collective-permute-start | bytes 595976 | tf_op jit(solution)/shard_map/ppermute | solution.py:586
  40.6 10.9 %collective-permute-start.3 = (bf16[96,1536]{1,0:T(8,128)(2,1)S(1)}, bf16[96,1536]{1,0:T(8,128)(2,1)S(1)}, u32[]{:S(2)}, u32[]{:S(2)}) collective-permute-start(bf16[96,1536]{1,0:T(8,128)(2,1)S(1)} %collective-permute-done.1.refs_2_), channel_id=1, source_target_pairs={{0,1},{1,0},{2,3},{3,2},{4,5},{5,4},{6,7},{7,6},{8,9},{9,8},{10,11... | collective-permute-start | bytes 884744 | tf_op jit(solution)/shard_map/ppermute | solution.py:586
  40.7 10.8 %collective-permute-start.4 = (bf16[96,1536]{1,0:T(8,128)(2,1)S(1)}, bf16[96,1536]{1,0:T(8,128)(2,1)S(1)}, u32[]{:S(2)}, u32[]{:S(2)}) collective-permute-start(bf16[96,1536]{1,0:T(8,128)(2,1)S(1)} %collective-permute-done.2.refs_3_), channel_id=1, source_target_pairs={{0,1},{1,0},{2,3},{3,2},{4,5},{5,4},{6,7},{7,6},{8,9},{9,8},{10,11... | collective-permute-start | bytes 884744 | tf_op jit(solution)/shard_map/ppermute | solution.py:586
  41.1 10.4 %collective-permute-start.9 = (bf16[776,128]{1,0:T(8,128)(2,1)S(1)}, bf16[776,128]{1,0:T(8,128)(2,1)S(1)}, u32[]{:S(2)}, u32[]{:S(2)}) collective-permute-start(bf16[776,128]{1,0:T(8,128)(2,1)S(1)} %back.1.refs_6_.refs_0_), channel_id=1, source_target_pairs={{0,4},{4,0},{8,12},{12,8},{1,5},{5,1},{9,13},{13,9},{2,6},{6,2},{1... | collective-permute-start | bytes 595976 | tf_op jit(solution)/shard_map/ppermute | solution.py:586
  50.4 6.2 %collective-permute-start.16 = (bf16[776,128]{1,0:T(8,128)(2,1)S(1)}, bf16[776,128]{1,0:T(8,128)(2,1)S(1)}, u32[]{:S(2)}, u32[]{:S(2)}) collective-permute-start(bf16[776,128]{1,0:T(8,128)(2,1)S(1)} %collective-permute-done.10.refs_2_), channel_id=1, source_target_pairs={{0,4},{4,0},{8,12},{12,8},{1,5},{5,1},{9,13},{13,9},{2,6},{6,2},{1... | collective-permute-start | bytes 595976 | tf_op jit(solution)/shard_map/ppermute | solution.py:586

commit v8 on v6

--- a/solution.py
+++ b/solution.py
@@ -194,10 +194,11 @@
 ):
     out_ref, all1, all2, patch = refs[-4:]
     splitter = split_matrix()
-    odd = got_ref[channels : 2 * channels, :].astype(F32)
-    all1[:channels, :] = later(odd).astype(BF)
-    all1[channels:, :] = got_ref[: 2 * channels, :]
-    even, odd = split_time(got_ref[2 * channels :, :], splitter)
+    got = got_ref[...]
+    got = jnp.where(lax.axis_index("seq") > 0, got, jnp.zeros_like(got))
+    all1[:channels, :] = later(got[channels : 2 * channels].astype(F32)).astype(BF)
+    all1[channels:, :] = got[: 2 * channels]
+    even, odd = split_time(got[2 * channels :], splitter)
     store_taps(all2, 0, even, odd)
     first = silu(first_ref[...] + dot(k1_ref[: 3 * channels, :], all1[...], 0, 0)).astype(BF)
     even, odd = split_time(first, splitter)
@@ -264,10 +265,23 @@
     return position ^ slot if swap else slot
 
 
-def prepare_kernel(order_ref, *refs, pieces, chunks, swap):
+def place_kernel(order_ref, perm_ref, *, swap):
+    shards, count = order_ref.shape
+    square = iota((count, count), 0) == iota((count, count), 1)
+    lane = iota((1, count), 1)
+    labels = jnp.concatenate([lane + place_of(slot, swap) * count for slot in range(shards)], axis=1)
+    labels = labels.astype(F32)
+    for slot in range(shards):
+        row = order_ref[pl.ds(place_of(slot, swap), 1), :].astype(F32)
+        across = jnp.broadcast_to(row, (count, count))
+        down = jnp.sum(jnp.where(square, across, 0.0), axis=1, keepdims=True)
+        perm_ref[slot * count : (slot + 1) * count, :] = one_hot(labels == down)
+
+
+def prepare_kernel(*refs, pieces, chunks):
     kv_refs = refs[:pieces]
     chunk_refs = refs[pieces : pieces + chunks]
-    joined, normed, keys, values, perm_ref, sems = refs[pieces + chunks :]
+    joined, normed, keys, values, sems = refs[pieces + chunks :]
     width = joined.shape[0]
     if pieces > 1:
         own, beside, near, far, near_corner, far_corner = kv_refs
@@ -284,17 +298,8 @@
     else:
         sources = [(kv_refs[0], 0, width, 1)]
     copies = collect(sources, joined, sems)
-    shards, count = order_ref.shape
-    square = iota((count, count), 0) == iota((count, count), 1)
-    lane = iota((1, count), 1)
-    labels = jnp.concatenate([lane + place_of(slot, swap) * count for slot in range(shards)], axis=1)
-    labels = labels.astype(F32)
-    for slot in range(shards):
-        row = order_ref[pl.ds(place_of(slot, swap), 1), :].astype(F32)
-        across = jnp.broadcast_to(row, (count, count))
-        down = jnp.sum(jnp.where(square, across, 0.0), axis=1, keepdims=True)
-        perm_ref[slot * count : (slot + 1) * count, :] = one_hot(labels == down)
     for slot, ref in enumerate(chunk_refs):
+        count = ref.shape[1]
         normed[slot * count : (slot + 1) * count, :] = normal(tokens_of(ref))
     for copy in copies:
         copy.wait()
@@ -505,19 +510,30 @@
     )(got, k1, k2, active, *parts)
 
 
-def prepare(order, weights, chunks, swap):
-    shards, count = order.shape
+def place(order, swap):
+    size = order.shape[0] * order.shape[1]
+    return pl.pallas_call(
+        functools.partial(place_kernel, swap=swap),
+        out_shape=array((size, size)),
+        in_specs=[vmem()],
+        out_specs=vmem(),
+        compiler_params=params(4 + size // 256),
+        name="place",
+    )(order)
+
+
+def prepare(weights, chunks):
     width = chunks[0].shape[0] - EXTRA
-    size, near = shards * count, len(chunks) * count
-    return pl.pallas_call(
-        functools.partial(prepare_kernel, pieces=len(weights), chunks=len(chunks), swap=swap),
-        out_shape=(array((width, 2 * width)),) + (array((near, width)),) * 2 + (array((near, 2 * width)), array((size, size))),
-        in_specs=[vmem()] + [fixed()] + [hbm()] * (len(weights) - 1) + [vmem()] * len(chunks),
-        out_specs=[vmem()] * 5,
+    near = len(chunks) * chunks[0].shape[1]
+    return pl.pallas_call(
+        functools.partial(prepare_kernel, pieces=len(weights), chunks=len(chunks)),
+        out_shape=(array((width, 2 * width)),) + (array((near, width)),) * 2 + (array((near, 2 * width)),),
+        in_specs=[fixed()] + [hbm()] * (len(weights) - 1) + [vmem()] * len(chunks),
+        out_specs=[vmem()] * 4,
         scratch_shapes=[pltpu.SemaphoreType.DMA((len(weights),))],
-        compiler_params=params(8 + size // 128),
+        compiler_params=params(8 + near // 64),
         name="prepare",
-    )(order, *weights, *chunks)
+    )(*weights, *chunks)
 
 
 def extend(ready, chunks, weights, early, swap):
@@ -608,7 +624,7 @@
     else:
         embeds = [lax.all_gather(embed_weight, ("mp", "section"), axis=0, tiled=True)]
         msg, rows, k1, k2 = front(rows, k1, k2, wires, ())
-    got = lax.ppermute(msg, "seq", [(i, i + 1) for i in range(shards - 1)])
+    got = lax.ppermute(msg, "seq", [(i, (i + 1) % shards) for i in range(shards)])
     first, second, patch = central(msg, rows, k1, k2, wires, count)
     token, low = mix(patch, embeds)
     parts = [first, second, token, low]
@@ -642,7 +658,8 @@
         query_weights = kv_weights
         output_weights = [lax.all_gather(output_weight, ("mp", "section"), axis=0, tiled=True)]
     early, later = shards // 2, shards // 2 + shards // 4
-    ready = prepare(order, kv_weights, chunks[:early], swap)
+    perm = place(order, swap)
+    ready = (*prepare(kv_weights, chunks[:early]), perm)
     extra = extend(ready, chunks[:later], query_weights, early, swap)
     output = gather(output_weights)
     result = finish(ready, extra, output, chunks[later:], swap)

time: 60.4 us -> 60.4 us (level)
  starting transfers between devices: 17.7 us -> 15.8 us
  waiting for transfers between devices: 28.6 us -> 30.4 us
    ppermute x1, starting transfers between devices: 4 us -> 2.09 us  [layer(): lax.ppermute(msg, 'seq', [(i, (i + 1) % shards) for i in range(shards)])]
    ppermute x16, waiting for transfers between devices: 27.3 us -> 28.2 us  [exchanged(): return lax.ppermute(value, axis, [(i, i ^ flip) for i in range(count)])]
    ppermute x1, waiting for transfers between devices: 1.29 us -> 2.17 us  [layer(): lax.ppermute(msg, 'seq', [(i, (i + 1) % shards) for i in range(shards)])]
  transfers between devices with their start and end apart: 17 -> 17, of which waited for: 8 -> 7; matrix products, arithmetic and copies ran while one was open for 0% -> 0% of each run, Pallas kernels for 17% -> 17%
where the time goes in v8:
time: 60.4 us; the launch traced here: 60.3 us
  waiting for transfers between devices  30.4 us (50%)
  starting transfers between devices  15.8 us (26%)
  Pallas kernels  14 us (23%)
    ppermute x16, waiting for transfers between devices, exchanged(): return lax.ppermute(value, axis, [(i, i ^ flip) for i in range(count)])  28.2 us
    ppermute x16, starting transfers between devices, exchanged(): return lax.ppermute(value, axis, [(i, i ^ flip) for i in range(count)])  13.7 us
    pallas_call x1, Pallas kernels, finish(): pl.pallas_call(functools.partial(finish_kernel, chunks=len(chunks), swap=...  3.8 us
    pallas_call x1, Pallas kernels, front(): pl.pallas_call(functools.partial(front_kernel, wires=wires, channels=chan...  2.39 us
    ppermute x1, waiting for transfers between devices, layer(): lax.ppermute(msg, 'seq', [(i, (i + 1) % shards) for i in range(shards)])  2.17 us
    ppermute x1, starting transfers between devices, layer(): lax.ppermute(msg, 'seq', [(i, (i + 1) % shards) for i in range(shards)])  2.09 us
    pallas_call x1, Pallas kernels, central(): pl.pallas_call(functools.partial(central_kernel, wires=wires, channels=ch...  2.03 us
    pallas_call x1, Pallas kernels, prepare(): pl.pallas_call(functools.partial(prepare_kernel, pieces=len(weights), chu...  1.48 us
  transfers between devices with their start and end apart: 17, of which 7 were waited for; matrix products, arithmetic and copies ran while one was open for 0% of the time, Pallas kernels for 17%

profile of v8, /device:TPU:0, one launch (start us, length us, event | category | flops | bytes accessed | tf_op | source)
XLA Modules:
  0.0 60.3 jit_solution(10759770080935938333)
XLA Ops:
  0.0 3.0 %collective-permute-start.7 = (bf16[256,768]{1,0:T(8,128)(2,1)}, bf16[256,768]{1,0:T(8,128)(2,1)S(1)}, u32[]{:S(2)}, u32[]{:S(2)}) collective-permute-start(bf16[256,768]{1,0:T(8,128)(2,1)} %refs_0_.5), channel_id=1, source_target_pairs={{0,2},{2,0},{1,3},{3,1},{4,6},{6,4},{5,7},{7,5},{8,10},{10,8},{9,1... | collective-permute-start | bytes 1179656 | tf_op jit(solution)/shard_map/ppermute | solution.py:603
  3.0 2.4 %front.1 = (bf16[256,512]{1,0:T(8,128)(2,1)S(1)}, bf16[512,1024]{1,0:T(8,128)(2,1)S(1)}, bf16[576,128]{1,0:T(8,128)(2,1)S(1)}, bf16[1152,256]{1,0:T(8,128)(2,1)S...) custom-call(bf16[512,1024]{1,0:T(8,128)(2,1)} %bitcast.6, bf16[576,128]{1,0:T(8,128)(2,1)} %bitcast.8, ...), custom_call_target="tpu_custom_call" | custom-call | tf_op jit(solution)/shard_map/front/pallas_call | solution.py:430
  5.5 2.1 %collective-permute-start.5 = (bf16[256,512]{1,0:T(8,128)(2,1)S(1)}, bf16[256,512]{1,0:T(8,128)(2,1)S(1)}, u32[]{:S(2)}, u32[]{:S(2)}) collective-permute-start(bf16[256,512]{1,0:T(8,128)(2,1)S(1)} %get-tuple-element.29.msg_ref), channel_id=1, source_target_pairs={{0,4},{4,8},{8,12},{12,0},{1,5},{5,9},{9,13},{13,1},{2,6},{6,10},{... | collective-permute-start | bytes 786440 | tf_op jit(solution)/shard_map/ppermute | solution.py:627
  7.5 1.5 %collective-permute-start.11 = (bf16[192,768]{1,0:T(8,128)(2,1)S(1)}, bf16[192,768]{1,0:T(8,128)(2,1)S(1)}, u32[]{:S(2)}, u32[]{:S(2)}) collective-permute-start(bf16[192,768]{1,0:T(8,128)(2,1)S(1)} %get-tuple-element.44), channel_id=1, source_target_pairs={{0,2},{2,0},{1,3},{3,1},{4,6},{6,4},{5,7},{7,5},{8,10},{10,8},{9,1... | collective-permute-start | bytes 884744 | tf_op jit(solution)/shard_map/ppermute | solution.py:603
  9.0 4.1 %collective-permute-done.7.refs_2_ = bf16[256,768]{1,0:T(8,128)(2,1)S(1)} collective-permute-done((bf16[256,768]{1,0:T(8,128)(2,1)}, bf16[256,768]{1,0:T(8,128)(2,1)S(1)}, u32[]{:S(2)}, u32[]{:S(2)}) %collective-permute-start.7) | collective-permute-done | bytes 393248 | tf_op jit(solution)/shard_map/ppermute | solution.py:603
  13.1 2.2 %collective-permute-done.5.got_ref = bf16[256,512]{1,0:T(8,128)(2,1)S(1)} collective-permute-done((bf16[256,512]{1,0:T(8,128)(2,1)S(1)}, bf16[256,512]{1,0:T(8,128)(2,1)S(1)}, u32[]{:S(2)}, u32[]{:S(2)}) %collective-permute-start.5) | collective-permute-done | bytes 262176 | tf_op jit(solution)/shard_map/ppermute | solution.py:627
  15.3 1.5 %collective-permute-start.14 = (bf16[192,768]{1,0:T(8,128)(2,1)S(1)}, bf16[192,768]{1,0:T(8,128)(2,1)S(1)}, u32[]{:S(2)}, u32[]{:S(2)}) collective-permute-start(bf16[192,768]{1,0:T(8,128)(2,1)S(1)} %copy-done.2), channel_id=1, source_target_pairs={{0,2},{2,0},{1,3},{3,1},{4,6},{6,4},{5,7},{7,5},{8,10},{10,8},{9,1... | collective-permute-start | bytes 884744 | tf_op jit(solution)/shard_map/ppermute | solution.py:603
  16.8 2.6 %collective-permute-done.1.refs_2_ = bf16[96,1536]{1,0:T(8,128)(2,1)S(1)} collective-permute-done((bf16[96,1536]{1,0:T(8,128)(2,1)S(1)}, bf16[96,1536]{1,0:T(8,128)(2,1)S(1)}, u32[]{:S(2)}, u32[]{:S(2)}) %collective-permute-start.1) | collective-permute-done | bytes 294944 | tf_op jit(solution)/shard_map/ppermute | solution.py:603
  19.5 6.3 %collective-permute-done.11.refs_5_ = bf16[192,768]{1,0:T(8,128)(2,1)S(1)} collective-permute-done((bf16[192,768]{1,0:T(8,128)(2,1)S(1)}, bf16[192,768]{1,0:T(8,128)(2,1)S(1)}, u32[]{:S(2)}, u32[]{:S(2)}) %collective-permute-start.11) | collective-permute-done | bytes 294944 | tf_op jit(solution)/shard_map/ppermute | solution.py:603
  25.8 5.5 %collective-permute-done.14.refs_2_ = bf16[192,768]{1,0:T(8,128)(2,1)S(1)} collective-permute-done((bf16[192,768]{1,0:T(8,128)(2,1)S(1)}, bf16[192,768]{1,0:T(8,128)(2,1)S(1)}, u32[]{:S(2)}, u32[]{:S(2)}) %collective-permute-start.14) | collective-permute-done | bytes 294944 | tf_op jit(solution)/shard_map/ppermute | solution.py:603
  31.2 1.8 %collective-permute-start.2 = (bf16[96,1536]{1,0:T(8,128)(2,1)S(1)}, bf16[96,1536]{1,0:T(8,128)(2,1)S(1)}, u32[]{:S(2)}, u32[]{:S(2)}) collective-permute-start(bf16[96,1536]{1,0:T(8,128)(2,1)S(1)} %collective-permute-done.1.refs_2_), channel_id=1, source_target_pairs={{0,16},{16,0},{1,17},{17,1},{2,18},{18,2},{3,19},{19,3},{4,20},{20... | collective-permute-start | bytes 884744 | tf_op jit(solution)/shard_map/ppermute | solution.py:603
  33.0 0.5 collective-permute-start.15
  33.5 2.0 %central.1 = (f32[128,512]{1,0:T(8,128)S(1)}, f32[256,256]{1,0:T(8,128)S(1)}, bf16[512,128]{1,0:T(8,128)(2,1)S(1)}) custom-call(bf16[256,512]{1,0:T(8,128)(2,1)S(1)} %get-tuple-element.29.msg_ref, bf16[512,1024]{1,0:T(8,128)(2,1)S(1)} %get-tuple-element.32.x_ref, bf16[576,128]{1,0:T(8,128)(2,1)S(1)} %get-tuple-element.30.k1_ref, ...), custom_call_target="tpu_custom_call" | custom-call | tf_op jit(solution)/shard_map/central/pallas_call | solution.py:450
  35.6 0.8 %mix.1 = (f32[128,768]{1,0:T(8,128)S(1)}, bf16[512,768]{1,0:T(8,128)(2,1)S(1)}) custom-call(bf16[512,128]{1,0:T(8,128)(2,1)S(1)} %get-tuple-element.35.patch, bf16[256,768]{1,0:T(8,128)(2,1)S(1)} %copy-done.1, bf16[256,768]{1,0:T(8,128)(2,1)S(1)} %collective-permute-done.6.refs_1_, bf16[256,768]{1,0:T(8,128)(2,1)S(1)} %collective-permute-done.7.refs_2_), custom_call_target="tpu_custom_call" | custom-call | tf_op jit(solution)/shard_map/mix/pallas_call | solution.py:470
  36.9 1.3 %back.1.refs_6_.refs_0_ = bf16[776,128]{1,0:T(8,128)(2,1)S(1)} custom-call(bf16[256,512]{1,0:T(8,128)(2,1)S(1)} %collective-permute-done.5.got_ref, bf16[576,128]{1,0:T(8,128)(2,1)S(1)} %get-tuple-element.30.k1_ref, bf16[1152,256]{1,0:T(8,128)(2,1)S(1)} %get-tuple-element.31.k2_ref, s32[1,128]{1,0:T(1,128)S(1)} %copy-done.4, ...), custom_call_target="tpu_custom_call" | custom-call | tf_op jit(solution)/shard_map/back/pallas_call | solution.py:498
  38.2 2.7 %collective-permute-start.10 = (bf16[776,128]{1,0:T(8,128)(2,1)S(1)}, bf16[776,128]{1,0:T(8,128)(2,1)S(1)}, u32[]{:S(2)}, u32[]{:S(2)}) collective-permute-start(bf16[776,128]{1,0:T(8,128)(2,1)S(1)} %back.1.refs_6_.refs_0_), channel_id=1, source_target_pairs={{0,8},{4,12},{8,0},{12,4},{1,9},{5,13},{9,1},{13,5},{2,10},{6,14},... | collective-permute-start | bytes 595976 | tf_op jit(solution)/shard_map/ppermute | solution.py:603
  40.9 0.5 collective-permute-start.12
  41.4 1.6 %collective-permute-start.9 = (bf16[776,128]{1,0:T(8,128)(2,1)S(1)}, bf16[776,128]{1,0:T(8,128)(2,1)S(1)}, u32[]{:S(2)}, u32[]{:S(2)}) collective-permute-start(bf16[776,128]{1,0:T(8,128)(2,1)S(1)} %back.1.refs_6_.refs_0_), channel_id=1, source_target_pairs={{0,4},{4,0},{8,12},{12,8},{1,5},{5,1},{9,13},{13,9},{2,6},{6,2},{1... | collective-permute-start | bytes 595976 | tf_op jit(solution)/shard_map/ppermute | solution.py:603
  43.0 7.5 %collective-permute-done.10.refs_2_ = bf16[776,128]{1,0:T(8,128)(2,1)S(1)} collective-permute-done((bf16[776,128]{1,0:T(8,128)(2,1)S(1)}, bf16[776,128]{1,0:T(8,128)(2,1)S(1)}, u32[]{:S(2)}, u32[]{:S(2)}) %collective-permute-start.10) | collective-permute-done | bytes 198688 | tf_op jit(solution)/shard_map/ppermute | solution.py:603
  50.5 0.6 %collective-permute-start.16 = (bf16[776,128]{1,0:T(8,128)(2,1)S(1)}, bf16[776,128]{1,0:T(8,128)(2,1)S(1)}, u32[]{:S(2)}, u32[]{:S(2)}) collective-permute-start(bf16[776,128]{1,0:T(8,128)(2,1)S(1)} %collective-permute-done.10.refs_2_), channel_id=1, source_target_pairs={{0,4},{4,0},{8,12},{12,8},{1,5},{5,1},{9,13},{13,9},{2,6},{6,2},{1... | collective-permute-start | bytes 595976 | tf_op jit(solution)/shard_map/ppermute | solution.py:603
  51.6 1.5 %prepare.1 = (bf16[768,1536]{1,0:T(8,128)(2,1)S(1)}, bf16[256,768]{1,0:T(8,128)(2,1)S(1)}, bf16[256,768]{1,0:T(8,128)(2,1)S(1)}, bf16[256,1536]{1,0:T(8,128)(2,1)S(1)}) custom-call(bf16[192,2304]{1,0:T(8,128)(2,1)S(1)} %copy-done, bf16[192,2304]{1,0:T(8,128)(2,1)S(1)} %collective-permute-done.refs_1_.refs_4_, ...), custom_call_target="tpu_custom_call" | custom-call | tf_op jit(solution)/shard_map/prepare/pallas_call | solution.py:528
  53.1 1.2 %extend.1 = (bf16[768,768]{1,0:T(8,128)(2,1)S(1)}, bf16[128,768]{1,0:T(8,128)(2,1)S(1)}, bf16[128,1536]{1,0:T(8,128)(2,1)S(1)}, f32[128,768]{1,0:T(8,128)S(1)}, ...) custom-call(bf16[512,512]{1,0:T(8,128)(2,1)S(1)} %place.1.perm_ref, bf16[768,1536]{1,0:T(8,128)(2,1)S(1)} %get-tuple-element.40.joined, ...), custom_call_target="tpu_custom_call" | custom-call | tf_op jit(solution)/shard_map/extend/pallas_call | solution.py:546
  54.3 2.2 %collective-permute-done.16.refs_0_ = bf16[776,128]{1,0:T(8,128)(2,1)S(1)} collective-permute-done((bf16[776,128]{1,0:T(8,128)(2,1)S(1)}, bf16[776,128]{1,0:T(8,128)(2,1)S(1)}, u32[]{:S(2)}, u32[]{:S(2)}) %collective-permute-start.16) | collective-permute-done | bytes 198688 | tf_op jit(solution)/shard_map/ppermute | solution.py:603
  56.5 3.8 %finish.1 = bf16[128,768]{1,0:T(8,128)(2,1)} custom-call(bf16[512,512]{1,0:T(8,128)(2,1)S(1)} %place.1.perm_ref, bf16[768,1536]{1,0:T(8,128)(2,1)S(1)} %get-tuple-element.40.joined, bf16[256,768]{1,0:T(8,128)(2,1)S(1)} %get-tuple-element.41.keys0, bf16[256,1536]{1,0:T(8,128)(2,1)S(1)} %get-tuple-element.42.values0, ...), custom_call_target="tpu_custom_call" | custom-call | tf_op jit(solution)/shard_map/finish/pallas_call | solution.py:584
  (30 shorter events, 1.1 us)
Async XLA Ops:
  0.0 13.1 %collective-permute-start.7 = (bf16[256,768]{1,0:T(8,128)(2,1)}, bf16[256,768]{1,0:T(8,128)(2,1)S(1)}, u32[]{:S(2)}, u32[]{:S(2)}) collective-permute-start(bf16[256,768]{1,0:T(8,128)(2,1)} %refs_0_.5), channel_id=1, source_target_pairs={{0,2},{2,0},{1,3},{3,1},{4,6},{6,4},{5,7},{7,5},{8,10},{10,8},{9,1... | collective-permute-start | bytes 1179656 | tf_op jit(solution)/shard_map/ppermute | solution.py:603
  3.0 6.1 %copy-start.1 = (bf16[256,768]{1,0:T(8,128)(2,1)S(1)}, bf16[256,768]{1,0:T(8,128)(2,1)}, u32[]{:S(2)}) copy-start(bf16[256,768]{1,0:T(8,128)(2,1)} %refs_0_.5) | copy-start | bytes 1179652
  3.0 12.3 %copy-start.2 = (bf16[192,768]{1,0:T(8,128)(2,1)S(1)}, bf16[192,768]{1,0:T(8,128)(2,1)}, u32[]{:S(2)}) copy-start(bf16[192,768]{1,0:T(8,128)(2,1)} %refs_0_.7) | copy-start | bytes 884740
  3.0 16.5 %copy-start = (bf16[192,2304]{1,0:T(8,128)(2,1)S(1)}, bf16[192,2304]{1,0:T(8,128)(2,1)}, u32[]{:S(2)}) copy-start(bf16[192,2304]{1,0:T(8,128)(2,1)} %refs_3_.1) | copy-start | bytes 2654212
  5.4 14.1 %collective-permute-start.1 = (bf16[96,1536]{1,0:T(8,128)(2,1)S(1)}, bf16[96,1536]{1,0:T(8,128)(2,1)S(1)}, u32[]{:S(2)}, u32[]{:S(2)}) collective-permute-start(bf16[96,1536]{1,0:T(8,128)(2,1)S(1)} %get-tuple-element.28), channel_id=1, source_target_pairs={{0,2},{2,0},{1,3},{3,1},{4,6},{6,4},{5,7},{7,5},{8,10},{10,8},{9,1... | collective-permute-start | bytes 884744 | tf_op jit(solution)/shard_map/ppermute | solution.py:603
  5.5 9.9 %collective-permute-start.5 = (bf16[256,512]{1,0:T(8,128)(2,1)S(1)}, bf16[256,512]{1,0:T(8,128)(2,1)S(1)}, u32[]{:S(2)}, u32[]{:S(2)}) collective-permute-start(bf16[256,512]{1,0:T(8,128)(2,1)S(1)} %get-tuple-element.29.msg_ref), channel_id=1, source_target_pairs={{0,4},{4,8},{8,12},{12,0},{1,5},{5,9},{9,13},{13,1},{2,6},{6,10},{... | collective-permute-start | bytes 786440 | tf_op jit(solution)/shard_map/ppermute | solution.py:627
  7.5 18.2 %collective-permute-start.11 = (bf16[192,768]{1,0:T(8,128)(2,1)S(1)}, bf16[192,768]{1,0:T(8,128)(2,1)S(1)}, u32[]{:S(2)}, u32[]{:S(2)}) collective-permute-start(bf16[192,768]{1,0:T(8,128)(2,1)S(1)} %get-tuple-element.44), channel_id=1, source_target_pairs={{0,2},{2,0},{1,3},{3,1},{4,6},{6,4},{5,7},{7,5},{8,10},{10,8},{9,1... | collective-permute-start | bytes 884744 | tf_op jit(solution)/shard_map/ppermute | solution.py:603
  9.0 24.0 %collective-permute-start.6 = (bf16[256,768]{1,0:T(8,128)(2,1)S(1)}, bf16[256,768]{1,0:T(8,128)(2,1)S(1)}, u32[]{:S(2)}, u32[]{:S(2)}) collective-permute-start(bf16[256,768]{1,0:T(8,128)(2,1)S(1)} %copy-done.1), channel_id=1, source_target_pairs={{0,1},{1,0},{2,3},{3,2},{4,5},{5,4},{6,7},{7,6},{8,9},{9,8},{10,11... | collective-permute-start | bytes 1179656 | tf_op jit(solution)/shard_map/ppermute | solution.py:603
  13.1 19.9 %collective-permute-start.8 = (bf16[256,768]{1,0:T(8,128)(2,1)S(1)}, bf16[256,768]{1,0:T(8,128)(2,1)S(1)}, u32[]{:S(2)}, u32[]{:S(2)}) collective-permute-start(bf16[256,768]{1,0:T(8,128)(2,1)S(1)} %collective-permute-done.7.refs_2_), channel_id=1, source_target_pairs={{0,1},{1,0},{2,3},{3,2},{4,5},{5,4},{6,7},{7,6},{8,9},{9,8},{10,11... | collective-permute-start | bytes 1179656 | tf_op jit(solution)/shard_map/ppermute | solution.py:603
  15.3 15.9 %collective-permute-start.14 = (bf16[192,768]{1,0:T(8,128)(2,1)S(1)}, bf16[192,768]{1,0:T(8,128)(2,1)S(1)}, u32[]{:S(2)}, u32[]{:S(2)}) collective-permute-start(bf16[192,768]{1,0:T(8,128)(2,1)S(1)} %copy-done.2), channel_id=1, source_target_pairs={{0,2},{2,0},{1,3},{3,1},{4,6},{6,4},{5,7},{7,5},{8,10},{10,8},{9,1... | collective-permute-start | bytes 884744 | tf_op jit(solution)/shard_map/ppermute | solution.py:603
  19.5 32.1 %collective-permute-start = (bf16[192,2304]{1,0:T(8,128)(2,1)S(1)}, bf16[192,2304]{1,0:T(8,128)(2,1)S(1)}, u32[]{:S(2)}, u32[]{:S(2)}) collective-permute-start(bf16[192,2304]{1,0:T(8,128)(2,1)S(1)} %copy-done), channel_id=1, source_target_pairs={{0,1},{1,0},{2,3},{3,2},{4,5},{5,4},{6,7},{7,6},{8,9},{9,8},{10,11... | collective-permute-start | bytes 2654216 | tf_op jit(solution)/shard_map/ppermute | solution.py:603
  25.8 12.4 %collective-permute-start.13 = (bf16[192,768]{1,0:T(8,128)(2,1)S(1)}, bf16[192,768]{1,0:T(8,128)(2,1)S(1)}, u32[]{:S(2)}, u32[]{:S(2)}) collective-permute-start(bf16[192,768]{1,0:T(8,128)(2,1)S(1)} %copy-done.2), channel_id=1, source_target_pairs={{0,1},{1,0},{2,3},{3,2},{4,5},{5,4},{6,7},{7,6},{8,9},{9,8},{10,11... | collective-permute-start | bytes 884744 | tf_op jit(solution)/shard_map/ppermute | solution.py:603
  31.2 9.7 %collective-permute-start.2 = (bf16[96,1536]{1,0:T(8,128)(2,1)S(1)}, bf16[96,1536]{1,0:T(8,128)(2,1)S(1)}, u32[]{:S(2)}, u32[]{:S(2)}) collective-permute-start(bf16[96,1536]{1,0:T(8,128)(2,1)S(1)} %collective-permute-done.1.refs_2_), channel_id=1, source_target_pairs={{0,16},{16,0},{1,17},{17,1},{2,18},{18,2},{3,19},{19,3},{4,20},{20... | collective-permute-start | bytes 884744 | tf_op jit(solution)/shard_map/ppermute | solution.py:603
  33.0 7.9 %collective-permute-start.3 = (bf16[96,1536]{1,0:T(8,128)(2,1)S(1)}, bf16[96,1536]{1,0:T(8,128)(2,1)S(1)}, u32[]{:S(2)}, u32[]{:S(2)}) collective-permute-start(bf16[96,1536]{1,0:T(8,128)(2,1)S(1)} %collective-permute-done.1.refs_2_), channel_id=1, source_target_pairs={{0,1},{1,0},{2,3},{3,2},{4,5},{5,4},{6,7},{7,6},{8,9},{9,8},{10,11... | collective-permute-start | bytes 884744 | tf_op jit(solution)/shard_map/ppermute | solution.py:603
  33.0 8.4 %collective-permute-start.15 = (bf16[192,768]{1,0:T(8,128)(2,1)S(1)}, bf16[192,768]{1,0:T(8,128)(2,1)S(1)}, u32[]{:S(2)}, u32[]{:S(2)}) collective-permute-start(bf16[192,768]{1,0:T(8,128)(2,1)S(1)} %collective-permute-done.14.refs_2_), channel_id=1, source_target_pairs={{0,1},{1,0},{2,3},{3,2},{4,5},{5,4},{6,7},{7,6},{8,9},{9,8},{10,11... | collective-permute-start | bytes 884744 | tf_op jit(solution)/shard_map/ppermute | solution.py:603
  35.6 1.3 %copy-start.4 = (s32[1,128]{1,0:T(1,128)S(1)}, s32[1,128]{1,0:T(1,128)}, u32[]{:S(2)}) copy-start(s32[1,128]{1,0:T(1,128)} %active_ref.1) | copy-start | bytes 1540
  36.9 14.2 %copy-start.3 = (s32[1,512]{1,0:T(1,128)S(1)}, s32[1,512]{1,0:T(1,128)}, u32[]{:S(2)}) copy-start(s32[1,512]{1,0:T(1,128)} %param.14) | copy-start | bytes 6148
  38.2 12.3 %collective-permute-start.10 = (bf16[776,128]{1,0:T(8,128)(2,1)S(1)}, bf16[776,128]{1,0:T(8,128)(2,1)S(1)}, u32[]{:S(2)}, u32[]{:S(2)}) collective-permute-start(bf16[776,128]{1,0:T(8,128)(2,1)S(1)} %back.1.refs_6_.refs_0_), channel_id=1, source_target_pairs={{0,8},{4,12},{8,0},{12,4},{1,9},{5,13},{9,1},{13,5},{2,10},{6,14},... | collective-permute-start | bytes 595976 | tf_op jit(solution)/shard_map/ppermute | solution.py:603
  40.9 10.7 %collective-permute-start.4 = (bf16[96,1536]{1,0:T(8,128)(2,1)S(1)}, bf16[96,1536]{1,0:T(8,128)(2,1)S(1)}, u32[]{:S(2)}, u32[]{:S(2)}) collective-permute-start(bf16[96,1536]{1,0:T(8,128)(2,1)S(1)} %collective-permute-done.2.refs_3_), channel_id=1, source_target_pairs={{0,1},{1,0},{2,3},{3,2},{4,5},{5,4},{6,7},{7,6},{8,9},{9,8},{10,11... | collective-permute-start | bytes 884744 | tf_op jit(solution)/shard_map/ppermute | solution.py:603
  40.9 12.2 %collective-permute-start.12 = (bf16[192,768]{1,0:T(8,128)(2,1)S(1)}, bf16[192,768]{1,0:T(8,128)(2,1)S(1)}, u32[]{:S(2)}, u32[]{:S(2)}) collective-permute-start(bf16[192,768]{1,0:T(8,128)(2,1)S(1)} %collective-permute-done.11.refs_5_), channel_id=1, source_target_pairs={{0,1},{1,0},{2,3},{3,2},{4,5},{5,4},{6,7},{7,6},{8,9},{9,8},{10,11... | collective-permute-start | bytes 884744 | tf_op jit(solution)/shard_map/ppermute | solution.py:603
  41.4 10.2 %collective-permute-start.9 = (bf16[776,128]{1,0:T(8,128)(2,1)S(1)}, bf16[776,128]{1,0:T(8,128)(2,1)S(1)}, u32[]{:S(2)}, u32[]{:S(2)}) collective-permute-start(bf16[776,128]{1,0:T(8,128)(2,1)S(1)} %back.1.refs_6_.refs_0_), channel_id=1, source_target_pairs={{0,4},{4,0},{8,12},{12,8},{1,5},{5,1},{9,13},{13,9},{2,6},{6,2},{1... | collective-permute-start | bytes 595976 | tf_op jit(solution)/shard_map/ppermute | solution.py:603
  50.5 6.0 %collective-permute-start.16 = (bf16[776,128]{1,0:T(8,128)(2,1)S(1)}, bf16[776,128]{1,0:T(8,128)(2,1)S(1)}, u32[]{:S(2)}, u32[]{:S(2)}) collective-permute-start(bf16[776,128]{1,0:T(8,128)(2,1)S(1)} %collective-permute-done.10.refs_2_), channel_id=1, source_target_pairs={{0,4},{4,0},{8,12},{12,8},{1,5},{5,1},{9,13},{13,9},{2,6},{6,2},{1... | collective-permute-start | bytes 595976 | tf_op jit(solution)/shard_map/ppermute | solution.py:603

commit v9 on v6

--- a/solution.py
+++ b/solution.py
@@ -194,10 +194,11 @@
 ):
     out_ref, all1, all2, patch = refs[-4:]
     splitter = split_matrix()
-    odd = got_ref[channels : 2 * channels, :].astype(F32)
-    all1[:channels, :] = later(odd).astype(BF)
-    all1[channels:, :] = got_ref[: 2 * channels, :]
-    even, odd = split_time(got_ref[2 * channels :, :], splitter)
+    got = got_ref[...]
+    got = jnp.where(lax.axis_index("seq") > 0, got, jnp.zeros_like(got))
+    all1[:channels, :] = later(got[channels : 2 * channels].astype(F32)).astype(BF)
+    all1[channels:, :] = got[: 2 * channels]
+    even, odd = split_time(got[2 * channels :], splitter)
     store_taps(all2, 0, even, odd)
     first = silu(first_ref[...] + dot(k1_ref[: 3 * channels, :], all1[...], 0, 0)).astype(BF)
     even, odd = split_time(first, splitter)
@@ -381,7 +382,7 @@
         weights = []
         for half in range(2):
             score = jnp.minimum(scores[half * count : (half + 1) * count], cap[...])
-            weights.append(jnp.exp(score - jnp.max(score, axis=-1, keepdims=True)).astype(BF))
+            weights.append(jnp.exp((score - jnp.max(score, axis=-1, keepdims=True)).astype(BF)))
         weights = jnp.concatenate(weights, axis=0)
         part, start = 0.0, 0
         there = slice(2 * pair * 2 * head, 2 * (pair + 1) * 2 * head)
@@ -608,7 +609,7 @@
     else:
         embeds = [lax.all_gather(embed_weight, ("mp", "section"), axis=0, tiled=True)]
         msg, rows, k1, k2 = front(rows, k1, k2, wires, ())
-    got = lax.ppermute(msg, "seq", [(i, i + 1) for i in range(shards - 1)])
+    got = lax.ppermute(msg, "seq", [(i, (i + 1) % shards) for i in range(shards)])
     first, second, patch = central(msg, rows, k1, k2, wires, count)
     token, low = mix(patch, embeds)
     parts = [first, second, token, low]

time: 60.4 us -> 60.4 us (level)
  starting transfers between devices: 17.7 us -> 15.8 us
  waiting for transfers between devices: 28.6 us -> 30.5 us
    ppermute x1, starting transfers between devices: 4 us -> 2.09 us  [layer(): lax.ppermute(msg, 'seq', [(i, (i + 1) % shards) for i in range(shards)])]
    ppermute x16, waiting for transfers between devices: 27.3 us -> 28.4 us  [exchanged(): return lax.ppermute(value, axis, [(i, i ^ flip) for i in range(count)])]
    ppermute x1, waiting for transfers between devices: 1.29 us -> 2.17 us  [layer(): lax.ppermute(msg, 'seq', [(i, (i + 1) % shards) for i in range(shards)])]
where the time goes in v9:
time: 60.4 us; the launch traced here: 60.2 us
  waiting for transfers between devices  30.5 us (50%)
  starting transfers between devices  15.8 us (26%)
  Pallas kernels  13.7 us (23%)
    ppermute x16, waiting for transfers between devices, exchanged(): return lax.ppermute(value, axis, [(i, i ^ flip) for i in range(count)])  28.4 us
    ppermute x16, starting transfers between devices, exchanged(): return lax.ppermute(value, axis, [(i, i ^ flip) for i in range(count)])  13.7 us
    pallas_call x1, Pallas kernels, finish(): pl.pallas_call(functools.partial(finish_kernel, chunks=len(chunks), swap=...  3.71 us
    pallas_call x1, Pallas kernels, front(): pl.pallas_call(functools.partial(front_kernel, wires=wires, channels=chan...  2.39 us
    ppermute x1, waiting for transfers between devices, layer(): lax.ppermute(msg, 'seq', [(i, (i + 1) % shards) for i in range(shards)])  2.17 us
    ppermute x1, starting transfers between devices, layer(): lax.ppermute(msg, 'seq', [(i, (i + 1) % shards) for i in range(shards)])  2.09 us
    pallas_call x1, Pallas kernels, central(): pl.pallas_call(functools.partial(central_kernel, wires=wires, channels=ch...  2.03 us
    pallas_call x1, Pallas kernels, prepare(): pl.pallas_call(functools.partial(prepare_kernel, pieces=len(weights), chu...  1.54 us
  transfers between devices with their start and end apart: 17, of which 8 were waited for; matrix products, arithmetic and copies ran while one was open for 0% of the time, Pallas kernels for 17%

profile of v9, /device:TPU:0, one launch (start us, length us, event | category | flops | bytes accessed | tf_op | source)
XLA Modules:
  0.0 60.2 jit_solution(15989662236759687951)
XLA Ops:
  0.0 3.0 %collective-permute-start.7 = (bf16[256,768]{1,0:T(8,128)(2,1)}, bf16[256,768]{1,0:T(8,128)(2,1)S(1)}, u32[]{:S(2)}, u32[]{:S(2)}) collective-permute-start(bf16[256,768]{1,0:T(8,128)(2,1)} %refs_0_.5), channel_id=1, source_target_pairs={{0,2},{2,0},{1,3},{3,1},{4,6},{6,4},{5,7},{7,5},{8,10},{10,8},{9,1... | collective-permute-start | bytes 1179656 | tf_op jit(solution)/shard_map/ppermute | solution.py:588
  3.0 2.4 %front.1 = (bf16[256,512]{1,0:T(8,128)(2,1)S(1)}, bf16[512,1024]{1,0:T(8,128)(2,1)S(1)}, bf16[576,128]{1,0:T(8,128)(2,1)S(1)}, bf16[1152,256]{1,0:T(8,128)(2,1)S...) custom-call(bf16[512,1024]{1,0:T(8,128)(2,1)} %bitcast.6, bf16[576,128]{1,0:T(8,128)(2,1)} %bitcast.8, ...), custom_call_target="tpu_custom_call" | custom-call | tf_op jit(solution)/shard_map/front/pallas_call | solution.py:426
  5.5 2.1 %collective-permute-start.5 = (bf16[256,512]{1,0:T(8,128)(2,1)S(1)}, bf16[256,512]{1,0:T(8,128)(2,1)S(1)}, u32[]{:S(2)}, u32[]{:S(2)}) collective-permute-start(bf16[256,512]{1,0:T(8,128)(2,1)S(1)} %get-tuple-element.30.msg_ref), channel_id=1, source_target_pairs={{0,4},{4,8},{8,12},{12,0},{1,5},{5,9},{9,13},{13,1},{2,6},{6,10},{... | collective-permute-start | bytes 786440 | tf_op jit(solution)/shard_map/ppermute | solution.py:612
  7.5 1.5 %collective-permute-start.11 = (bf16[192,768]{1,0:T(8,128)(2,1)S(1)}, bf16[192,768]{1,0:T(8,128)(2,1)S(1)}, u32[]{:S(2)}, u32[]{:S(2)}) collective-permute-start(bf16[192,768]{1,0:T(8,128)(2,1)S(1)} %get-tuple-element.46), channel_id=1, source_target_pairs={{0,2},{2,0},{1,3},{3,1},{4,6},{6,4},{5,7},{7,5},{8,10},{10,8},{9,1... | collective-permute-start | bytes 884744 | tf_op jit(solution)/shard_map/ppermute | solution.py:588
  9.0 4.1 %collective-permute-done.7.refs_2_ = bf16[256,768]{1,0:T(8,128)(2,1)S(1)} collective-permute-done((bf16[256,768]{1,0:T(8,128)(2,1)}, bf16[256,768]{1,0:T(8,128)(2,1)S(1)}, u32[]{:S(2)}, u32[]{:S(2)}) %collective-permute-start.7) | collective-permute-done | bytes 393248 | tf_op jit(solution)/shard_map/ppermute | solution.py:588
  13.1 2.2 %collective-permute-done.5.got_ref = bf16[256,512]{1,0:T(8,128)(2,1)S(1)} collective-permute-done((bf16[256,512]{1,0:T(8,128)(2,1)S(1)}, bf16[256,512]{1,0:T(8,128)(2,1)S(1)}, u32[]{:S(2)}, u32[]{:S(2)}) %collective-permute-start.5) | collective-permute-done | bytes 262176 | tf_op jit(solution)/shard_map/ppermute | solution.py:612
  15.3 1.5 %collective-permute-start.14 = (bf16[192,768]{1,0:T(8,128)(2,1)S(1)}, bf16[192,768]{1,0:T(8,128)(2,1)S(1)}, u32[]{:S(2)}, u32[]{:S(2)}) collective-permute-start(bf16[192,768]{1,0:T(8,128)(2,1)S(1)} %copy-done.2), channel_id=1, source_target_pairs={{0,2},{2,0},{1,3},{3,1},{4,6},{6,4},{5,7},{7,5},{8,10},{10,8},{9,1... | collective-permute-start | bytes 884744 | tf_op jit(solution)/shard_map/ppermute | solution.py:588
  16.8 2.6 %collective-permute-done.1.refs_2_ = bf16[96,1536]{1,0:T(8,128)(2,1)S(1)} collective-permute-done((bf16[96,1536]{1,0:T(8,128)(2,1)S(1)}, bf16[96,1536]{1,0:T(8,128)(2,1)S(1)}, u32[]{:S(2)}, u32[]{:S(2)}) %collective-permute-start.1) | collective-permute-done | bytes 294944 | tf_op jit(solution)/shard_map/ppermute | solution.py:588
  19.5 6.3 %collective-permute-done.11.refs_5_ = bf16[192,768]{1,0:T(8,128)(2,1)S(1)} collective-permute-done((bf16[192,768]{1,0:T(8,128)(2,1)S(1)}, bf16[192,768]{1,0:T(8,128)(2,1)S(1)}, u32[]{:S(2)}, u32[]{:S(2)}) %collective-permute-start.11) | collective-permute-done | bytes 294944 | tf_op jit(solution)/shard_map/ppermute | solution.py:588
  25.8 5.5 %collective-permute-done.14.refs_2_ = bf16[192,768]{1,0:T(8,128)(2,1)S(1)} collective-permute-done((bf16[192,768]{1,0:T(8,128)(2,1)S(1)}, bf16[192,768]{1,0:T(8,128)(2,1)S(1)}, u32[]{:S(2)}, u32[]{:S(2)}) %collective-permute-start.14) | collective-permute-done | bytes 294944 | tf_op jit(solution)/shard_map/ppermute | solution.py:588
  31.2 1.8 %collective-permute-start.2 = (bf16[96,1536]{1,0:T(8,128)(2,1)S(1)}, bf16[96,1536]{1,0:T(8,128)(2,1)S(1)}, u32[]{:S(2)}, u32[]{:S(2)}) collective-permute-start(bf16[96,1536]{1,0:T(8,128)(2,1)S(1)} %collective-permute-done.1.refs_2_), channel_id=1, source_target_pairs={{0,16},{16,0},{1,17},{17,1},{2,18},{18,2},{3,19},{19,3},{4,20},{20... | collective-permute-start | bytes 884744 | tf_op jit(solution)/shard_map/ppermute | solution.py:588
  33.0 0.5 collective-permute-start.15
  33.5 2.0 %central.1 = (f32[128,512]{1,0:T(8,128)S(1)}, f32[256,256]{1,0:T(8,128)S(1)}, bf16[512,128]{1,0:T(8,128)(2,1)S(1)}) custom-call(bf16[256,512]{1,0:T(8,128)(2,1)S(1)} %get-tuple-element.30.msg_ref, bf16[512,1024]{1,0:T(8,128)(2,1)S(1)} %get-tuple-element.33.x_ref, bf16[576,128]{1,0:T(8,128)(2,1)S(1)} %get-tuple-element.31.k1_ref, ...), custom_call_target="tpu_custom_call" | custom-call | tf_op jit(solution)/shard_map/central/pallas_call | solution.py:446
  35.6 0.8 %mix.1 = (f32[128,768]{1,0:T(8,128)S(1)}, bf16[512,768]{1,0:T(8,128)(2,1)S(1)}) custom-call(bf16[512,128]{1,0:T(8,128)(2,1)S(1)} %get-tuple-element.36.patch, bf16[256,768]{1,0:T(8,128)(2,1)S(1)} %copy-done.1, bf16[256,768]{1,0:T(8,128)(2,1)S(1)} %collective-permute-done.6.refs_1_, bf16[256,768]{1,0:T(8,128)(2,1)S(1)} %collective-permute-done.7.refs_2_), custom_call_target="tpu_custom_call" | custom-call | tf_op jit(solution)/shard_map/mix/pallas_call | solution.py:466
  36.9 1.3 %back.1.refs_6_.refs_0_ = bf16[776,128]{1,0:T(8,128)(2,1)S(1)} custom-call(bf16[256,512]{1,0:T(8,128)(2,1)S(1)} %collective-permute-done.5.got_ref, bf16[576,128]{1,0:T(8,128)(2,1)S(1)} %get-tuple-element.31.k1_ref, bf16[1152,256]{1,0:T(8,128)(2,1)S(1)} %get-tuple-element.32.k2_ref, s32[1,128]{1,0:T(1,128)S(1)} %copy-done.4, ...), custom_call_target="tpu_custom_call" | custom-call | tf_op jit(solution)/shard_map/back/pallas_call | solution.py:494
  38.2 2.7 %collective-permute-start.10 = (bf16[776,128]{1,0:T(8,128)(2,1)S(1)}, bf16[776,128]{1,0:T(8,128)(2,1)S(1)}, u32[]{:S(2)}, u32[]{:S(2)}) collective-permute-start(bf16[776,128]{1,0:T(8,128)(2,1)S(1)} %back.1.refs_6_.refs_0_), channel_id=1, source_target_pairs={{0,8},{4,12},{8,0},{12,4},{1,9},{5,13},{9,1},{13,5},{2,10},{6,14},... | collective-permute-start | bytes 595976 | tf_op jit(solution)/shard_map/ppermute | solution.py:588
  40.9 0.5 collective-permute-start.12
  41.4 1.6 %collective-permute-start.9 = (bf16[776,128]{1,0:T(8,128)(2,1)S(1)}, bf16[776,128]{1,0:T(8,128)(2,1)S(1)}, u32[]{:S(2)}, u32[]{:S(2)}) collective-permute-start(bf16[776,128]{1,0:T(8,128)(2,1)S(1)} %back.1.refs_6_.refs_0_), channel_id=1, source_target_pairs={{0,4},{4,0},{8,12},{12,8},{1,5},{5,1},{9,13},{13,9},{2,6},{6,2},{1... | collective-permute-start | bytes 595976 | tf_op jit(solution)/shard_map/ppermute | solution.py:588
  43.0 7.5 %collective-permute-done.10.refs_2_ = bf16[776,128]{1,0:T(8,128)(2,1)S(1)} collective-permute-done((bf16[776,128]{1,0:T(8,128)(2,1)S(1)}, bf16[776,128]{1,0:T(8,128)(2,1)S(1)}, u32[]{:S(2)}, u32[]{:S(2)}) %collective-permute-start.10) | collective-permute-done | bytes 198688 | tf_op jit(solution)/shard_map/ppermute | solution.py:588
  50.5 0.6 %collective-permute-start.16 = (bf16[776,128]{1,0:T(8,128)(2,1)S(1)}, bf16[776,128]{1,0:T(8,128)(2,1)S(1)}, u32[]{:S(2)}, u32[]{:S(2)}) collective-permute-start(bf16[776,128]{1,0:T(8,128)(2,1)S(1)} %collective-permute-done.10.refs_2_), channel_id=1, source_target_pairs={{0,4},{4,0},{8,12},{12,8},{1,5},{5,1},{9,13},{13,9},{2,6},{6,2},{1... | collective-permute-start | bytes 595976 | tf_op jit(solution)/shard_map/ppermute | solution.py:588
  51.5 1.5 %prepare.1 = (bf16[768,1536]{1,0:T(8,128)(2,1)S(1)}, bf16[256,768]{1,0:T(8,128)(2,1)S(1)}, bf16[256,768]{1,0:T(8,128)(2,1)S(1)}, bf16[256,1536]{1,0:T(8,128)(2,1)S(1)}, bf16[512,512]{1,0:T(8,128)(2,1)S(1)}) custom-call(s32[4,128]{1,0:T(4,128)S(1)} %bitcast.5, bf16[192,2304]{1,0:T(8,128)(2,1)S(1)} %copy-done, ...), custom_call_target="tpu_custom_call" | custom-call | tf_op jit(solution)/shard_map/prepare/pallas_call | solution.py:513
  53.1 1.2 %extend.1 = (bf16[768,768]{1,0:T(8,128)(2,1)S(1)}, bf16[128,768]{1,0:T(8,128)(2,1)S(1)}, bf16[128,1536]{1,0:T(8,128)(2,1)S(1)}, f32[128,768]{1,0:T(8,128)S(1)}, ...) custom-call(bf16[512,512]{1,0:T(8,128)(2,1)S(1)} %get-tuple-element.41.perm_ref, ...), custom_call_target="tpu_custom_call" | custom-call | tf_op jit(solution)/shard_map/extend/pallas_call | solution.py:531
  54.2 2.3 %collective-permute-done.16.refs_0_ = bf16[776,128]{1,0:T(8,128)(2,1)S(1)} collective-permute-done((bf16[776,128]{1,0:T(8,128)(2,1)S(1)}, bf16[776,128]{1,0:T(8,128)(2,1)S(1)}, u32[]{:S(2)}, u32[]{:S(2)}) %collective-permute-start.16) | collective-permute-done | bytes 198688 | tf_op jit(solution)/shard_map/ppermute | solution.py:588
  56.5 3.7 %finish.1 = bf16[128,768]{1,0:T(8,128)(2,1)} custom-call(bf16[512,512]{1,0:T(8,128)(2,1)S(1)} %get-tuple-element.41.perm_ref, bf16[768,1536]{1,0:T(8,128)(2,1)S(1)} %get-tuple-element.42.joined, bf16[256,768]{1,0:T(8,128)(2,1)S(1)} %get-tuple-element.43.keys0, bf16[256,1536]{1,0:T(8,128)(2,1)S(1)} %get-tuple-element.44.values0, ...), custom_call_target="tpu_custom_call" | custom-call | tf_op jit(solution)/shard_map/finish/pallas_call | solution.py:569
  (29 shorter events, 1.0 us)
Async XLA Ops:
  0.0 13.1 %collective-permute-start.7 = (bf16[256,768]{1,0:T(8,128)(2,1)}, bf16[256,768]{1,0:T(8,128)(2,1)S(1)}, u32[]{:S(2)}, u32[]{:S(2)}) collective-permute-start(bf16[256,768]{1,0:T(8,128)(2,1)} %refs_0_.5), channel_id=1, source_target_pairs={{0,2},{2,0},{1,3},{3,1},{4,6},{6,4},{5,7},{7,5},{8,10},{10,8},{9,1... | collective-permute-start | bytes 1179656 | tf_op jit(solution)/shard_map/ppermute | solution.py:588
  3.0 6.1 %copy-start.1 = (bf16[256,768]{1,0:T(8,128)(2,1)S(1)}, bf16[256,768]{1,0:T(8,128)(2,1)}, u32[]{:S(2)}) copy-start(bf16[256,768]{1,0:T(8,128)(2,1)} %refs_0_.5) | copy-start | bytes 1179652
  3.0 12.3 %copy-start.2 = (bf16[192,768]{1,0:T(8,128)(2,1)S(1)}, bf16[192,768]{1,0:T(8,128)(2,1)}, u32[]{:S(2)}) copy-start(bf16[192,768]{1,0:T(8,128)(2,1)} %refs_0_.7) | copy-start | bytes 884740
  3.0 16.5 %copy-start = (bf16[192,2304]{1,0:T(8,128)(2,1)S(1)}, bf16[192,2304]{1,0:T(8,128)(2,1)}, u32[]{:S(2)}) copy-start(bf16[192,2304]{1,0:T(8,128)(2,1)} %refs_3_.1) | copy-start | bytes 2654212
  5.4 14.1 %collective-permute-start.1 = (bf16[96,1536]{1,0:T(8,128)(2,1)S(1)}, bf16[96,1536]{1,0:T(8,128)(2,1)S(1)}, u32[]{:S(2)}, u32[]{:S(2)}) collective-permute-start(bf16[96,1536]{1,0:T(8,128)(2,1)S(1)} %get-tuple-element.29), channel_id=1, source_target_pairs={{0,2},{2,0},{1,3},{3,1},{4,6},{6,4},{5,7},{7,5},{8,10},{10,8},{9,1... | collective-permute-start | bytes 884744 | tf_op jit(solution)/shard_map/ppermute | solution.py:588
  5.5 9.9 %collective-permute-start.5 = (bf16[256,512]{1,0:T(8,128)(2,1)S(1)}, bf16[256,512]{1,0:T(8,128)(2,1)S(1)}, u32[]{:S(2)}, u32[]{:S(2)}) collective-permute-start(bf16[256,512]{1,0:T(8,128)(2,1)S(1)} %get-tuple-element.30.msg_ref), channel_id=1, source_target_pairs={{0,4},{4,8},{8,12},{12,0},{1,5},{5,9},{9,13},{13,1},{2,6},{6,10},{... | collective-permute-start | bytes 786440 | tf_op jit(solution)/shard_map/ppermute | solution.py:612
  7.5 18.2 %collective-permute-start.11 = (bf16[192,768]{1,0:T(8,128)(2,1)S(1)}, bf16[192,768]{1,0:T(8,128)(2,1)S(1)}, u32[]{:S(2)}, u32[]{:S(2)}) collective-permute-start(bf16[192,768]{1,0:T(8,128)(2,1)S(1)} %get-tuple-element.46), channel_id=1, source_target_pairs={{0,2},{2,0},{1,3},{3,1},{4,6},{6,4},{5,7},{7,5},{8,10},{10,8},{9,1... | collective-permute-start | bytes 884744 | tf_op jit(solution)/shard_map/ppermute | solution.py:588
  9.0 24.0 %collective-permute-start.6 = (bf16[256,768]{1,0:T(8,128)(2,1)S(1)}, bf16[256,768]{1,0:T(8,128)(2,1)S(1)}, u32[]{:S(2)}, u32[]{:S(2)}) collective-permute-start(bf16[256,768]{1,0:T(8,128)(2,1)S(1)} %copy-done.1), channel_id=1, source_target_pairs={{0,1},{1,0},{2,3},{3,2},{4,5},{5,4},{6,7},{7,6},{8,9},{9,8},{10,11... | collective-permute-start | bytes 1179656 | tf_op jit(solution)/shard_map/ppermute | solution.py:588
  13.1 19.9 %collective-permute-start.8 = (bf16[256,768]{1,0:T(8,128)(2,1)S(1)}, bf16[256,768]{1,0:T(8,128)(2,1)S(1)}, u32[]{:S(2)}, u32[]{:S(2)}) collective-permute-start(bf16[256,768]{1,0:T(8,128)(2,1)S(1)} %collective-permute-done.7.refs_2_), channel_id=1, source_target_pairs={{0,1},{1,0},{2,3},{3,2},{4,5},{5,4},{6,7},{7,6},{8,9},{9,8},{10,11... | collective-permute-start | bytes 1179656 | tf_op jit(solution)/shard_map/ppermute | solution.py:588
  15.3 15.9 %collective-permute-start.14 = (bf16[192,768]{1,0:T(8,128)(2,1)S(1)}, bf16[192,768]{1,0:T(8,128)(2,1)S(1)}, u32[]{:S(2)}, u32[]{:S(2)}) collective-permute-start(bf16[192,768]{1,0:T(8,128)(2,1)S(1)} %copy-done.2), channel_id=1, source_target_pairs={{0,2},{2,0},{1,3},{3,1},{4,6},{6,4},{5,7},{7,5},{8,10},{10,8},{9,1... | collective-permute-start | bytes 884744 | tf_op jit(solution)/shard_map/ppermute | solution.py:588
  19.5 31.9 %collective-permute-start = (bf16[192,2304]{1,0:T(8,128)(2,1)S(1)}, bf16[192,2304]{1,0:T(8,128)(2,1)S(1)}, u32[]{:S(2)}, u32[]{:S(2)}) collective-permute-start(bf16[192,2304]{1,0:T(8,128)(2,1)S(1)} %copy-done), channel_id=1, source_target_pairs={{0,1},{1,0},{2,3},{3,2},{4,5},{5,4},{6,7},{7,6},{8,9},{9,8},{10,11... | collective-permute-start | bytes 2654216 | tf_op jit(solution)/shard_map/ppermute | solution.py:588
  25.8 12.4 %collective-permute-start.13 = (bf16[192,768]{1,0:T(8,128)(2,1)S(1)}, bf16[192,768]{1,0:T(8,128)(2,1)S(1)}, u32[]{:S(2)}, u32[]{:S(2)}) collective-permute-start(bf16[192,768]{1,0:T(8,128)(2,1)S(1)} %copy-done.2), channel_id=1, source_target_pairs={{0,1},{1,0},{2,3},{3,2},{4,5},{5,4},{6,7},{7,6},{8,9},{9,8},{10,11... | collective-permute-start | bytes 884744 | tf_op jit(solution)/shard_map/ppermute | solution.py:588
  31.2 9.7 %collective-permute-start.2 = (bf16[96,1536]{1,0:T(8,128)(2,1)S(1)}, bf16[96,1536]{1,0:T(8,128)(2,1)S(1)}, u32[]{:S(2)}, u32[]{:S(2)}) collective-permute-start(bf16[96,1536]{1,0:T(8,128)(2,1)S(1)} %collective-permute-done.1.refs_2_), channel_id=1, source_target_pairs={{0,16},{16,0},{1,17},{17,1},{2,18},{18,2},{3,19},{19,3},{4,20},{20... | collective-permute-start | bytes 884744 | tf_op jit(solution)/shard_map/ppermute | solution.py:588
  33.0 7.9 %collective-permute-start.3 = (bf16[96,1536]{1,0:T(8,128)(2,1)S(1)}, bf16[96,1536]{1,0:T(8,128)(2,1)S(1)}, u32[]{:S(2)}, u32[]{:S(2)}) collective-permute-start(bf16[96,1536]{1,0:T(8,128)(2,1)S(1)} %collective-permute-done.1.refs_2_), channel_id=1, source_target_pairs={{0,1},{1,0},{2,3},{3,2},{4,5},{5,4},{6,7},{7,6},{8,9},{9,8},{10,11... | collective-permute-start | bytes 884744 | tf_op jit(solution)/shard_map/ppermute | solution.py:588
  33.0 8.4 %collective-permute-start.15 = (bf16[192,768]{1,0:T(8,128)(2,1)S(1)}, bf16[192,768]{1,0:T(8,128)(2,1)S(1)}, u32[]{:S(2)}, u32[]{:S(2)}) collective-permute-start(bf16[192,768]{1,0:T(8,128)(2,1)S(1)} %collective-permute-done.14.refs_2_), channel_id=1, source_target_pairs={{0,1},{1,0},{2,3},{3,2},{4,5},{5,4},{6,7},{7,6},{8,9},{9,8},{10,11... | collective-permute-start | bytes 884744 | tf_op jit(solution)/shard_map/ppermute | solution.py:588
  35.6 1.3 %copy-start.4 = (s32[1,128]{1,0:T(1,128)S(1)}, s32[1,128]{1,0:T(1,128)}, u32[]{:S(2)}) copy-start(s32[1,128]{1,0:T(1,128)} %active_ref.1) | copy-start | bytes 1540
  38.2 13.3 %copy-start.3 = (s32[1,512]{1,0:T(1,128)S(1)}, s32[1,512]{1,0:T(1,128)}, u32[]{:S(2)}) copy-start(s32[1,512]{1,0:T(1,128)} %param.14) | copy-start | bytes 6148
  38.2 12.3 %collective-permute-start.10 = (bf16[776,128]{1,0:T(8,128)(2,1)S(1)}, bf16[776,128]{1,0:T(8,128)(2,1)S(1)}, u32[]{:S(2)}, u32[]{:S(2)}) collective-permute-start(bf16[776,128]{1,0:T(8,128)(2,1)S(1)} %back.1.refs_6_.refs_0_), channel_id=1, source_target_pairs={{0,8},{4,12},{8,0},{12,4},{1,9},{5,13},{9,1},{13,5},{2,10},{6,14},... | collective-permute-start | bytes 595976 | tf_op jit(solution)/shard_map/ppermute | solution.py:588
  40.9 10.5 %collective-permute-start.4 = (bf16[96,1536]{1,0:T(8,128)(2,1)S(1)}, bf16[96,1536]{1,0:T(8,128)(2,1)S(1)}, u32[]{:S(2)}, u32[]{:S(2)}) collective-permute-start(bf16[96,1536]{1,0:T(8,128)(2,1)S(1)} %collective-permute-done.2.refs_3_), channel_id=1, source_target_pairs={{0,1},{1,0},{2,3},{3,2},{4,5},{5,4},{6,7},{7,6},{8,9},{9,8},{10,11... | collective-permute-start | bytes 884744 | tf_op jit(solution)/shard_map/ppermute | solution.py:588
  40.9 12.1 %collective-permute-start.12 = (bf16[192,768]{1,0:T(8,128)(2,1)S(1)}, bf16[192,768]{1,0:T(8,128)(2,1)S(1)}, u32[]{:S(2)}, u32[]{:S(2)}) collective-permute-start(bf16[192,768]{1,0:T(8,128)(2,1)S(1)} %collective-permute-done.11.refs_5_), channel_id=1, source_target_pairs={{0,1},{1,0},{2,3},{3,2},{4,5},{5,4},{6,7},{7,6},{8,9},{9,8},{10,11... | collective-permute-start | bytes 884744 | tf_op jit(solution)/shard_map/ppermute | solution.py:588
  41.4 10.1 %collective-permute-start.9 = (bf16[776,128]{1,0:T(8,128)(2,1)S(1)}, bf16[776,128]{1,0:T(8,128)(2,1)S(1)}, u32[]{:S(2)}, u32[]{:S(2)}) collective-permute-start(bf16[776,128]{1,0:T(8,128)(2,1)S(1)} %back.1.refs_6_.refs_0_), channel_id=1, source_target_pairs={{0,4},{4,0},{8,12},{12,8},{1,5},{5,1},{9,13},{13,9},{2,6},{6,2},{1... | collective-permute-start | bytes 595976 | tf_op jit(solution)/shard_map/ppermute | solution.py:588
  50.5 6.0 %collective-permute-start.16 = (bf16[776,128]{1,0:T(8,128)(2,1)S(1)}, bf16[776,128]{1,0:T(8,128)(2,1)S(1)}, u32[]{:S(2)}, u32[]{:S(2)}) collective-permute-start(bf16[776,128]{1,0:T(8,128)(2,1)S(1)} %collective-permute-done.10.refs_2_), channel_id=1, source_target_pairs={{0,4},{4,0},{8,12},{12,8},{1,5},{5,1},{9,13},{13,9},{2,6},{6,2},{1... | collective-permute-start | bytes 595976 | tf_op jit(solution)/shard_map/ppermute | solution.py:588
